TPU v7x, 32 devices: a whole 2x2x4 slice. The times are simulated.
32 devices in a mesh: seq: 8 (over z, y), row: 4 (over x, core).
Axes of the slice: x: 2, y: 2, z: 4, core: 2. Of those that a mesh axis runs over, the one named last changes fastest.
Arguments:
- hidden_in: bfloat16 [8, 4096, 1024], P('row', 'seq'), may hold values from -6 to 6
- mixer_gain: bfloat16 [1024], replicated, may hold values from 0.099609375 to 1.8984375
- in_weight: bfloat16 [1024, 3072], replicated, may hold values from -0.1875 to 0.1875
- conv_kernel: bfloat16 [1024, 3], replicated, may hold values from -2.5 to 2.5
- out_weight: bfloat16 [1024, 1024], replicated, may hold values from -0.1875 to 0.1875
- feed_gain: bfloat16 [1024], replicated, may hold values from 0.099609375 to 1.8984375
- gate_weight: bfloat16 [1024, 4608], replicated, may hold values from -0.1875 to 0.1875
- up_weight: bfloat16 [1024, 4608], replicated, may hold values from -0.1875 to 0.1875
- down_weight: bfloat16 [4608, 1024], replicated, may hold values from -0.1875 to 0.1875
- document_lengths: int32 [8, 16], P('row'), may hold values from 1 to 1024, 4096 in all within a row
- valid_tokens: int32 [8], P('row'), may hold values from 3687 to 4096, as said below
- cotangent: bfloat16 [8, 4096, 1024], P('row', 'seq'), may hold values from -6 to 6
Outputs:
- output: bfloat16 [8, 4096, 1024], P('row', 'seq')
- input_grad: bfloat16 [8, 4096, 1024], P('row', 'seq')
- mixer_gain_grad: float32 [1024], P('seq')
- in_weight_grad: float32 [1024, 3072], P('seq', 'row')
- conv_kernel_grad: float32 [1024, 3], P('seq')
- out_weight_grad: float32 [1024, 1024], P('seq', 'row')
- feed_gain_grad: float32 [1024], P('seq')
- gate_weight_grad: float32 [1024, 4608], P('seq', 'row')
- up_weight_grad: float32 [1024, 4608], P('seq', 'row')
- down_weight_grad: float32 [4608, 1024], P('seq', 'row')
Inputs may be any that keep to these rules, and one draw needn't show every extreme that they name: Positions from valid_tokens on are padding at the end of a row; some row is full and some row holds exactly 3687 valid positions.
All inputs are finite; a program needn't handle non-finite values.
Results may differ from a plain program's by a relative error of at most 0.015.
Values may be sent and summed in bfloat16 or wider, within the bound.
No kernel may reach another device: no remote copies, remote signals or barrier semaphores. Data moves between devices by JAX's collectives and lax.ppermute only.
A program may use at most 256 MiB of HBM per device.

v0:
```python
import jax
import jax.numpy as jnp
from jax import lax
from jax.sharding import PartitionSpec as P

EPS = 1e-05


def passed_along(value, axis, by):
    length = lax.axis_size(axis)
    pairs = [(i, i + by) for i in range(length) if 0 <= i + by < length]
    return lax.ppermute(value, axis, pairs)


def contract_rows(left, right):
    return lax.dot_general(
        left, right, (((0,), (0,)), ((), ())), preferred_element_type=jnp.float32
    )


def contract_cols(left, right):
    return lax.dot_general(
        left, right, (((1,), (1,)), ((), ())), preferred_element_type=jnp.float32
    )


def local(
    hidden_in,
    mixer_gain,
    in_weight,
    conv_kernel,
    out_weight,
    feed_gain,
    gate_weight,
    up_weight,
    down_weight,
    document_lengths,
    valid_tokens,
    cotangent,
):
    row_count, span_length, model_width = hidden_in.shape
    token_count = row_count * span_length
    offset = lax.axis_index("seq") * span_length
    positions = offset + jnp.arange(span_length, dtype=jnp.int32)
    starts = jnp.cumsum(document_lengths, axis=1) - document_lengths
    is_start = jnp.any(positions[None, :, None] == starts[:, None, :], axis=2)
    before = jnp.any((positions - 1)[None, :, None] == starts[:, None, :], axis=2)
    keep_one = (1.0 - is_start.astype(jnp.float32))[:, :, None]
    keep_two = keep_one * (1.0 - before.astype(jnp.float32))[:, :, None]
    valid_mask = (
        (positions[None, :] < valid_tokens[:, None]).astype(jnp.float32).reshape(token_count, 1)
    )
    mixer_scale = mixer_gain.astype(jnp.float32)
    feed_scale = feed_gain.astype(jnp.float32)
    kernel = conv_kernel.astype(jnp.float32)
    source = hidden_in.astype(jnp.float32).reshape(token_count, model_width)
    inverse_one = lax.rsqrt(jnp.mean(source * source, axis=1, keepdims=True) + EPS)
    normed = (source * inverse_one * mixer_scale).astype(jnp.bfloat16)
    project = jnp.dot(normed, in_weight, preferred_element_type=jnp.float32)
    input_gate = project[:, :model_width]
    output_gate = project[:, model_width : 2 * model_width]
    values = project[:, 2 * model_width :]
    product = (
        (input_gate * values).astype(jnp.bfloat16).reshape(row_count, span_length, model_width)
    )
    rim_values = passed_along(product[:, span_length - 2 :, :], "seq", 1)
    extended = jnp.concatenate([rim_values, product], axis=1).astype(jnp.float32)
    tap_zero = extended[:, 2:, :]
    tap_one = keep_one * extended[:, 1:-1, :]
    tap_two = keep_two * extended[:, :-2, :]
    conv_out = (kernel[:, 0] * tap_zero + kernel[:, 1] * tap_one + kernel[:, 2] * tap_two).reshape(
        token_count, model_width
    )
    mixed_in = (output_gate * conv_out).astype(jnp.bfloat16)
    mixer_out = jnp.dot(mixed_in, out_weight, preferred_element_type=jnp.float32)
    residual = source + valid_mask * mixer_out
    inverse_two = lax.rsqrt(jnp.mean(residual * residual, axis=1, keepdims=True) + EPS)
    normed_two = (residual * inverse_two * feed_scale).astype(jnp.bfloat16)
    gate_pre = jnp.dot(normed_two, gate_weight, preferred_element_type=jnp.float32)
    up_pre = jnp.dot(normed_two, up_weight, preferred_element_type=jnp.float32)
    sigmoid_gate = jax.nn.sigmoid(gate_pre)
    activation = (gate_pre * sigmoid_gate * up_pre).astype(jnp.bfloat16)
    feed_out = jnp.dot(activation, down_weight, preferred_element_type=jnp.float32)
    output = (
        (residual + valid_mask * feed_out)
        .astype(jnp.bfloat16)
        .reshape(row_count, span_length, model_width)
    )
    upstream = cotangent.astype(jnp.float32).reshape(token_count, model_width)
    feed_grad = (valid_mask * upstream).astype(jnp.bfloat16)
    down_grad = contract_rows(activation, feed_grad)
    activation_grad = contract_cols(feed_grad, down_weight)
    up_grad = (activation_grad * gate_pre * sigmoid_gate).astype(jnp.bfloat16)
    gate_grad = (
        activation_grad * up_pre * sigmoid_gate * (1.0 + gate_pre * (1.0 - sigmoid_gate))
    ).astype(jnp.bfloat16)
    gate_wgrad = contract_rows(normed_two, gate_grad)
    up_wgrad = contract_rows(normed_two, up_grad)
    normed_two_grad = contract_cols(gate_grad, gate_weight) + contract_cols(up_grad, up_weight)
    feed_gain_grad = jnp.sum(normed_two_grad * residual * inverse_two, axis=0)
    scaled_two = feed_scale * normed_two_grad
    residual_grad = (
        upstream
        + inverse_two * scaled_two
        - residual
        * (inverse_two * inverse_two * inverse_two)
        * jnp.mean(scaled_two * residual, axis=1, keepdims=True)
    )
    feed_gain_part, gate_part, up_part, down_part = (
        lax.psum_scatter(
            feed_gain_grad.astype(jnp.bfloat16), "seq", scatter_dimension=0, tiled=True
        ).astype(jnp.float32),
        lax.psum_scatter(
            gate_wgrad.astype(jnp.bfloat16), "seq", scatter_dimension=0, tiled=True
        ).astype(jnp.float32),
        lax.psum_scatter(
            up_wgrad.astype(jnp.bfloat16), "seq", scatter_dimension=0, tiled=True
        ).astype(jnp.float32),
        lax.psum_scatter(
            down_grad.astype(jnp.bfloat16), "seq", scatter_dimension=0, tiled=True
        ).astype(jnp.float32),
    )
    gate_part, up_part, down_part = (
        lax.psum_scatter(
            gate_part.astype(jnp.bfloat16), "row", scatter_dimension=1, tiled=True
        ).astype(jnp.float32),
        lax.psum_scatter(
            up_part.astype(jnp.bfloat16), "row", scatter_dimension=1, tiled=True
        ).astype(jnp.float32),
        lax.psum_scatter(
            down_part.astype(jnp.bfloat16), "row", scatter_dimension=1, tiled=True
        ).astype(jnp.float32),
    )
    mixer_grad = (valid_mask * residual_grad).astype(jnp.bfloat16)
    out_wgrad = contract_rows(mixed_in, mixer_grad)
    mixed_grad = contract_cols(mixer_grad, out_weight)
    output_gate_grad = mixed_grad * conv_out
    conv_grad = (mixed_grad * output_gate).reshape(row_count, span_length, model_width)
    kernel_grad = jnp.stack(
        [
            jnp.sum(conv_grad * tap_zero, axis=(0, 1)),
            jnp.sum(conv_grad * tap_one, axis=(0, 1)),
            jnp.sum(conv_grad * tap_two, axis=(0, 1)),
        ],
        axis=1,
    )
    grad_zero = kernel[:, 0] * conv_grad
    grad_one = keep_one * kernel[:, 1] * conv_grad
    grad_two = keep_two * kernel[:, 2] * conv_grad
    extended_grad = (
        jnp.pad(grad_zero, ((0, 0), (2, 0), (0, 0)))
        + jnp.pad(grad_one, ((0, 0), (1, 1), (0, 0)))
        + jnp.pad(grad_two, ((0, 0), (0, 2), (0, 0)))
    )
    returned = passed_along(extended_grad[:, :2, :], "seq", -1)
    product_grad = extended_grad[:, 2:, :] + jnp.pad(
        returned, ((0, 0), (span_length - 2, 0), (0, 0))
    )
    flat_grad = product_grad.reshape(token_count, model_width)
    project_grad = jnp.concatenate(
        [flat_grad * values, output_gate_grad, flat_grad * input_gate], axis=1
    ).astype(jnp.bfloat16)
    in_wgrad = contract_rows(normed, project_grad)
    normed_grad = contract_cols(project_grad, in_weight)
    mixer_gain_grad = jnp.sum(normed_grad * source * inverse_one, axis=0)
    scaled_one = mixer_scale * normed_grad
    input_grad = (
        residual_grad
        + inverse_one * scaled_one
        - source
        * (inverse_one * inverse_one * inverse_one)
        * jnp.mean(scaled_one * source, axis=1, keepdims=True)
    )
    input_grad = input_grad.astype(jnp.bfloat16).reshape(row_count, span_length, model_width)
    mixer_gain_part, in_part, kernel_part, out_part = (
        lax.psum_scatter(
            mixer_gain_grad.astype(jnp.bfloat16), "seq", scatter_dimension=0, tiled=True
        ).astype(jnp.float32),
        lax.psum_scatter(
            in_wgrad.astype(jnp.bfloat16), "seq", scatter_dimension=0, tiled=True
        ).astype(jnp.float32),
        lax.psum_scatter(
            kernel_grad.astype(jnp.bfloat16), "seq", scatter_dimension=0, tiled=True
        ).astype(jnp.float32),
        lax.psum_scatter(
            out_wgrad.astype(jnp.bfloat16), "seq", scatter_dimension=0, tiled=True
        ).astype(jnp.float32),
    )
    in_part, out_part = (
        lax.psum_scatter(
            in_part.astype(jnp.bfloat16), "row", scatter_dimension=1, tiled=True
        ).astype(jnp.float32),
        lax.psum_scatter(
            out_part.astype(jnp.bfloat16), "row", scatter_dimension=1, tiled=True
        ).astype(jnp.float32),
    )
    mixer_gain_part, feed_gain_part, kernel_part = lax.psum(
        (mixer_gain_part, feed_gain_part, kernel_part), "row"
    )
    return (
        output,
        input_grad,
        mixer_gain_part,
        in_part,
        kernel_part,
        out_part,
        feed_gain_part,
        gate_part,
        up_part,
        down_part,
    )


def solution(mesh):
    in_specs = (
        P("row", "seq", None),
        P(),
        P(),
        P(),
        P(),
        P(),
        P(),
        P(),
        P(),
        P("row", None),
        P("row"),
        P("row", "seq", None),
    )
    out_specs = (
        P("row", "seq", None),
        P("row", "seq", None),
        P("seq"),
        P("seq", "row"),
        P("seq", None),
        P("seq", "row"),
        P("seq"),
        P("seq", "row"),
        P("seq", "row"),
        P("seq", "row"),
    )
    return jax.shard_map(local, mesh=mesh, in_specs=in_specs, out_specs=out_specs, check_vma=False)
```

profile of v0, /device:TPU:0, one launch (start us, length us, event | category | flops | bytes accessed | tf_op | source)
XLA Modules:
  0.0 1041.4 jit_solution(650245236480478050)
XLA Ops:
  14.7 6.7 fusion.21
  21.4 4.5 copy-done.3
  27.9 5.1 collective-permute-start
  33.5 3.5 fusion
  41.4 5.2 fusion.4
  50.0 12.9 %fusion.22 = f32[1024,4608]{1,0:T(8,128)} fusion(bf16[1024,1024]{1,0:T(8,128)(2,1)S(1)} %multiply_convert_fusion.4, bf16[1024,4608]{1,0:T(8,128)(2,1)S(1)} %bitcast.114), kind=kOutput, calls=%fused_computation.82 | convolution fusion | flops 9663676416 | bytes 30408704 | tf_op jit(solution)/shard_map/dot_general | solution.py:79
  62.9 16.1 %fusion.23 = f32[1024,4608]{1,0:T(8,128)} fusion(bf16[1024,1024]{1,0:T(8,128)(2,1)S(1)} %multiply_convert_fusion.4, bf16[1024,4608]{1,0:T(8,128)(2,1)} %param.19), kind=kOutput, calls=%fused_computation.83 | convolution fusion | flops 9663676416 | bytes 30408704 | tf_op jit(solution)/shard_map/dot_general | solution.py:80
  79.0 32.1 %multiply_convert_fusion = (bf16[1024,4608]{1,0:T(8,128)(2,1)}, bf16[1024,4608]{1,0:T(8,128)(2,1)}, bf16[1024,4608]{1,0:T(8,128)(2,1)}) fusion(f32[1024,4608]{1,0:T(8,128)} %fusion.22, f32[1024,4608]{1,0:T(8,128)} %fusion.23, bf16[1024,1024]{1,0:T(8,128)(2,1)} %fusion, bf16[4608,1024]{1,0:T(8,128)(2,1)} %param.20), kind=kOutput, calls=%fused_computation | convolution fusion | flops 9739173888 | bytes 77594624 | tf_op jit(solution)/shard_map/dot_general | solution.py:22
  111.1 15.9 %fusion.24 = f32[1024,1024]{1,0:T(8,128)} fusion(bf16[1024,4608]{1,0:T(8,128)(2,1)} %get-tuple-element.26, bf16[1024,4608]{1,0:T(8,128)(2,1)} %param.18), kind=kOutput, calls=%fused_computation.84 | convolution fusion | flops 9663676416 | bytes 23068672 | tf_op jit(solution)/shard_map/dot_general | solution.py:22
  127.0 17.3 %multiply_reduce_fusion = (bf16[1024]{0:T(1024)(128)(2,1)}, f32[1024]{0:T(1024)S(1)}, f32[1024,1024]{1,0:T(8,128)S(1)}) fusion(f32[1024,1024]{1,0:T(8,128)S(1)} %get-tuple-element.41, f32[1024]{0:T(1024)S(1)} %get-tuple-element.37, f32[1024]{0:T(1024)S(1)} %convert_element_type.152, f32[1024,1024]{1,0:T(8,128)} %fusion.24, ...), kind=kOutput, calls=%fused_computation.40 | convolution fusion | flops 9671014400 | bytes 31471616 | tf_op jit(solution)/shard_map/dot_general | solution.py:22
  147.9 3.8 convolution_convert_fusion.4
  151.9 9.3 multiply_reduce_fusion.3
  169.0 8.0 pad_add_fusion
  177.0 5.2 slice_add_fusion
  182.3 6.2 fusion.2
  188.5 11.0 %convolution_convert_fusion.3 = bf16[1024,3072]{1,0:T(8,128)(2,1)} fusion(bf16[1024,1024]{1,0:T(8,128)(2,1)S(1)} %copy-done.20, bf16[1024,1024]{1,0:T(8,128)(2,1)} %get-tuple-element.29, bf16[1024,1024]{1,0:T(8,128)(2,1)S(1)} %fusion.5, bf16[1024,1024]{1,0:T(8,128)(2,1)} %get-tuple-element.28), kind=kOutput, calls=%fused_computation.8 | convolution fusion | flops 6464471040 | bytes 14680064 | tf_op jit(solution)/shard_map/dot_general | solution.py:16
  201.1 15.7 %convolution_convert_fusion.1 = bf16[1024,4608]{1,0:T(8,128)(2,1)} fusion(bf16[1024,1024]{1,0:T(8,128)(2,1)S(1)} %copy-done.22, bf16[1024,4608]{1,0:T(8,128)(2,1)} %get-tuple-element.26), kind=kOutput, calls=%fused_computation.5 | convolution fusion | flops 9668395008 | bytes 20971520 | tf_op jit(solution)/shard_map/dot_general | solution.py:16
  216.9 15.8 %convolution_convert_fusion = bf16[1024,4608]{1,0:T(8,128)(2,1)} fusion(bf16[1024,1024]{1,0:T(8,128)(2,1)S(1)} %copy-done.22, bf16[1024,4608]{1,0:T(8,128)(2,1)} %get-tuple-element.25), kind=kOutput, calls=%fused_computation.4 | convolution fusion | flops 9668395008 | bytes 20971520 | tf_op jit(solution)/shard_map/dot_general | solution.py:16
  234.4 16.0 %convolution_convert_fusion.2 = bf16[4608,1024]{1,0:T(8,128)(2,1)} fusion(bf16[1024,4608]{1,0:T(8,128)(2,1)} %get-tuple-element.27, bf16[1024,1024]{1,0:T(8,128)(2,1)S(1)} %copy-done.18), kind=kOutput, calls=%fused_computation.6 | convolution fusion | flops 9668395008 | bytes 20971520 | tf_op jit(solution)/shard_map/dot_general | solution.py:16
  251.3 90.1 %reduce-scatter.18.cloned.1.call-done = bf16[128,3072]{1,0:T(8,128)(2,1)} async-done(((bf16[1024,3072]{1,0:T(8,128)(2,1)}), bf16[128,3072]{1,0:T(8,128)(2,1)}) %reduce-scatter.18.cloned.1.call-update) | async-done | bytes 786448 | tf_op jit(solution)/shard_map/reduce_scatter | solution.py:179
  341.5 164.9 %reduce-scatter.26.cloned.1.call-done = bf16[128,4608]{1,0:T(8,128)(2,1)} async-done(((bf16[1024,4608]{1,0:T(8,128)(2,1)}), bf16[128,4608]{1,0:T(8,128)(2,1)}) %reduce-scatter.26.cloned.1.call-update) | async-done | bytes 1179664 | tf_op jit(solution)/shard_map/reduce_scatter | solution.py:113
  508.9 162.2 %reduce-scatter.28.cloned.1.call-done = bf16[128,4608]{1,0:T(8,128)(2,1)} async-done(((bf16[1024,4608]{1,0:T(8,128)(2,1)}), bf16[128,4608]{1,0:T(8,128)(2,1)}) %reduce-scatter.28.cloned.1.call-update) | async-done | bytes 1179664 | tf_op jit(solution)/shard_map/reduce_scatter | solution.py:116
  675.1 16.9 %add_convert_fusion = bf16[1024,1024]{1,0:T(8,128)(2,1)} fusion(f32[1024,1024]{1,0:T(8,128)} %copy-done.11, bf16[1024,4608]{1,0:T(8,128)(2,1)} %get-tuple-element.27, bf16[4608,1024]{1,0:T(8,128)(2,1)} %param.20, f32[1024]{0:T(1024)S(1)} %bitcast.106), kind=kOutput, calls=%fused_computation.48 | convolution fusion | flops 9666822144 | bytes 25169920 | tf_op jit(solution)/shard_map/dot_general | solution.py:83
  692.0 44.1 %reduce-scatter.34.cloned.1.call-done = bf16[128,3]{1,0:T(8,128)(2,1)} async-done(((bf16[1024,3]{1,0:T(8,128)(2,1)}), bf16[128,3]{1,0:T(8,128)(2,1)}) %reduce-scatter.34.cloned.1.call-update) | async-done | bytes 784
  736.9 163.8 %reduce-scatter.30.cloned.1.call-done = bf16[576,1024]{1,0:T(8,128)(2,1)} async-done(((bf16[4608,1024]{1,0:T(8,128)(2,1)}), bf16[576,1024]{1,0:T(8,128)(2,1)}) %reduce-scatter.30.cloned.1.call-update) | async-done | bytes 1179664 | tf_op jit(solution)/shard_map/reduce_scatter | solution.py:119
  900.7 12.6 %fusion.14 = (bf16[1024]{0:T(1024)(128)(2,1)S(1)}, f32[1024]{0:T(1024)S(1)}, f32[1024,1024]{1,0:T(8,128)}) fusion(bf16[2,512,1024]{2,1,0:T(8,128)(2,1)S(1)} %copy-done.10, f32[1024]{0:T(1024)S(1)} %bitcast.100, f32[1024]{0:T(1024)S(1)} %copy-done.32, bf16[1024,3072]{1,0:T(8,128)(2,1)} %param.14, bf16[1024,1024]{1,0:T(8,128)(2,1)} %get-tuple-element.29, ...), kind=kOutput, calls=%fused_computation.39 | convolution fusion | flops 6468663296 | bytes 18888704 | tf_op jit(solution)/shard_map/dot_general | solution.py:22
  913.3 19.5 %all-reduce.7 = (bf16[1024]{0:T(1024)(128)(2,1)S(1)}, bf16[1024]{0:T(1024)(128)(2,1)S(1)}) all-reduce(bf16[1024]{0:T(1024)(128)(2,1)S(1)} %get-tuple-element.15, bf16[1024]{0:T(1024)(128)(2,1)S(1)} %copy-done.42), channel_id=2, replica_groups=mesh['seq'=8,'row'=4] {'seq'}, use_global_device_ids=true, to_apply=%region_8.9.clone | all-reduce | flops 2048 | bytes 8192
  933.0 6.2 all-reduce.6
  939.2 5.9 fusion.11
  949.8 26.5 %reduce-scatter.36.cloned.1.call-done = bf16[1152,128]{1,0:T(8,128)(2,1)} async-done(((bf16[4608,128]{1,0:T(8,128)(2,1)}), bf16[1152,128]{1,0:T(8,128)(2,1)}) %reduce-scatter.36.cloned.1.call-update) | async-done | bytes 294928
  978.3 26.0 %reduce-scatter.38.cloned.1.call-done = bf16[1152,128]{1,0:T(8,128)(2,1)} async-done(((bf16[4608,128]{1,0:T(8,128)(2,1)}), bf16[1152,128]{1,0:T(8,128)(2,1)}) %reduce-scatter.38.cloned.1.call-update) | async-done | bytes 294928
  1006.4 26.2 %reduce-scatter.32.cloned.1.call-done = bf16[576,256]{1,0:T(8,128)(2,1)} async-done(((bf16[576,1024]{1,0:T(8,128)(2,1)}), bf16[576,256]{1,0:T(8,128)(2,1)}) %reduce-scatter.32.cloned.1.call-update) | async-done | bytes 294928 | tf_op jit(solution)/shard_map/reduce_scatter | solution.py:130
  (179 shorter events, 50.1 us)
Async XLA Ops:
  7.2 39.5 %copy-start = (bf16[1024,1024]{1,0:T(8,128)(2,1)S(1)}, bf16[1024,1024]{1,0:T(8,128)(2,1)}, u32[]{:S(2)}) copy-start(bf16[1024,1024]{1,0:T(8,128)(2,1)} %param.16) | copy-start | bytes 6291460
  7.2 243.3 %reduce-scatter.22.cloned.1.call-start = ((), (), s32[]{:S(2)}) async-start(), calls=%async_computation.13 | async-start | bytes 2359296 | tf_op jit(solution)/shard_map/reduce_scatter | solution.py:185
  26.6 10.4 copy-start.41
  27.9 9.1 collective-permute-start
  33.4 13.3 %copy-start.29 = (f32[1,4,2,128]{3,1,2,0:T(4,128)}, f32[1,4,2,128]{3,1,2,0:T(4,128)S(1)}, u32[]{:S(2)}) copy-start(f32[1,4,2,128]{3,1,2,0:T(4,128)S(1)} %copy.28) | copy-start | bytes 12292
  49.3 95.0 %copy-start.11 = (f32[1024,1024]{1,0:T(8,128)}, f32[1024,1024]{1,0:T(8,128)S(1)}, u32[]{:S(2)}) copy-start(f32[1024,1024]{1,0:T(8,128)S(1)} %get-tuple-element.41) | copy-start | bytes 12582916
  50.0 12.9 %copy-start.21 = (bf16[1024,1024]{1,0:T(8,128)(2,1)}, bf16[1024,1024]{1,0:T(8,128)(2,1)S(1)}, u32[]{:S(2)}) copy-start(bf16[1024,1024]{1,0:T(8,128)(2,1)S(1)} %multiply_convert_fusion.4) | copy-start | bytes 6291460
  127.0 17.3 %copy-start.14 = (bf16[2,512,1024]{2,1,0:T(8,128)(2,1)S(1)}, bf16[2,512,1024]{2,1,0:T(8,128)(2,1)}, u32[]{:S(2)}) copy-start(bf16[2,512,1024]{2,1,0:T(8,128)(2,1)} %param.23) | copy-start | bytes 6291460
  151.8 9.4 copy-start.34
  151.8 9.4 copy-start.36
  151.8 9.4 copy-start.38
  151.8 189.6 %reduce-scatter.18.cloned.1.call-start = ((), (), s32[]{:S(2)}) async-start(), calls=%async_computation.11 | async-start | bytes 7077888 | tf_op jit(solution)/shard_map/reduce_scatter | solution.py:179
  166.4 10.6 %collective-permute-start.1 = (f32[2,2,1024]{2,1,0:T(2,128)S(1)}, f32[2,2,1024]{2,1,0:T(2,128)S(1)}, u32[]{:S(2)}, u32[]{:S(2)}) collective-permute-start(f32[2,2,1024]{2,1,0:T(2,128)S(1)} %pad_add_fusion.1), channel_id=1, source_target_pairs={{4,0},{8,4},{12,8},{16,12},{20,16},{24,20},{28,24},{5,1},{9,5},{13... | collective-permute-start | bytes 49160 | tf_op jit(solution)/shard_map/ppermute | solution.py:12
  167.8 14.4 %slice-start = ((s8[12582912]{0:T(1024)(128)(4,1)}), s8[4194304]{0:T(1024)(128)(4,1)S(1)}, s32[]{:S(2)}) async-start(s8[12582912]{0:T(1024)(128)(4,1)} %bitcast.88), calls=%async_computation.22 | async-start | bytes 8388608
  168.9 19.6 %copy-start.15 = (bf16[1024,1024]{1,0:T(8,128)(2,1)}, bf16[1024,1024]{1,0:T(8,128)(2,1)S(1)}, u32[]{:S(2)}) copy-start(bf16[1024,1024]{1,0:T(8,128)(2,1)S(1)} %fusion.5) | copy-start | bytes 6291460
  168.9 13.3 %slice-start.1 = ((s8[12582912]{0:T(1024)(128)(4,1)}), s8[4194304]{0:T(1024)(128)(4,1)S(1)}, s32[]{:S(2)}) async-start(s8[12582912]{0:T(1024)(128)(4,1)} %bitcast.88), calls=%async_computation.23 | async-start | bytes 8388608
  168.9 13.3 %slice-start.2 = ((s8[12582912]{0:T(1024)(128)(4,1)}), s8[4194304]{0:T(1024)(128)(4,1)S(1)}, s32[]{:S(2)}) async-start(s8[12582912]{0:T(1024)(128)(4,1)} %bitcast.88), calls=%async_computation.24 | async-start | bytes 8388608
  199.5 306.9 %reduce-scatter.26.cloned.1.call-start = ((), (), s32[]{:S(2)}) async-start(), calls=%async_computation.15 | async-start | bytes 10616832 | tf_op jit(solution)/shard_map/reduce_scatter | solution.py:113
  216.9 454.2 %reduce-scatter.28.cloned.1.call-start = ((), (), s32[]{:S(2)}) async-start(), calls=%async_computation.16 | async-start | bytes 10616832 | tf_op jit(solution)/shard_map/reduce_scatter | solution.py:116
  232.8 503.3 %reduce-scatter.34.cloned.1.call-start = ((), (), s32[]{:S(2)}) async-start(), calls=%async_computation.19 | async-start | bytes 294912
  233.8 666.9 %reduce-scatter.30.cloned.1.call-start = ((), (), s32[]{:S(2)}) async-start(), calls=%async_computation.17 | async-start | bytes 10616832 | tf_op jit(solution)/shard_map/reduce_scatter | solution.py:119
  250.4 423.3 %copy-start.24 = (f32[1,4,2,128]{3,1,2,0:T(4,128)S(1)}, f32[1,4,2,128]{3,1,2,0:T(4,128)}, u32[]{:S(2)}) copy-start(f32[1,4,2,128]{3,1,2,0:T(4,128)} %copy-done.23) | copy-start | bytes 12292
  250.4 423.4 %copy-start.45 = (u32[32]{0:T(128)S(1)}, u32[32]{0:T(128)}, u32[]{:S(2)}) copy-start(u32[32]{0:T(128)} %constant.46) | copy-start | bytes 388
  250.5 694.6 %reduce-scatter.24.cloned.1.call-start = ((), (), s32[]{:S(2)}) async-start(), calls=%async_computation.14 | async-start | bytes 327680 | tf_op jit(solution)/shard_map/reduce_scatter | solution.py:193
  251.2 696.9 %reduce-scatter.20.cloned.1.call-start = ((), (), s32[]{:S(2)}) async-start(), calls=%async_computation.12 | async-start | bytes 983040 | tf_op jit(solution)/shard_map/reduce_scatter | solution.py:190
  341.4 634.9 %reduce-scatter.36.cloned.1.call-start = ((), (), s32[]{:S(2)}) async-start(), calls=%async_computation.20 | async-start | bytes 1474560
  508.8 495.5 %reduce-scatter.38.cloned.1.call-start = ((), (), s32[]{:S(2)}) async-start(), calls=%async_computation.21 | async-start | bytes 1474560
  673.7 358.9 %reduce-scatter.32.cloned.1.call-start = ((), (), s32[]{:S(2)}) async-start(), calls=%async_computation.18 | async-start | bytes 1474560 | tf_op jit(solution)/shard_map/reduce_scatter | solution.py:130
  675.0 225.7 %copy-start.10 = (bf16[2,512,1024]{2,1,0:T(8,128)(2,1)S(1)}, bf16[2,512,1024]{2,1,0:T(8,128)(2,1)}, u32[]{:S(2)}) copy-start(bf16[2,512,1024]{2,1,0:T(8,128)(2,1)} %param.12) | copy-start | bytes 6291460
  675.0 225.7 %copy-start.32 = (f32[1024]{0:T(1024)S(1)}, f32[1024]{0:T(1024)}, u32[]{:S(2)}) copy-start(f32[1024]{0:T(1024)} %copy-done.31) | copy-start | bytes 12292
  900.7 12.6 %copy-start.42 = (bf16[1024]{0:T(1024)(128)(2,1)S(1)}, bf16[1024]{0:T(1024)(128)(2,1)}, u32[]{:S(2)}) copy-start(bf16[1024]{0:T(1024)(128)(2,1)} %get-tuple-element.13) | copy-start | bytes 6148
  939.2 95.2 %copy-start.1 = (bf16[1024,1024]{1,0:T(8,128)(2,1)S(1)}, bf16[1024,1024]{1,0:T(8,128)(2,1)}, u32[]{:S(2)}) copy-start(bf16[1024,1024]{1,0:T(8,128)(2,1)} %param.16) | copy-start | bytes 6291460
  (33 other events, 125.1 us)
Sparse Core Ops, SparseCore 0:
  151.9 68.7 reduce-scatter.21
  224.3 117.0 reduce-scatter.17
  345.0 161.3 reduce-scatter.25
  509.8 161.1 reduce-scatter.27
  674.8 61.1 reduce-scatter.33
  739.5 161.1 reduce-scatter.29
  903.1 19.1 reduce-scatter.23
  924.8 23.2 reduce-scatter.19
  950.7 25.5 reduce-scatter.35
  978.7 25.6 reduce-scatter.37
  1006.9 25.6 reduce-scatter.31
where the time goes:
time: 1050 us; the launch traced here: 1040 us
  waiting for transfers between devices  706 us (67%)
  matrix products  205 us (20%)
  other arithmetic  53.9 us (5%)
  local copies, waits for them, and re-layouts  27.9 us (3%)
  blocking collectives  25.7 us (2%)
  between operations  15.8 us (2%)
    reduce_scatter x1, waiting for transfers between devices, local(): lax.psum_scatter(gate_wgrad.astype(jnp.bfloat16), 'seq', scatter_dimensio...  165 us
    reduce_scatter x1, waiting for transfers between devices, local(): lax.psum_scatter(down_grad.astype(jnp.bfloat16), 'seq', scatter_dimension...  164 us
    reduce_scatter x1, waiting for transfers between devices, local(): lax.psum_scatter(up_wgrad.astype(jnp.bfloat16), 'seq', scatter_dimension=...  162 us
    unnamed x14, waiting for transfers between devices  97.5 us
    reduce_scatter x1, waiting for transfers between devices, local(): lax.psum_scatter(in_wgrad.astype(jnp.bfloat16), 'seq', scatter_dimension=...  90.1 us
    dot_general x5, matrix products, contract_cols(): lax.dot_general(left, right, (((1,), (1,)), ((), ())), preferred_element_...  87.3 us
    dot_general x5, matrix products, contract_rows(): lax.dot_general(left, right, (((0,), (0,)), ((), ())), preferred_element_...  62.4 us
    unnamed x113, local copies, waits for them, and re-layouts  27.9 us
  transfers between devices with their start and end apart: 13, of which 9 were waited for; matrix products, arithmetic and copies ran while one was open for 14% of the time, Pallas kernels for 0%

commit v1 on v0

--- a/solution.py
+++ b/solution.py
@@ -1,6 +1,8 @@
 import jax
 import jax.numpy as jnp
 from jax import lax
+from jax.experimental import pallas as pl
+from jax.experimental.pallas import tpu as pltpu
 from jax.sharding import PartitionSpec as P
 
 EPS = 1e-05
@@ -24,7 +26,284 @@
     )
 
 
-def local(
+def swapped(value, axis, bit):
+    length = lax.axis_size(axis)
+    return lax.ppermute(value, axis, [(i, i ^ bit) for i in range(length)])
+
+
+def wide(left, right):
+    return left.astype(jnp.float32) + right.astype(jnp.float32)
+
+
+def narrow(value):
+    return value.astype(jnp.bfloat16)
+
+
+def feed_chunk(place, own_in, other_in, own_grad, other_grad, gate_weight, up_weight, down_weight, chunk, chunks):
+    tokens, width = own_in.shape
+    hidden = gate_weight.shape[1]
+    rows = 2
+    block = hidden // 4
+    part = block // chunks
+    span = rows * part
+    tile = min(512, tokens)
+    tiles = 2 * tokens // tile
+    half_tiles = tokens // tile
+    eighth = width // 8
+    step = 256
+
+    def kernel(
+        place_ref, own_ref, other_ref, own_grad_ref, other_grad_ref, gate_ref, up_ref, down_ref,
+        act_out, gate_out, up_out, gate_send, gate_keep, up_send, up_keep, down_send, down_keep,
+        tok, grd, wg, wu, wd, act, gg, ug, gw, uw, dw, in_sem, w_sem, out_sem, grad_sem,
+    ):
+        def token_copy(t, which):
+            buf = (tok, grd)[which]
+            src = ((own_ref, other_ref), (own_grad_ref, other_grad_ref))[which][0 if t < half_tiles else 1]
+            return pltpu.make_async_copy(
+                src.at[pl.ds((t % half_tiles) * tile, tile)],
+                buf.at[pl.ds(t * tile, tile)],
+                in_sem.at[which, t],
+            )
+
+        weight_copies = []
+        for n, (ref, buf) in enumerate(((gate_ref, wg), (up_ref, wu))):
+            weight_copies.append([
+                pltpu.make_async_copy(
+                    ref.at[:, pl.ds(pl.multiple_of(place_ref[j] * block + chunk * part, 128), part)],
+                    buf.at[:, pl.ds(j * part, part)],
+                    w_sem.at[n, j],
+                )
+                for j in range(2)
+            ])
+        weight_copies.append([
+            pltpu.make_async_copy(
+                down_ref.at[pl.ds(pl.multiple_of(place_ref[j] * block + chunk * part, 128), part), :],
+                wd.at[pl.ds(j * part, part), :],
+                w_sem.at[2, j],
+            )
+            for j in range(2)
+        ])
+        token_copy(0, 0).start()
+        for copy in weight_copies[0]:
+            copy.start()
+        for copy in weight_copies[1]:
+            copy.start()
+        token_copy(0, 1).start()
+        for copy in weight_copies[2]:
+            copy.start()
+        outs = []
+        for t in range(tiles):
+            at = pl.ds(t * tile, tile)
+            token_copy(t, 0).wait()
+            if t == 0:
+                for copy in weight_copies[0] + weight_copies[1]:
+                    copy.wait()
+            if t + 1 < tiles:
+                token_copy(t + 1, 0).start()
+                token_copy(t + 1, 1).start()
+            token_copy(t, 1).wait()
+            if t == 0:
+                for copy in weight_copies[2]:
+                    copy.wait()
+            for n in range(span // step):
+                cols = pl.ds(n * step, step)
+                gate = jnp.dot(tok[at, :], wg[:, cols], preferred_element_type=jnp.float32)
+                up = jnp.dot(tok[at, :], wu[:, cols], preferred_element_type=jnp.float32)
+                grad = contract_cols(grd[at, :], wd[cols, :])
+                sig = jax.nn.sigmoid(gate)
+                gate_sig = gate * sig
+                act[at, cols] = narrow(gate_sig * up)
+                ug[at, cols] = narrow(grad * gate_sig)
+                gg[at, cols] = narrow(grad * up * (sig + gate_sig * (1.0 - sig)))
+            for n, (buf, out) in enumerate(((act, act_out), (gg, gate_out), (ug, up_out))):
+                copy = pltpu.make_async_copy(buf.at[at], out.at[at], out_sem.at[n, t])
+                copy.start()
+                outs.append(copy)
+
+        for buf, grad in ((gw, gg), (uw, ug)):
+            for n in range(span // step):
+                cols = pl.ds(n * step, step)
+                total = narrow(contract_rows(tok[...], grad[:, cols]))
+                for i in range(8):
+                    spot = place_ref[2 + i]
+                    rows_i = total[i * eighth : (i + 1) * eighth]
+                    for c in range(step // 128):
+                        col = n * step + c * 128
+                        buf[col // part, spot, :, pl.ds(col % part, 128)] = rows_i[:, c * 128 : (c + 1) * 128]
+            if buf is gw:
+                pairs = [
+                    (gw.at[j, pl.ds(4 * h + 2 * z, 2)], out.at[j, h], grad_sem.at[8 + 4 * z + 2 * j + h])
+                    for z, out in enumerate((gate_send, gate_keep))
+                    for j in range(2)
+                    for h in range(2)
+                ]
+            else:
+                pairs = [
+                    (uw.at[j, 2 * h + y], out.at[j, h], grad_sem.at[16 + 8 * y + 4 * j + h])
+                    for y, out in enumerate((up_send, up_keep))
+                    for j in range(2)
+                    for h in range(4)
+                ]
+            for src, out, sem in pairs:
+                copy = pltpu.make_async_copy(src, out, sem)
+                copy.start()
+                outs.append(copy)
+        for side in range(2):
+            for n in range(2):
+                cols = pl.ds(pl.multiple_of(place_ref[10 + side] * (width // 2) + n * (width // 4), 128), width // 4)
+                total = narrow(contract_rows(act[...], grd[:, cols]))
+                for j in range(2):
+                    dw[side, place_ref[12 + j], :, pl.ds(n * (width // 4), width // 4)] = total[j * part : (j + 1) * part]
+            copy = pltpu.make_async_copy(dw.at[side], (down_send, down_keep)[side], grad_sem.at[side])
+            copy.start()
+            outs.append(copy)
+        for copy in outs:
+            copy.wait()
+
+    any_spec = pl.BlockSpec(memory_space=pl.ANY)
+    low = jnp.bfloat16
+    both = 2 * tokens
+    flops = 6 * 2 * both * width * span
+    return pl.pallas_call(
+        kernel,
+        out_shape=[jax.ShapeDtypeStruct((both, span), low)] * 3
+        + [jax.ShapeDtypeStruct((2, 2, 2, eighth, part), low)] * 2
+        + [jax.ShapeDtypeStruct((2, 4, eighth, part), low)] * 2
+        + [jax.ShapeDtypeStruct((2, part, width // 2), low)] * 2,
+        grid_spec=pltpu.PrefetchScalarGridSpec(
+            num_scalar_prefetch=1,
+            grid=(1,),
+            in_specs=[any_spec] * 7,
+            out_specs=[any_spec] * 9,
+            scratch_shapes=[
+                pltpu.VMEM((both, width), low),
+                pltpu.VMEM((both, width), low),
+                pltpu.VMEM((width, span), low),
+                pltpu.VMEM((width, span), low),
+                pltpu.VMEM((span, width), low),
+                pltpu.VMEM((both, span), low),
+                pltpu.VMEM((both, span), low),
+                pltpu.VMEM((both, span), low),
+                pltpu.VMEM((2, 8, eighth, part), low),
+                pltpu.VMEM((2, 8, eighth, part), low),
+                pltpu.VMEM((2, 2, part, width // 2), low),
+                pltpu.SemaphoreType.DMA((2, tiles)),
+                pltpu.SemaphoreType.DMA((3, 2)),
+                pltpu.SemaphoreType.DMA((3, tiles)),
+                pltpu.SemaphoreType.DMA((32,)),
+            ],
+        ),
+        compiler_params=pltpu.CompilerParams(vmem_limit_bytes=56 << 20),
+        cost_estimate=pl.CostEstimate(flops=flops, bytes_accessed=24 << 20, transcendentals=both * span),
+        name=f"feed_{chunk}",
+    )(place, own_in, other_in, own_grad, other_grad, gate_weight, up_weight, down_weight)
+
+
+def feed_sum(place, groups, weights, across, block, name):
+    chunks = len(groups[0])
+    both, span = groups[0][0].shape
+    part = span // 2
+    width = weights[0].shape[0] if across else weights[0].shape[1]
+    tokens = both // 2
+    tile = min(512, tokens)
+    tiles = both // tile
+    half_tiles = tiles // 2
+    kinds = len(groups)
+
+    def kernel(place_ref, *refs):
+        lefts = [refs[g * chunks : (g + 1) * chunks] for g in range(kinds)]
+        rights = refs[kinds * chunks : kinds * chunks + kinds]
+        own_out, other_out, lbuf, wbuf, total, obuf, l_sem, w_sem, o_sem = refs[kinds * chunks + kinds :]
+
+        def weight_copies(k):
+            slot = k % 2
+            copies = []
+            for g in range(kinds):
+                for j in range(2):
+                    rows = pl.ds(pl.multiple_of(place_ref[j] * block + k * part, 128), part)
+                    if across:
+                        src, dst = rights[g].at[:, rows], wbuf.at[slot, g, :, pl.ds(j * part, part)]
+                    else:
+                        src, dst = rights[g].at[rows, :], wbuf.at[slot, g, pl.ds(j * part, part), :]
+                    copies.append(pltpu.make_async_copy(src, dst, w_sem.at[slot, g, j]))
+            return copies
+
+        def left_copies(k, t, slot):
+            return [
+                pltpu.make_async_copy(lefts[g][k].at[pl.ds(t * tile, tile)], lbuf.at[slot, g], l_sem.at[slot, g])
+                for g in range(kinds)
+            ]
+
+        def out_copy(t, slot):
+            ref = own_out if t < half_tiles else other_out
+            return pltpu.make_async_copy(
+                obuf.at[slot], ref.at[pl.ds((t % half_tiles) * tile, tile)], o_sem.at[slot]
+            )
+
+        for copy in left_copies(0, 0, 0) + weight_copies(0):
+            copy.start()
+        for k in range(chunks):
+            for t in range(tiles):
+                n = k * tiles + t
+                for copy in left_copies(k, t, n % 2):
+                    copy.wait()
+                if t == 0:
+                    for copy in weight_copies(k):
+                        copy.wait()
+                if n + 1 < chunks * tiles:
+                    for copy in left_copies((n + 1) // tiles, (n + 1) % tiles, (n + 1) % 2):
+                        copy.start()
+                if t == 0 and k + 1 < chunks:
+                    for copy in weight_copies(k + 1):
+                        copy.start()
+                value = None
+                for g in range(kinds):
+                    left, right = lbuf[n % 2, g], wbuf[k % 2, g]
+                    term = contract_cols(left, right) if across else jnp.dot(left, right, preferred_element_type=jnp.float32)
+                    value = term if value is None else value + term
+                if k > 0:
+                    value = value + total[t]
+                if k + 1 < chunks:
+                    total[t] = value
+                else:
+                    if t >= 2:
+                        out_copy(t - 2, t % 2).wait()
+                    obuf[t % 2] = narrow(value)
+                    out_copy(t, t % 2).start()
+        for t in range(max(0, tiles - 2), tiles):
+            out_copy(t, t % 2).wait()
+
+    any_spec = pl.BlockSpec(memory_space=pl.ANY)
+    low = jnp.bfloat16
+    wshape = (width, span) if across else (span, width)
+    return pl.pallas_call(
+        kernel,
+        out_shape=[jax.ShapeDtypeStruct((tokens, width), low)] * 2,
+        grid_spec=pltpu.PrefetchScalarGridSpec(
+            num_scalar_prefetch=1,
+            grid=(1,),
+            in_specs=[any_spec] * (kinds * chunks + kinds),
+            out_specs=[any_spec] * 2,
+            scratch_shapes=[
+                pltpu.VMEM((2, kinds, tile, span), low),
+                pltpu.VMEM((2, kinds) + wshape, low),
+                pltpu.VMEM((tiles, tile, width), jnp.float32),
+                pltpu.VMEM((2, tile, width), low),
+                pltpu.SemaphoreType.DMA((2, kinds)),
+                pltpu.SemaphoreType.DMA((2, kinds, 2)),
+                pltpu.SemaphoreType.DMA((2,)),
+            ],
+        ),
+        compiler_params=pltpu.CompilerParams(vmem_limit_bytes=48 << 20),
+        cost_estimate=pl.CostEstimate(
+            flops=kinds * chunks * 2 * both * width * span, bytes_accessed=24 << 20, transcendentals=0
+        ),
+        name=name,
+    )(place, *[item for group in groups for item in group], *weights)
+
+
+def plain(
     hidden_in,
     mixer_gain,
     in_weight,
@@ -211,6 +490,259 @@
     )
 
 
+def settle(value, order):
+    names = ["x", "z1", "z0", "y"]
+    links = {"x": ("row", 2), "y": ("seq", 1), "z0": ("seq", 2), "z1": ("seq", 4)}
+    for name in order:
+        at = names.index(name)
+        names.remove(name)
+        give = lax.index_in_dim(value, 0, at, keepdims=False)
+        keep = lax.index_in_dim(value, 1, at, keepdims=False)
+        value = wide(keep, swapped(narrow(give), *links[name]))
+        if names:
+            value = narrow(value)
+    return value
+
+
+def fast(
+    hidden_in,
+    mixer_gain,
+    in_weight,
+    conv_kernel,
+    out_weight,
+    feed_gain,
+    gate_weight,
+    up_weight,
+    down_weight,
+    document_lengths,
+    valid_tokens,
+    cotangent,
+):
+    row_count, span_length, model_width = hidden_in.shape
+    token_count = row_count * span_length
+    hidden_width = gate_weight.shape[1]
+    block = hidden_width // 4
+    chunks = 3
+    part = block // chunks
+    seq = lax.axis_index("seq")
+    row = lax.axis_index("row")
+    row_x, core = row // 2, row % 2
+    seq_y, seq_z0, seq_z1 = seq % 2, (seq // 2) % 2, seq // 4
+    place = jnp.stack(
+        [row ^ 2, row]
+        + [i ^ seq ^ 7 for i in range(8)]
+        + [1 - row_x, row_x, 1 - ((1 - row_x) ^ seq_z1), 1 - (row_x ^ seq_z1)]
+    ).astype(jnp.int32)
+    offset = seq * span_length
+    positions = offset + jnp.arange(span_length, dtype=jnp.int32)
+    starts = jnp.cumsum(document_lengths, axis=1) - document_lengths
+    is_start = jnp.any(positions[None, :, None] == starts[:, None, :], axis=2)
+    before = jnp.any((positions - 1)[None, :, None] == starts[:, None, :], axis=2)
+    keep_one = (1.0 - is_start.astype(jnp.float32))[:, :, None]
+    keep_two = keep_one * (1.0 - before.astype(jnp.float32))[:, :, None]
+    valid_mask = (
+        (positions[None, :] < valid_tokens[:, None]).astype(jnp.float32).reshape(token_count, 1)
+    )
+    mixer_scale = mixer_gain.astype(jnp.float32)
+    feed_scale = feed_gain.astype(jnp.float32)
+    kernel = conv_kernel.astype(jnp.float32)
+    upstream = cotangent.astype(jnp.float32).reshape(token_count, model_width)
+    feed_grad = narrow(valid_mask * upstream)
+    other_grad = swapped(feed_grad, "row", 1)
+
+    source = hidden_in.astype(jnp.float32).reshape(token_count, model_width)
+    inverse_one = lax.rsqrt(jnp.mean(source * source, axis=1, keepdims=True) + EPS)
+    normed = (source * inverse_one * mixer_scale).astype(jnp.bfloat16)
+    project = jnp.dot(normed, in_weight, preferred_element_type=jnp.float32)
+    input_gate = project[:, :model_width]
+    output_gate = project[:, model_width : 2 * model_width]
+    values = project[:, 2 * model_width :]
+    product = (
+        (input_gate * values).astype(jnp.bfloat16).reshape(row_count, span_length, model_width)
+    )
+    rim_values = passed_along(product[:, span_length - 2 :, :], "seq", 1)
+    extended = jnp.concatenate([rim_values, product], axis=1).astype(jnp.float32)
+    tap_zero = extended[:, 2:, :]
+    tap_one = keep_one * extended[:, 1:-1, :]
+    tap_two = keep_two * extended[:, :-2, :]
+    conv_out = (kernel[:, 0] * tap_zero + kernel[:, 1] * tap_one + kernel[:, 2] * tap_two).reshape(
+        token_count, model_width
+    )
+    mixed_in = (output_gate * conv_out).astype(jnp.bfloat16)
+    mixer_out = jnp.dot(mixed_in, out_weight, preferred_element_type=jnp.float32)
+    residual = source + valid_mask * mixer_out
+    inverse_two = lax.rsqrt(jnp.mean(residual * residual, axis=1, keepdims=True) + EPS)
+    normed_two = (residual * inverse_two * feed_scale).astype(jnp.bfloat16)
+    other_normed = swapped(normed_two, "row", 1)
+
+    acts, gates, ups, gate_parts, up_parts, down_parts = [], [], [], [], [], []
+    for chunk in range(chunks):
+        act, gate_grad, up_grad, gs, gk, us, uk, ds, dk = feed_chunk(
+            place, normed_two, other_normed, feed_grad, other_grad, gate_weight, up_weight, down_weight, chunk, chunks
+        )
+        acts.append(act)
+        gates.append(gate_grad)
+        ups.append(up_grad)
+        gate = narrow(wide(gk, swapped(gs, "seq", 2)))
+        gate = narrow(wide(gate[1], swapped(gate[0], "row", 2)))
+        gate_parts.append(gate)
+        up = narrow(wide(uk, swapped(us, "seq", 1)))
+        up = narrow(wide(up[1], swapped(up[0], "row", 2)))
+        up_parts.append(up)
+        down_parts.append(narrow(wide(dk, swapped(ds, "row", 2))))
+    own_ntg, give_ntg = feed_sum(place, [gates, ups], [gate_weight, up_weight], True, block, "normed_two_grad")
+    take_ntg = swapped(give_ntg, "row", 1)
+    own_feed, give_feed = feed_sum(place, [acts], [down_weight], False, block, "feed_out")
+    take_feed = swapped(give_feed, "row", 1)
+    output = narrow(residual + valid_mask * wide(own_feed, take_feed)).reshape(row_count, span_length, model_width)
+
+    gate = jnp.stack(gate_parts)
+    gate = narrow(wide(gate[:, :, 1], swapped(gate[:, :, 0], "seq", 1)))
+    gate = wide(gate[:, 1], swapped(gate[:, 0], "seq", 4))
+    gate_part = jnp.concatenate([gate[i] for i in range(chunks)], axis=1)
+    up = jnp.stack(up_parts).reshape(chunks, 2, 2, model_width // 8, part)
+    up = narrow(wide(up[:, :, 1], swapped(up[:, :, 0], "seq", 2)))
+    up = wide(up[:, 1], swapped(up[:, 0], "seq", 4))
+    up_part = jnp.concatenate([up[i] for i in range(chunks)], axis=1)
+    down = jnp.concatenate(down_parts, axis=1)
+    low_half, high_half = down[:, : block // 2], down[:, block // 2 :]
+    down = narrow(
+        wide(
+            jnp.where(seq_y == 0, low_half, high_half),
+            swapped(jnp.where(seq_y == 0, high_half, low_half), "seq", 1),
+        )
+    )
+    down = narrow(wide(down[1], swapped(down[0], "seq", 4)))
+    holder = [[(r & 1) == ((s >> 1) & 1) for r in range(4)] for s in range(8)]
+    down = wide(
+        down,
+        lax.ppermute(
+            down,
+            ("seq", "row"),
+            [(s * 4 + r, (s ^ 2) * 4 + r) for s in range(8) for r in range(4) if not holder[s][r]],
+        ),
+    )
+    quarter = model_width // 4
+    down_own = jnp.where(core == 0, down[:, :quarter], down[:, quarter:])
+    down_other = narrow(jnp.where(core == 0, down[:, quarter:], down[:, :quarter]))
+    down_other = lax.ppermute(
+        down_other,
+        ("seq", "row"),
+        [(s * 4 + r, s * 4 + (r ^ 1)) for s in range(8) for r in range(4) if holder[s][r]],
+    )
+    down_part = jnp.where(core == seq_z0, down_own, down_other.astype(jnp.float32))
+
+    normed_two_grad = wide(own_ntg, take_ntg)
+    feed_gain_grad = jnp.sum(normed_two_grad * residual * inverse_two, axis=0)
+    scaled_two = feed_scale * normed_two_grad
+    residual_grad = (
+        upstream
+        + inverse_two * scaled_two
+        - residual
+        * (inverse_two * inverse_two * inverse_two)
+        * jnp.mean(scaled_two * residual, axis=1, keepdims=True)
+    )
+    mixer_grad = (valid_mask * residual_grad).astype(jnp.bfloat16)
+
+    def by_seq(value):
+        width = value.shape[1] // 8
+        return jnp.concatenate(
+            [lax.dynamic_slice_in_dim(value, (p ^ seq ^ 7) * width, width, 1) for p in range(8)], axis=1
+        )
+
+    def by_row(value, core_at):
+        width = value.shape[1] // 4
+        return jnp.concatenate(
+            [
+                lax.dynamic_slice_in_dim(value, ((row ^ 3) ^ (2 * x + core_at)) * width, width, 1)
+                for x in range(2)
+            ],
+            axis=1,
+        )
+
+    def pair_summed(left, right):
+        give = contract_rows(left, by_row(right, 0))
+        keep = contract_rows(left, by_row(right, 1))
+        both = narrow(keep + swapped(narrow(give), "row", 1).astype(jnp.float32))
+        width = both.shape[1] // 2
+        return jnp.stack(
+            [both[:, i * width : (i + 1) * width].reshape(2, 2, 2, model_width // 8, width) for i in range(2)]
+        )
+
+    out_sum = pair_summed(by_seq(mixed_in), mixer_grad)
+    mixed_grad = contract_cols(mixer_grad, out_weight)
+    output_gate_grad = mixed_grad * conv_out
+    conv_grad = (mixed_grad * output_gate).reshape(row_count, span_length, model_width)
+    kernel_grad = [
+        jnp.sum(conv_grad * tap_zero, axis=(0, 1)),
+        jnp.sum(conv_grad * tap_one, axis=(0, 1)),
+        jnp.sum(conv_grad * tap_two, axis=(0, 1)),
+    ]
+    grad_zero = kernel[:, 0] * conv_grad
+    grad_one = keep_one * kernel[:, 1] * conv_grad
+    grad_two = keep_two * kernel[:, 2] * conv_grad
+    extended_grad = (
+        jnp.pad(grad_zero, ((0, 0), (2, 0), (0, 0)))
+        + jnp.pad(grad_one, ((0, 0), (1, 1), (0, 0)))
+        + jnp.pad(grad_two, ((0, 0), (0, 2), (0, 0)))
+    )
+    returned = passed_along(extended_grad[:, :2, :], "seq", -1)
+    product_grad = extended_grad[:, 2:, :] + jnp.pad(
+        returned, ((0, 0), (span_length - 2, 0), (0, 0))
+    )
+    flat_grad = product_grad.reshape(token_count, model_width)
+    project_grad = jnp.concatenate(
+        [flat_grad * values, output_gate_grad, flat_grad * input_gate], axis=1
+    ).astype(jnp.bfloat16)
+    in_sum = pair_summed(by_seq(normed), project_grad)
+    third = in_sum.shape[-1] // 3
+    in_part = jnp.concatenate(
+        [
+            settle(in_sum[..., i * third : (i + 1) * third], order)
+            for i, order in enumerate((("x", "y", "z0", "z1"), ("y", "x", "z0", "z1"), ("z0", "x", "y", "z1")))
+        ],
+        axis=1,
+    )
+    out_part = settle(out_sum, ("y", "z0", "x", "z1"))
+    normed_grad = contract_cols(project_grad, in_weight)
+    mixer_gain_grad = jnp.sum(normed_grad * source * inverse_one, axis=0)
+    scaled_one = mixer_scale * normed_grad
+    input_grad = (
+        residual_grad
+        + inverse_one * scaled_one
+        - source
+        * (inverse_one * inverse_one * inverse_one)
+        * jnp.mean(scaled_one * source, axis=1, keepdims=True)
+    )
+    input_grad = input_grad.astype(jnp.bfloat16).reshape(row_count, span_length, model_width)
+    small = jnp.stack([mixer_gain_grad, feed_gain_grad] + kernel_grad)
+    for axis, bit in (("row", 1), ("row", 2), ("seq", 1), ("seq", 2), ("seq", 4)):
+        small = small + swapped(small, axis, bit)
+    small = lax.dynamic_slice_in_dim(small, seq * (model_width // 8), model_width // 8, 1)
+    return (
+        output,
+        input_grad,
+        small[0],
+        in_part,
+        small[2:].T,
+        out_part,
+        small[1],
+        gate_part,
+        up_part,
+        down_part,
+    )
+
+
+def local(*args):
+    hidden_in, gate_weight = args[0], args[6]
+    tokens = hidden_in.shape[0] * hidden_in.shape[1]
+    width, hidden = gate_weight.shape
+    tiled = lax.axis_size("seq") == 8 and lax.axis_size("row") == 4 and hidden % (4 * 3 * 128) == 0
+    if tiled and width % 1024 == 0 and tokens % 512 == 0:
+        return fast(*args)
+    return plain(*args)
+
+
 def solution(mesh):
     in_specs = (
         P("row", "seq", None),

time: 1050 us -> 479 us (0.46)
  waiting for transfers between devices: 706 us -> 142 us
  matrix products: 205 us -> 42.4 us
  Pallas kernels: 0 us -> 127 us
  starting transfers between devices: 6.97 us -> 56.3 us
  blocking collectives: 25.7 us -> 0 us
  other arithmetic: 53.9 us -> 70.8 us
  between operations: 15.8 us -> 2.85 us
    reduce_scatter x8 -> x0, waiting for transfers between devices: 609 us -> none  [the longest x1 165 us: local(): lax.psum_scatter(gate_wgrad.astype(jnp.bfloat16), 'seq', scatter_dimensio...]
    ppermute x0 -> x50, waiting for transfers between devices: none -> 142 us  [the longest x48 140 us: swapped(): return lax.ppermute(value, axis, [(i, i ^ bit) for i in range(length)])]
    pallas_call x0 -> x5, Pallas kernels: none -> 127 us  [the longest x3 83.7 us: feed_chunk(): pl.pallas_call(kernel, out_shape=[jax.ShapeDtypeStruct((both, span), low)...]
    unnamed x14 -> x0, waiting for transfers between devices: 97.5 us -> none
    dot_general x5 -> x2, matrix products: 87.3 us -> 19.8 us  [contract_cols(): lax.dot_general(left, right, (((1,), (1,)), ((), ())), preferred_element_...]
    ppermute x0 -> x50, starting transfers between devices: none -> 50.3 us  [the longest x48 47.7 us: swapped(): return lax.ppermute(value, axis, [(i, i ^ bit) for i in range(length)])]
    dot_general x5 -> x4, matrix products: 62.4 us -> 13.3 us  [contract_rows(): lax.dot_general(left, right, (((0,), (0,)), ((), ())), preferred_element_...]
    dot_general x5 -> x2, matrix products: 55.2 us -> 9.34 us  [the longest x1 6.74 us: fast(): project = jnp.dot(normed, in_weight, preferred_element_type=jnp.float32)]
  transfers between devices with their start and end apart: 13 -> 52, of which waited for: 9 -> 26; matrix products, arithmetic and copies ran while one was open for 14% -> 25% of each run, Pallas kernels for 0% -> 21%
where the time goes in v1:
time: 479 us; the launch traced here: 471 us
  waiting for transfers between devices  142 us (30%)
  Pallas kernels  127 us (27%)
  other arithmetic  70.8 us (15%)
  starting transfers between devices  56.3 us (12%)
  matrix products  42.4 us (9%)
  local copies, waits for them, and re-layouts  30.5 us (6%)
    ppermute x48, waiting for transfers between devices, swapped(): return lax.ppermute(value, axis, [(i, i ^ bit) for i in range(length)])  140 us
    pallas_call x3, Pallas kernels, feed_chunk(): pl.pallas_call(kernel, out_shape=[jax.ShapeDtypeStruct((both, span), low)...  83.7 us
    ppermute x48, starting transfers between devices, swapped(): return lax.ppermute(value, axis, [(i, i ^ bit) for i in range(length)])  47.7 us
    pallas_call x2, Pallas kernels, feed_sum(): pl.pallas_call(kernel, out_shape=[jax.ShapeDtypeStruct((tokens, width), l...  43.2 us
    unnamed x142, local copies, waits for them, and re-layouts  23.7 us
    dot_general x2, matrix products, contract_cols(): lax.dot_general(left, right, (((1,), (1,)), ((), ())), preferred_element_...  19.8 us
    convert_element_type x30, other arithmetic, narrow(): return value.astype(jnp.bfloat16)  15.9 us
    dot_general x4, matrix products, contract_rows(): lax.dot_general(left, right, (((0,), (0,)), ((), ())), preferred_element_...  13.3 us
  transfers between devices with their start and end apart: 52, of which 26 were waited for; matrix products, arithmetic and copies ran while one was open for 25% of the time, Pallas kernels for 21%

profile of v1, /device:TPU:0, one launch (start us, length us, event | category | flops | bytes accessed | tf_op | source)
XLA Modules:
  0.0 471.4 jit_solution(6970316754836290653)
XLA Ops:
  1.6 3.5 fusion.own_grad_ref
  9.1 6.7 %fusion.71 = f32[1024,3072]{1,0:T(8,128)S(1)} fusion(bf16[1024,1024]{1,0:T(8,128)(2,1)S(1)} %fusion.8, bf16[1024,3072]{1,0:T(8,128)(2,1)S(1)} %copy-done.52), kind=kOutput, calls=%fused_computation.262 | convolution fusion | flops 6442450944 | bytes 20971520 | tf_op jit(solution)/shard_map/dot_general | solution.py:556
  15.8 4.6 copy-done.3
  22.5 4.4 collective-permute-start
  34.7 3.7 fusion.4
  49.5 27.9 %feed_2.1 = (bf16[2048,768]{1,0:T(8,128)(2,1)}, bf16[2048,768]{1,0:T(8,128)(2,1)}, bf16[2048,768]{1,0:T(8,128)(2,1)}, bf16[2,2,2,128,384]{4,3,2,1,0:T(8,128)(2,1...) custom-call(s32[14]{0:T(128)} %stack.107.place_ref, ...), custom_call_target="tpu_custom_call" | custom-call | flops 19327352832 | bytes 25165824 | tf_op jit(solution)/shard_map/feed_2/pallas_call | solution.py:168
  77.4 3.3 collective-permute-start.33
  82.8 27.9 %feed_1.1 = (bf16[2048,768]{1,0:T(8,128)(2,1)}, bf16[2048,768]{1,0:T(8,128)(2,1)}, bf16[2048,768]{1,0:T(8,128)(2,1)}, bf16[2,2,2,128,384]{4,3,2,1,0:T(8,128)(2,1...) custom-call(s32[14]{0:T(128)} %stack.107.place_ref, ...), custom_call_target="tpu_custom_call" | custom-call | flops 19327352832 | bytes 25165824 | tf_op jit(solution)/shard_map/feed_1/pallas_call | solution.py:168
  112.2 27.9 %feed_0.1 = (bf16[2048,768]{1,0:T(8,128)(2,1)}, bf16[2048,768]{1,0:T(8,128)(2,1)}, bf16[2048,768]{1,0:T(8,128)(2,1)}, bf16[2,2,2,128,384]{4,3,2,1,0:T(8,128)(2,1...) custom-call(s32[14]{0:T(128)} %stack.107.place_ref, ...), custom_call_target="tpu_custom_call" | custom-call | flops 19327352832 | bytes 25165824 | tf_op jit(solution)/shard_map/feed_0/pallas_call | solution.py:168
  140.1 16.5 %feed_out.1 = (bf16[1024,1024]{1,0:T(8,128)(2,1)S(1)}, bf16[1024,1024]{1,0:T(8,128)(2,1)S(1)}) custom-call(s32[14]{0:T(128)S(1)} %copy-done.1, bf16[2048,768]{1,0:T(8,128)(2,1)} %get-tuple-element.41.refs_0_, bf16[2048,768]{1,0:T(8,128)(2,1)} %get-tuple-element.42.refs_1_, bf16[2048,768]{1,0:T(8,128)(2,1)} %get-tuple-element.43.refs_2_, ...), custom_call_target="tpu_custom_call" | custom-call | flops 9663676416 | bytes 25165824 | tf_op jit(solution)/shard_map/feed_out/pallas_call | solution.py:280
  167.7 9.7 %collective-permute-done.46 = bf16[2,384,512]{2,1,0:T(8,128)(2,1)S(1)} collective-permute-done((bf16[2,384,512]{2,1,0:T(8,128)(2,1)}, bf16[2,384,512]{2,1,0:T(8,128)(2,1)S(1)}, u32[]{:S(2)}, u32[]{:S(2)}) %collective-permute-start.46) | collective-permute-done | bytes 786464 | tf_op jit(solution)/shard_map/ppermute | solution.py:31
  181.0 13.2 %collective-permute-done.45 = bf16[2,384,512]{2,1,0:T(8,128)(2,1)S(1)} collective-permute-done((bf16[2,384,512]{2,1,0:T(8,128)(2,1)S(1)}, bf16[2,384,512]{2,1,0:T(8,128)(2,1)S(1)}, u32[]{:S(2)}, u32[]{:S(2)}) %collective-permute-start.45) | collective-permute-done | bytes 786464 | tf_op jit(solution)/shard_map/ppermute | solution.py:31
  196.4 6.2 %collective-permute-done.34 = bf16[2,2,128,384]{3,2,1,0:T(8,128)(2,1)S(1)} collective-permute-done((bf16[2,2,128,384]{3,2,1,0:T(8,128)(2,1)S(1)}, bf16[2,2,128,384]{3,2,1,0:T(8,128)(2,1)S(1)}, u32[]{:S(2)}, u32[]{:S(2)}) %collective-permute-start.34) | collective-permute-done | bytes 393248 | tf_op jit(solution)/shard_map/ppermute | solution.py:31
  203.3 16.2 %collective-permute-done.32 = bf16[2,2,128,384]{3,2,1,0:T(8,128)(2,1)S(1)} collective-permute-done((bf16[2,2,128,384]{3,2,1,0:T(8,128)(2,1)S(1)}, bf16[2,2,128,384]{3,2,1,0:T(8,128)(2,1)S(1)}, u32[]{:S(2)}, u32[]{:S(2)}) %collective-permute-start.32) | collective-permute-done | bytes 393248 | tf_op jit(solution)/shard_map/ppermute | solution.py:31
  220.1 16.2 %collective-permute-done.30 = bf16[2,2,128,384]{3,2,1,0:T(8,128)(2,1)S(1)} collective-permute-done((bf16[2,2,128,384]{3,2,1,0:T(8,128)(2,1)S(1)}, bf16[2,2,128,384]{3,2,1,0:T(8,128)(2,1)S(1)}, u32[]{:S(2)}, u32[]{:S(2)}) %collective-permute-start.30) | collective-permute-done | bytes 393248 | tf_op jit(solution)/shard_map/ppermute | solution.py:31
  246.0 26.6 %normed_two_grad.1 = (bf16[1024,1024]{1,0:T(8,128)(2,1)S(1)}, bf16[1024,1024]{1,0:T(8,128)(2,1)S(1)}) custom-call(s32[14]{0:T(128)S(1)} %copy-done.1, bf16[2048,768]{1,0:T(8,128)(2,1)} %get-tuple-element.46.refs_0_, bf16[2048,768]{1,0:T(8,128)(2,1)} %get-tuple-element.47.refs_1_, bf16[2048,768]{1,0:T(8,128)(2,1)} %get-tuple-element.48.refs_2_, ...), custom_call_target="tpu_custom_call" | custom-call | flops 19327352832 | bytes 25165824 | tf_op jit(solution)/shard_map/normed_two_grad/pallas_call | solution.py:280
  283.1 26.6 %collective-permute-done.36 = bf16[3,128,384]{2,1,0:T(8,128)(2,1)S(1)} collective-permute-done((bf16[3,128,384]{2,1,0:T(8,128)(2,1)S(1)}, bf16[3,128,384]{2,1,0:T(8,128)(2,1)S(1)}, u32[]{:S(2)}, u32[]{:S(2)}) %collective-permute-start.36) | collective-permute-done | bytes 294944 | tf_op jit(solution)/shard_map/ppermute | solution.py:31
  309.8 6.2 %collective-permute-done.44 = bf16[3,128,384]{2,1,0:T(8,128)(2,1)S(1)} collective-permute-done((bf16[3,128,384]{2,1,0:T(8,128)(2,1)S(1)}, bf16[3,128,384]{2,1,0:T(8,128)(2,1)S(1)}, u32[]{:S(2)}, u32[]{:S(2)}) %collective-permute-start.44) | collective-permute-done | bytes 294944 | tf_op jit(solution)/shard_map/ppermute | solution.py:31
  319.5 6.3 %multiply_convert_fusion = (bf16[1024,1024]{1,0:T(8,128)(2,1)S(1)}, f32[1024,1024]{1,0:T(8,128)}, bf16[1024,1024]{1,0:T(8,128)(2,1)}) fusion(f32[1024]{0:T(1024)S(1)} %bitcast.346, f32[1024]{0:T(1024)S(1)} %broadcast_multiply_fusion.2, f32[1024,1024]{1,0:T(8,128)S(1)} %copy-done.5, f32[1024]{0:T(1024)S(1)} %get-tuple-element.121, ...), kind=kLoop, calls=%fused_computation.39 | loop fusion | flops 18874368 | bytes 23089152 | tf_op jit(solution)/shard_map/convert_element_type | solution.py:645
  325.8 7.0 %multiply_reduce_fusion = (f32[1024]{0:T(1024)S(1)}, f32[1024]{0:T(1024)S(1)}, f32[1024]{0:T(1024)S(1)}, f32[1024,1024]{1,0:T(8,128)}, f32[1024,1024]{1,0:T(8,128)S(1)}) fusion(f32[2,514,1024]{2,1,0:T(8,128)S(1)} %bitcast.318, f32[2,512]{1,0:T(2,128)S(1)} %get-tuple-element.124, f32[2,512]{1,0:T(2,128)S(1)} %get-tuple-element.123, ...), kind=kOutput, calls=%fused_computation.33 | convolution fusion | flops 2156917760 | bytes 29380608 | tf_op jit(solution)/shard_map/dot_general | solution.py:24
  346.3 7.7 %pad_add_fusion = f32[2,514,1024]{2,1,0:T(8,128)} fusion(f32[2,512,1024]{2,1,0:T(8,128)} %copy-done.6, f32[2,512,1024]{2,1,0:T(8,128)} %copy-done.7, f32[2,512,1024]{2,1,0:T(8,128)S(1)} %get-tuple-element.91), kind=kLoop, calls=%fused_computation.4 | loop fusion | flops 2105344 | bytes 16793600 | tf_op jit(solution)/shard_map/add | solution.py:685
  354.0 5.2 %slice_add_fusion = f32[2,512,1024]{2,1,0:T(8,128)} fusion(f32[2,514,1024]{2,1,0:T(8,128)} %pad_add_fusion, f32[2,2,1024]{2,1,0:T(2,128)S(1)} %collective-permute-done.5), kind=kLoop, calls=%fused_computation.7 | loop fusion | flops 1048576 | bytes 8404992 | tf_op jit(solution)/shard_map/add | solution.py:690
  359.2 6.1 %fusion.2 = (bf16[1024,1024]{1,0:T(8,128)(2,1)}, bf16[1024,1024]{1,0:T(8,128)(2,1)}) fusion(f32[2,512,1024]{2,1,0:T(8,128)} %slice_add_fusion, f32[1024,3072]{1,0:T(8,128)S(1)} %bitcast.320), kind=kLoop, calls=%fused_computation.12 | loop fusion | flops 4194304 | bytes 16777216 | tf_op jit(solution)/shard_map/convert.29
  365.3 12.8 %fusion.14 = (f32[1024]{0:T(1024)S(1)}, f32[1024]{0:T(1024)S(1)}, f32[1024,1024]{1,0:T(8,128)}) fusion(bf16[2,512,1024]{2,1,0:T(8,128)(2,1)S(1)} %copy-done.10, f32[1024]{0:T(1024)S(1)} %bitcast.342, f32[1024]{0:T(1024)S(1)} %copy-done.41, bf16[1024,3072]{1,0:T(8,128)(2,1)} %param.14, bf16[1024,1024]{1,0:T(8,128)(2,1)} %get-tuple-element.85, ...), kind=kOutput, calls=%fused_computation.32 | convolution fusion | flops 6468663296 | bytes 18890752 | tf_op jit(solution)/shard_map/dot_general | solution.py:24
  378.8 3.5 pad_maximum_fusion
  388.0 4.1 convolution_convert_fusion
  392.8 3.3 collective-permute-done.9
  406.8 8.7 %collective-permute-done.25 = bf16[2,2,2,128,256]{4,3,1,0,2:T(8,128)(2,1)S(1)} collective-permute-done((bf16[2,2,2,128,256]{4,3,1,0,2:T(8,128)(2,1)S(1)}, bf16[2,2,2,128,256]{4,3,1,0,2:T(8,128)(2,1)S(1)}, u32[]{:S(2)}, u32[]{:S(2)}) %collective-permute-start.25) | collective-permute-done | bytes 524320 | tf_op jit(solution)/shard_map/ppermute | solution.py:31
  418.3 4.1 collective-permute-done.26
  429.7 4.4 add_convert_fusion
  438.4 6.4 %collective-permute-done.12 = bf16[2,2,2,128,256]{4,3,0,1,2:T(8,128)(2,1)S(1)} collective-permute-done((bf16[2,2,2,128,256]{4,3,0,1,2:T(8,128)(2,1)S(1)}, bf16[2,2,2,128,256]{4,3,0,1,2:T(8,128)(2,1)S(1)}, u32[]{:S(2)}, u32[]{:S(2)}) %collective-permute-start.12) | collective-permute-done | bytes 524320 | tf_op jit(solution)/shard_map/ppermute | solution.py:31
  448.5 3.5 collective-permute-done.16
  (352 shorter events, 138.0 us)
Async XLA Ops:
  5.0 44.5 %collective-permute-start.2 = (bf16[1024,1024]{1,0:T(8,128)(2,1)}, bf16[1024,1024]{1,0:T(8,128)(2,1)}, u32[]{:S(2)}, u32[]{:S(2)}) collective-permute-start(bf16[1024,1024]{1,0:T(8,128)(2,1)} %fusion.own_grad_ref), channel_id=1, source_target_pairs={{0,1},{1,0},{2,3},{3,2},{4,5},{5,4},{6,7},{7,6},{8,9},{9,8},{10,11... | collective-permute-start | bytes 6291464 | tf_op jit(solution)/shard_map/ppermute | solution.py:31
  77.4 79.3 %collective-permute-start.33 = (bf16[2,2,2,128,384]{4,3,2,1,0:T(8,128)(2,1)}, bf16[2,2,2,128,384]{4,3,2,1,0:T(8,128)(2,1)}, u32[]{:S(2)}, u32[]{:S(2)}) collective-permute-start(bf16[2,2,2,128,384]{4,3,2,1,0:T(8,128)(2,1)} %get-tuple-element.59), channel_id=1, source_target_pairs={{0,8},{4,12},{8,0},{12,4},{16,24},{20,28},{24,16},{28,20},{1,9},{5... | collective-permute-start | bytes 2359304 | tf_op jit(solution)/shard_map/ppermute | solution.py:31
  80.7 78.0 %collective-permute-start.41 = (bf16[2,4,128,384]{3,2,1,0:T(8,128)(2,1)}, bf16[2,4,128,384]{3,2,1,0:T(8,128)(2,1)}, u32[]{:S(2)}, u32[]{:S(2)}) collective-permute-start(bf16[2,4,128,384]{3,2,1,0:T(8,128)(2,1)} %get-tuple-element.65), channel_id=1, source_target_pairs={{0,4},{4,0},{8,12},{12,8},{16,20},{20,16},{24,28},{28,24},{1,5},{5... | collective-permute-start | bytes 2359304 | tf_op jit(solution)/shard_map/ppermute | solution.py:31
  81.3 80.7 %collective-permute-start.47 = (bf16[2,384,512]{2,1,0:T(8,128)(2,1)}, bf16[2,384,512]{2,1,0:T(8,128)(2,1)S(1)}, u32[]{:S(2)}, u32[]{:S(2)}) collective-permute-start(bf16[2,384,512]{2,1,0:T(8,128)(2,1)} %get-tuple-element.71), channel_id=1, source_target_pairs={{0,2},{1,3},{2,0},{3,1},{4,6},{5,7},{6,4},{7,5},{8,10},{9,11},{10,... | collective-permute-start | bytes 2359304 | tf_op jit(solution)/shard_map/ppermute | solution.py:31
  110.7 53.7 %collective-permute-start.31 = (bf16[2,2,2,128,384]{4,3,2,1,0:T(8,128)(2,1)}, bf16[2,2,2,128,384]{4,3,2,1,0:T(8,128)(2,1)}, u32[]{:S(2)}, u32[]{:S(2)}) collective-permute-start(bf16[2,2,2,128,384]{4,3,2,1,0:T(8,128)(2,1)} %get-tuple-element.57), channel_id=1, source_target_pairs={{0,8},{4,12},{8,0},{12,4},{16,24},{20,28},{24,16},{28,20},{1,9},{5... | collective-permute-start | bytes 2359304 | tf_op jit(solution)/shard_map/ppermute | solution.py:31
  111.2 56.2 %collective-permute-start.39 = (bf16[2,4,128,384]{3,2,1,0:T(8,128)(2,1)}, bf16[2,4,128,384]{3,2,1,0:T(8,128)(2,1)S(1)}, u32[]{:S(2)}, u32[]{:S(2)}) collective-permute-start(bf16[2,4,128,384]{3,2,1,0:T(8,128)(2,1)} %get-tuple-element.63), channel_id=1, source_target_pairs={{0,4},{4,0},{8,12},{12,8},{16,20},{20,16},{24,28},{28,24},{1,5},{5... | collective-permute-start | bytes 2359304 | tf_op jit(solution)/shard_map/ppermute | solution.py:31
  156.7 20.7 %collective-permute-start.46 = (bf16[2,384,512]{2,1,0:T(8,128)(2,1)}, bf16[2,384,512]{2,1,0:T(8,128)(2,1)S(1)}, u32[]{:S(2)}, u32[]{:S(2)}) collective-permute-start(bf16[2,384,512]{2,1,0:T(8,128)(2,1)} %get-tuple-element.69), channel_id=1, source_target_pairs={{0,2},{1,3},{2,0},{3,1},{4,6},{5,7},{6,4},{7,5},{8,10},{9,11},{10,... | collective-permute-start | bytes 2359304 | tf_op jit(solution)/shard_map/ppermute | solution.py:31
  158.7 19.5 %collective-permute-start.29 = (bf16[2,2,2,128,384]{4,3,2,1,0:T(8,128)(2,1)S(1)}, bf16[2,2,2,128,384]{4,3,2,1,0:T(8,128)(2,1)S(1)}, u32[]{:S(2)}, u32[]{:S(2)}) collective-permute-start(bf16[2,2,2,128,384]{4,3,2,1,0:T(8,128)(2,1)S(1)} %copy-done.55), channel_id=1, source_target_pairs={{0,8},{4,12},{8,0},{12,4},{16,24},{20,28},{24,16},{28,20},{1,9},{5... | collective-permute-start | bytes 2359304 | tf_op jit(solution)/shard_map/ppermute | solution.py:31
  162.1 17.9 %collective-permute-start.37 = (bf16[2,4,128,384]{3,2,1,0:T(8,128)(2,1)S(1)}, bf16[2,4,128,384]{3,2,1,0:T(8,128)(2,1)S(1)}, u32[]{:S(2)}, u32[]{:S(2)}) collective-permute-start(bf16[2,4,128,384]{3,2,1,0:T(8,128)(2,1)S(1)} %copy-done.54), channel_id=1, source_target_pairs={{0,4},{4,0},{8,12},{12,8},{16,20},{20,16},{24,28},{28,24},{1,5},{5... | collective-permute-start | bytes 2359304 | tf_op jit(solution)/shard_map/ppermute | solution.py:31
  164.4 29.8 %collective-permute-start.45 = (bf16[2,384,512]{2,1,0:T(8,128)(2,1)S(1)}, bf16[2,384,512]{2,1,0:T(8,128)(2,1)S(1)}, u32[]{:S(2)}, u32[]{:S(2)}) collective-permute-start(bf16[2,384,512]{2,1,0:T(8,128)(2,1)S(1)} %copy-done.53), channel_id=1, source_target_pairs={{0,2},{1,3},{2,0},{3,1},{4,6},{5,7},{6,4},{7,5},{8,10},{9,11},{10,... | collective-permute-start | bytes 2359304 | tf_op jit(solution)/shard_map/ppermute | solution.py:31
  167.4 152.0 %collective-permute-start.3 = (bf16[1024,1024]{1,0:T(8,128)(2,1)S(1)}, bf16[1024,1024]{1,0:T(8,128)(2,1)}, u32[]{:S(2)}, u32[]{:S(2)}) collective-permute-start(bf16[1024,1024]{1,0:T(8,128)(2,1)S(1)} %get-tuple-element.45), channel_id=1, source_target_pairs={{0,1},{1,0},{2,3},{3,2},{4,5},{5,4},{6,7},{7,6},{8,9},{9,8},{10,11... | collective-permute-start | bytes 6291464 | tf_op jit(solution)/shard_map/ppermute | solution.py:31
  177.4 25.3 %collective-permute-start.34 = (bf16[2,2,128,384]{3,2,1,0:T(8,128)(2,1)S(1)}, bf16[2,2,128,384]{3,2,1,0:T(8,128)(2,1)S(1)}, u32[]{:S(2)}, u32[]{:S(2)}) collective-permute-start(bf16[2,2,128,384]{3,2,1,0:T(8,128)(2,1)S(1)} %slice_bitcast_fusion.10), channel_id=1, source_target_pairs={{0,2},{1,3},{2,0},{3,1},{4,6},{5,7},{6,4},{7,5},{8,10},{9,11},{10,... | collective-permute-start | bytes 1179656 | tf_op jit(solution)/shard_map/ppermute | solution.py:31
  178.3 60.3 %collective-permute-start.42 = (bf16[4,128,384]{2,1,0:T(8,128)(2,1)S(1)}, bf16[4,128,384]{2,1,0:T(8,128)(2,1)S(1)}, u32[]{:S(2)}, u32[]{:S(2)}) collective-permute-start(bf16[4,128,384]{2,1,0:T(8,128)(2,1)S(1)} %slice_bitcast_fusion.4), channel_id=1, source_target_pairs={{0,2},{1,3},{2,0},{3,1},{4,6},{5,7},{6,4},{7,5},{8,10},{9,11},{10,... | collective-permute-start | bytes 1179656 | tf_op jit(solution)/shard_map/ppermute | solution.py:31
  180.1 39.4 %collective-permute-start.32 = (bf16[2,2,128,384]{3,2,1,0:T(8,128)(2,1)S(1)}, bf16[2,2,128,384]{3,2,1,0:T(8,128)(2,1)S(1)}, u32[]{:S(2)}, u32[]{:S(2)}) collective-permute-start(bf16[2,2,128,384]{3,2,1,0:T(8,128)(2,1)S(1)} %slice_bitcast_fusion.12), channel_id=1, source_target_pairs={{0,2},{1,3},{2,0},{3,1},{4,6},{5,7},{6,4},{7,5},{8,10},{9,11},{10,... | collective-permute-start | bytes 1179656 | tf_op jit(solution)/shard_map/ppermute | solution.py:31
  194.2 45.5 %collective-permute-start.40 = (bf16[4,128,384]{2,1,0:T(8,128)(2,1)S(1)}, bf16[4,128,384]{2,1,0:T(8,128)(2,1)S(1)}, u32[]{:S(2)}, u32[]{:S(2)}) collective-permute-start(bf16[4,128,384]{2,1,0:T(8,128)(2,1)S(1)} %slice_bitcast_fusion.6), channel_id=1, source_target_pairs={{0,2},{1,3},{2,0},{3,1},{4,6},{5,7},{6,4},{7,5},{8,10},{9,11},{10,... | collective-permute-start | bytes 1179656 | tf_op jit(solution)/shard_map/ppermute | solution.py:31
  202.7 33.7 %collective-permute-start.30 = (bf16[2,2,128,384]{3,2,1,0:T(8,128)(2,1)S(1)}, bf16[2,2,128,384]{3,2,1,0:T(8,128)(2,1)S(1)}, u32[]{:S(2)}, u32[]{:S(2)}) collective-permute-start(bf16[2,2,128,384]{3,2,1,0:T(8,128)(2,1)S(1)} %slice_bitcast_fusion.14), channel_id=1, source_target_pairs={{0,2},{1,3},{2,0},{3,1},{4,6},{5,7},{6,4},{7,5},{8,10},{9,11},{10,... | collective-permute-start | bytes 1179656 | tf_op jit(solution)/shard_map/ppermute | solution.py:31
  219.5 22.7 %collective-permute-start.38 = (bf16[4,128,384]{2,1,0:T(8,128)(2,1)S(1)}, bf16[4,128,384]{2,1,0:T(8,128)(2,1)S(1)}, u32[]{:S(2)}, u32[]{:S(2)}) collective-permute-start(bf16[4,128,384]{2,1,0:T(8,128)(2,1)S(1)} %slice_bitcast_fusion.8), channel_id=1, source_target_pairs={{0,2},{1,3},{2,0},{3,1},{4,6},{5,7},{6,4},{7,5},{8,10},{9,11},{10,... | collective-permute-start | bytes 1179656 | tf_op jit(solution)/shard_map/ppermute | solution.py:31
  236.4 42.2 %collective-permute-start.48 = (bf16[2,576,512]{2,1,0:T(8,128)(2,1)}, bf16[2,576,512]{2,1,0:T(8,128)(2,1)}, u32[]{:S(2)}, u32[]{:S(2)}) collective-permute-start(bf16[2,576,512]{2,1,0:T(8,128)(2,1)} %broadcast_select_fusion), channel_id=1, source_target_pairs={{0,4},{4,0},{8,12},{12,8},{16,20},{20,16},{24,28},{28,24},{1,5},{5... | collective-permute-start | bytes 3538952 | tf_op jit(solution)/shard_map/ppermute | solution.py:31
  238.6 34.1 %collective-permute-start.35 = (bf16[3,2,128,384]{3,2,1,0:T(8,128)(2,1)}, bf16[3,2,128,384]{3,2,1,0:T(8,128)(2,1)}, u32[]{:S(2)}, u32[]{:S(2)}) collective-permute-start(bf16[3,2,128,384]{3,2,1,0:T(8,128)(2,1)} %slice_bitcast_fusion.2), channel_id=1, source_target_pairs={{0,4},{4,0},{8,12},{12,8},{16,20},{20,16},{24,28},{28,24},{1,5},{5... | collective-permute-start | bytes 1769480 | tf_op jit(solution)/shard_map/ppermute | solution.py:31
  244.3 32.6 %collective-permute-start.43 = (bf16[3,2,128,384]{3,2,0,1:T(8,128)(2,1)}, bf16[3,2,128,384]{3,2,0,1:T(8,128)(2,1)}, u32[]{:S(2)}, u32[]{:S(2)}) collective-permute-start(bf16[3,2,128,384]{3,2,0,1:T(8,128)(2,1)} %bitcast.313), channel_id=1, source_target_pairs={{0,8},{4,12},{8,0},{12,4},{16,24},{20,28},{24,16},{28,20},{1,9},{5... | collective-permute-start | bytes 1769480 | tf_op jit(solution)/shard_map/ppermute | solution.py:31
  272.7 45.2 %collective-permute-start.4 = (bf16[1024,1024]{1,0:T(8,128)(2,1)S(1)}, bf16[1024,1024]{1,0:T(8,128)(2,1)S(1)}, u32[]{:S(2)}, u32[]{:S(2)}) collective-permute-start(bf16[1024,1024]{1,0:T(8,128)(2,1)S(1)} %get-tuple-element.53), channel_id=1, source_target_pairs={{0,1},{1,0},{2,3},{3,2},{4,5},{5,4},{6,7},{7,6},{8,9},{9,8},{10,11... | collective-permute-start | bytes 6291464 | tf_op jit(solution)/shard_map/ppermute | solution.py:31
  274.3 35.4 %collective-permute-start.36 = (bf16[3,128,384]{2,1,0:T(8,128)(2,1)S(1)}, bf16[3,128,384]{2,1,0:T(8,128)(2,1)S(1)}, u32[]{:S(2)}, u32[]{:S(2)}) collective-permute-start(bf16[3,128,384]{2,1,0:T(8,128)(2,1)S(1)} %slice_bitcast_fusion.18), channel_id=1, source_target_pairs={{0,16},{4,20},{8,24},{12,28},{16,0},{20,4},{24,8},{28,12},{1,17},{... | collective-permute-start | bytes 884744 | tf_op jit(solution)/shard_map/ppermute | solution.py:31
  278.2 37.8 %collective-permute-start.44 = (bf16[3,128,384]{2,1,0:T(8,128)(2,1)S(1)}, bf16[3,128,384]{2,1,0:T(8,128)(2,1)S(1)}, u32[]{:S(2)}, u32[]{:S(2)}) collective-permute-start(bf16[3,128,384]{2,1,0:T(8,128)(2,1)S(1)} %slice_bitcast_fusion.16), channel_id=1, source_target_pairs={{0,16},{4,20},{8,24},{12,28},{16,0},{20,4},{24,8},{28,12},{1,17},{... | collective-permute-start | bytes 884744 | tf_op jit(solution)/shard_map/ppermute | solution.py:31
  280.4 124.3 %collective-permute-start.49 = (bf16[576,512]{1,0:T(8,128)(2,1)S(1)}, bf16[576,512]{1,0:T(8,128)(2,1)S(1)}, u32[]{:S(2)}, u32[]{:S(2)}) collective-permute-start(bf16[576,512]{1,0:T(8,128)(2,1)S(1)} %slice_bitcast_fusion), channel_id=1, source_target_pairs={{0,16},{4,20},{8,24},{12,28},{16,0},{20,4},{24,8},{28,12},{1,17},{... | collective-permute-start | bytes 1769480 | tf_op jit(solution)/shard_map/ppermute | solution.py:31
  337.0 64.0 %collective-permute-start.24 = (bf16[1024,512]{1,0:T(8,128)(2,1)}, bf16[1024,512]{1,0:T(8,128)(2,1)}, u32[]{:S(2)}, u32[]{:S(2)}) collective-permute-start(bf16[1024,512]{1,0:T(8,128)(2,1)} %convolution_convert_fusion.1), channel_id=1, source_target_pairs={{0,1},{1,0},{2,3},{3,2},{4,5},{5,4},{6,7},{7,6},{8,9},{9,8},{10,11... | collective-permute-start | bytes 3145736 | tf_op jit(solution)/shard_map/ppermute | solution.py:31
  392.8 36.9 %collective-permute-start.11 = (bf16[1024,1536]{1,0:T(8,128)(2,1)S(1)}, bf16[1024,1536]{1,0:T(8,128)(2,1)S(1)}, u32[]{:S(2)}, u32[]{:S(2)}) collective-permute-start(bf16[1024,1536]{1,0:T(8,128)(2,1)S(1)} %convolution_convert_fusion), channel_id=1, source_target_pairs={{0,1},{1,0},{2,3},{3,2},{4,5},{5,4},{6,7},{7,6},{8,9},{9,8},{10,11... | collective-permute-start | bytes 9437192 | tf_op jit(solution)/shard_map/ppermute | solution.py:31
  403.7 11.8 %collective-permute-start.25 = (bf16[2,2,2,128,256]{4,3,1,0,2:T(8,128)(2,1)S(1)}, bf16[2,2,2,128,256]{4,3,1,0,2:T(8,128)(2,1)S(1)}, u32[]{:S(2)}, u32[]{:S(2)}) collective-permute-start(bf16[2,2,2,128,256]{4,3,1,0,2:T(8,128)(2,1)S(1)} %bitcast.339), channel_id=1, source_target_pairs={{0,4},{4,0},{8,12},{12,8},{16,20},{20,16},{24,28},{28,24},{1,5},{5... | collective-permute-start | bytes 1572872 | tf_op jit(solution)/shard_map/ppermute | solution.py:31
  405.0 13.1 %collective-permute-start.50 = (bf16[576,512]{1,0:T(8,128)(2,1)S(1)}, bf16[576,512]{1,0:T(8,128)(2,1)S(1)}, u32[]{:S(2)}, u32[]{:S(2)}) collective-permute-start(bf16[576,512]{1,0:T(8,128)(2,1)S(1)} %fusion.25), channel_id=1, source_target_pairs={{1,9},{3,11},{5,13},{7,15},{8,0},{10,2},{12,4},{14,6},{17,25},{19,... | collective-permute-start | bytes 1769480 | tf_op jit(solution)/shard_map/ppermute | solution.py:619
  423.1 11.8 %collective-permute-start.51 = (bf16[576,256]{1,0:T(8,128)(2,1)S(1)}, bf16[576,256]{1,0:T(8,128)(2,1)S(1)}, u32[]{:S(2)}, u32[]{:S(2)}) collective-permute-start(bf16[576,256]{1,0:T(8,128)(2,1)S(1)} %select_convert_fusion), channel_id=1, source_target_pairs={{0,1},{2,3},{4,5},{6,7},{9,8},{11,10},{13,12},{15,14},{16,17},{18,... | collective-permute-start | bytes 884744 | tf_op jit(solution)/shard_map/ppermute | solution.py:628
  434.4 10.4 %collective-permute-start.12 = (bf16[2,2,2,128,256]{4,3,0,1,2:T(8,128)(2,1)S(1)}, bf16[2,2,2,128,256]{4,3,0,1,2:T(8,128)(2,1)S(1)}, u32[]{:S(2)}, u32[]{:S(2)}) collective-permute-start(bf16[2,2,2,128,256]{4,3,0,1,2:T(8,128)(2,1)S(1)} %copy_bitcast_fusion.8), channel_id=1, source_target_pairs={{0,2},{1,3},{2,0},{3,1},{4,6},{5,7},{6,4},{7,5},{8,10},{9,11},{10,... | collective-permute-start | bytes 1572872 | tf_op jit(solution)/shard_map/ppermute | solution.py:31
  436.6 11.0 %collective-permute-start.20 = (bf16[2,2,2,128,256]{4,3,1,2,0:T(8,128)(2,1)S(1)}, bf16[2,2,2,128,256]{4,3,1,2,0:T(8,128)(2,1)S(1)}, u32[]{:S(2)}, u32[]{:S(2)}) collective-permute-start(bf16[2,2,2,128,256]{4,3,1,2,0:T(8,128)(2,1)S(1)} %bitcast.338), channel_id=1, source_target_pairs={{0,8},{4,12},{8,0},{12,4},{16,24},{20,28},{24,16},{28,20},{1,9},{5... | collective-permute-start | bytes 1572872 | tf_op jit(solution)/shard_map/ppermute | solution.py:31
  437.2 14.9 %collective-permute-start.16 = (bf16[2,2,2,128,256]{4,3,1,0,2:T(8,128)(2,1)S(1)}, bf16[2,2,2,128,256]{4,3,1,0,2:T(8,128)(2,1)S(1)}, u32[]{:S(2)}, u32[]{:S(2)}) collective-permute-start(bf16[2,2,2,128,256]{4,3,1,0,2:T(8,128)(2,1)S(1)} %bitcast.337), channel_id=1, source_target_pairs={{0,4},{4,0},{8,12},{12,8},{16,20},{20,16},{24,28},{28,24},{1,5},{5... | collective-permute-start | bytes 1572872 | tf_op jit(solution)/shard_map/ppermute | solution.py:31
  (81 other events, 572.1 us)

commit v2 on v1

--- a/solution.py
+++ b/solution.py
@@ -161,7 +161,7 @@
         for copy in outs:
             copy.wait()
 
-    any_spec = pl.BlockSpec(memory_space=pl.ANY)
+    any_spec = pl.BlockSpec(memory_space=pltpu.HBM)
     low = jnp.bfloat16
     both = 2 * tokens
     flops = 6 * 2 * both * width * span
@@ -274,7 +274,7 @@
         for t in range(max(0, tiles - 2), tiles):
             out_copy(t, t % 2).wait()
 
-    any_spec = pl.BlockSpec(memory_space=pl.ANY)
+    any_spec = pl.BlockSpec(memory_space=pltpu.HBM)
     low = jnp.bfloat16
     wshape = (width, span) if across else (span, width)
     return pl.pallas_call(
@@ -303,6 +303,269 @@
     )(place, *[item for group in groups for item in group], *weights)
 
 
+LOW = jnp.bfloat16
+FULL = jnp.float32
+MARGIN = 16
+
+
+def whole(shape):
+    return pl.BlockSpec(shape, lambda *_: (0,) * len(shape), pipeline_mode=pl.Buffered(1))
+
+
+def mixer_forward(marks, hidden, rim, in_weight, out_weight, scales):
+    tokens, width = hidden.shape
+    tile = 256
+    per_row = tokens // 2 // tile
+    steps = tokens // tile
+
+    def kernel(
+        marks_ref, hidden_ref, rim_ref, in_ref, out_ref, scale_ref,
+        normed_out, gate_out, open_out, value_out, product_out, mixed_out, residual_out, next_out, before_out,
+        ext, carry,
+    ):
+        at = pl.program_id(0) % per_row
+        tile_in = hidden_ref[...].astype(FULL)
+
+        @pl.when(at == 0)
+        def _():
+            carry[...] = rim_ref[...].astype(FULL)
+
+        source = jnp.concatenate([carry[...], tile_in], axis=0)
+        carry[...] = tile_in[tile - MARGIN :]
+        inverse = lax.rsqrt(jnp.mean(source * source, axis=1, keepdims=True) + EPS)
+        normed = narrow(source * inverse * scale_ref[0:1, :])
+        gate = jnp.dot(normed, in_ref[:, :width], preferred_element_type=FULL)
+        value = jnp.dot(normed, in_ref[:, 2 * width :], preferred_element_type=FULL)
+        product = narrow(gate * value)
+        ext[...] = product.astype(FULL)
+        opened = jnp.dot(normed[MARGIN:], in_ref[:, width : 2 * width], preferred_element_type=FULL)
+        conv = (
+            scale_ref[2:3, :] * ext[MARGIN:, :]
+            + marks_ref[:, 0:1] * scale_ref[3:4, :] * ext[MARGIN - 1 : MARGIN - 1 + tile, :]
+            + marks_ref[:, 1:2] * scale_ref[4:5, :] * ext[MARGIN - 2 : MARGIN - 2 + tile, :]
+        )
+        mixed = narrow(opened * conv)
+        residual = tile_in + marks_ref[:, 2:3] * jnp.dot(mixed, out_ref[...], preferred_element_type=FULL)
+        inverse_two = lax.rsqrt(jnp.mean(residual * residual, axis=1, keepdims=True) + EPS)
+        next_out[...] = narrow(residual * inverse_two * scale_ref[1:2, :])
+        normed_out[...] = normed[MARGIN:]
+        gate_out[...] = narrow(gate[MARGIN:])
+        open_out[...] = narrow(opened)
+        value_out[...] = narrow(value[MARGIN:])
+        product_out[...] = product[MARGIN:]
+        mixed_out[...] = mixed
+        residual_out[...] = residual
+
+        @pl.when(at == 0)
+        def _():
+            before_out[...] = product[:MARGIN]
+
+    def rows(last, size=tile):
+        return pl.BlockSpec((size, last), lambda i: (i, 0))
+
+    row_spec = pl.BlockSpec((MARGIN, width), lambda i: (i // per_row, 0))
+    return pl.pallas_call(
+        kernel,
+        grid=(steps,),
+        in_specs=[rows(8), rows(width), row_spec, whole(in_weight.shape), whole(out_weight.shape), whole(scales.shape)],
+        out_specs=[rows(width)] * 8 + [row_spec],
+        out_shape=[jax.ShapeDtypeStruct((tokens, width), LOW)] * 6
+        + [jax.ShapeDtypeStruct((tokens, width), FULL), jax.ShapeDtypeStruct((tokens, width), LOW)]
+        + [jax.ShapeDtypeStruct((2 * MARGIN, width), LOW)],
+        scratch_shapes=[pltpu.VMEM((tile + MARGIN, width), FULL), pltpu.VMEM((MARGIN, width), FULL)],
+        compiler_params=pltpu.CompilerParams(vmem_limit_bytes=44 << 20),
+        cost_estimate=pl.CostEstimate(flops=8 * tokens * width * width, bytes_accessed=28 << 20, transcendentals=0),
+        name="mixer_forward",
+    )(marks, hidden, rim, in_weight, out_weight, scales)
+
+
+def mixer_middle(marks, own, other, residual, cotangent, product, before, opened, out_weight, scales):
+    tokens, width = own.shape
+    tile = 256
+    per_row = tokens // 2 // tile
+    steps = tokens // tile
+
+    def kernel(
+        marks_ref, own_ref, other_ref, residual_ref, cot_ref, product_ref, before_ref, open_ref, out_ref, scale_ref,
+        grad_out, mixer_out, open_grad_out, conv_out, sums_out,
+        ext, carry,
+    ):
+        step = pl.program_id(0)
+        at = step % per_row
+
+        @pl.when(at == 0)
+        def _():
+            carry[...] = before_ref[...].astype(FULL)
+
+        @pl.when(step == 0)
+        def _():
+            sums_out[...] = jnp.zeros_like(sums_out)
+
+        grad = own_ref[...].astype(FULL) + other_ref[...].astype(FULL)
+        residual = residual_ref[...]
+        inverse = lax.rsqrt(jnp.mean(residual * residual, axis=1, keepdims=True) + EPS)
+        sums_out[1:2, :] += jnp.sum(grad * (residual * inverse), axis=0, keepdims=True)
+        scaled = scale_ref[1:2, :] * grad
+        lean = (inverse * inverse * inverse) * jnp.mean(scaled * residual, axis=1, keepdims=True)
+        residual_grad = cot_ref[...].astype(FULL) + inverse * scaled - residual * lean
+        grad_out[...] = residual_grad
+        mixer = narrow(marks_ref[:, 2:3] * residual_grad)
+        mixer_out[...] = mixer
+        mixed = contract_cols(mixer, out_ref[...])
+        product = product_ref[...].astype(FULL)
+        ext[:MARGIN, :] = carry[...]
+        ext[MARGIN:, :] = product
+        carry[...] = product[tile - MARGIN :]
+        one = marks_ref[:, 0:1] * ext[MARGIN - 1 : MARGIN - 1 + tile, :]
+        two = marks_ref[:, 1:2] * ext[MARGIN - 2 : MARGIN - 2 + tile, :]
+        conv = scale_ref[2:3, :] * product + scale_ref[3:4, :] * one + scale_ref[4:5, :] * two
+        open_grad_out[...] = narrow(mixed * conv)
+        conv_grad = mixed * open_ref[...].astype(FULL)
+        conv_out[...] = conv_grad
+        sums_out[2:3, :] += jnp.sum(conv_grad * product, axis=0, keepdims=True)
+        sums_out[3:4, :] += jnp.sum(conv_grad * one, axis=0, keepdims=True)
+        sums_out[4:5, :] += jnp.sum(conv_grad * two, axis=0, keepdims=True)
+
+    def rows(last):
+        return pl.BlockSpec((tile, last), lambda i: (i, 0))
+
+    row_spec = pl.BlockSpec((MARGIN, width), lambda i: (i // per_row, 0))
+    return pl.pallas_call(
+        kernel,
+        grid=(steps,),
+        in_specs=[rows(8)] + [rows(width)] * 5 + [row_spec, rows(width), whole(out_weight.shape), whole(scales.shape)],
+        out_specs=[rows(width)] * 4 + [pl.BlockSpec((8, width), lambda i: (0, 0))],
+        out_shape=[jax.ShapeDtypeStruct((tokens, width), kind) for kind in (FULL, LOW, LOW, FULL)]
+        + [jax.ShapeDtypeStruct((8, width), FULL)],
+        scratch_shapes=[pltpu.VMEM((tile + MARGIN, width), FULL), pltpu.VMEM((MARGIN, width), FULL)],
+        compiler_params=pltpu.CompilerParams(vmem_limit_bytes=44 << 20),
+        cost_estimate=pl.CostEstimate(flops=2 * tokens * width * width, bytes_accessed=32 << 20, transcendentals=0),
+        name="mixer_middle",
+    )(marks, own, other, residual, cotangent, product, before, opened, out_weight, scales)
+
+
+def project_grads(marks, conv_grad, after, gate, value, open_grad, scales):
+    tokens, width = conv_grad.shape
+    tile = 256
+    per_row = tokens // 2 // tile
+    steps = tokens // tile
+
+    def kernel(marks_ref, conv_ref, after_ref, gate_ref, value_ref, open_ref, scale_ref, grad_out, ext, carry):
+        at = (steps - 1 - pl.program_id(0)) % per_row
+
+        @pl.when(at == per_row - 1)
+        def _():
+            carry[...] = after_ref[...]
+
+        grad = conv_ref[...]
+        ext[:tile, :] = grad
+        ext[tile:, :] = carry[...]
+        carry[...] = grad[:8]
+        product_grad = (
+            scale_ref[2:3, :] * grad
+            + marks_ref[:, 3:4] * scale_ref[3:4, :] * ext[1 : 1 + tile, :]
+            + marks_ref[:, 4:5] * scale_ref[4:5, :] * ext[2 : 2 + tile, :]
+        )
+        grad_out[:, :width] = narrow(product_grad * value_ref[...].astype(FULL))
+        grad_out[:, width : 2 * width] = open_ref[...]
+        grad_out[:, 2 * width :] = narrow(product_grad * gate_ref[...].astype(FULL))
+
+    def rows(last):
+        return pl.BlockSpec((tile, last), lambda i: (steps - 1 - i, 0))
+
+    row_spec = pl.BlockSpec((8, width), lambda i: ((steps - 1 - i) // per_row, 0))
+    return pl.pallas_call(
+        kernel,
+        grid=(steps,),
+        in_specs=[rows(8), rows(width), row_spec, rows(width), rows(width), rows(width), whole(scales.shape)],
+        out_specs=rows(3 * width),
+        out_shape=jax.ShapeDtypeStruct((tokens, 3 * width), LOW),
+        scratch_shapes=[pltpu.VMEM((tile + 8, width), FULL), pltpu.VMEM((8, width), FULL)],
+        compiler_params=pltpu.CompilerParams(vmem_limit_bytes=32 << 20),
+        cost_estimate=pl.CostEstimate(flops=10 * tokens * width, bytes_accessed=16 << 20, transcendentals=0),
+        name="project_grads",
+    )(marks, conv_grad, after, gate, value, open_grad, scales)
+
+
+def pair_grads(place, left, right, cores, name):
+    tokens, width = left.shape
+    block = right.shape[1] // 4
+    eighth = width // 8
+    count = len(cores)
+    step = 256
+
+    def kernel(place_ref, left_ref, right_ref, *outs):
+        at = pl.program_id(0)
+        for n in range(block // step):
+            total = narrow(contract_rows(left_ref[...], right_ref[:, n * step : (n + 1) * step]))
+            for c in range(count):
+                @pl.when(at // 2 == c)
+                def _():
+                    for i in range(8):
+                        outs[c][0, place_ref[2 + i], :, n * step : (n + 1) * step] = total[i * eighth : (i + 1) * eighth]
+
+    def column(i, place_ref):
+        return (0, place_ref[14 + 2 * cores[0] + i])
+
+    def out_spec(c):
+        return pl.BlockSpec(
+            (1, 8, eighth, block), lambda i, place_ref: (jnp.clip(i - 2 * c, 0, 1), 0, 0, 0)
+        )
+
+    return pl.pallas_call(
+        kernel,
+        grid_spec=pltpu.PrefetchScalarGridSpec(
+            num_scalar_prefetch=1,
+            grid=(2 * count,),
+            in_specs=[
+                pl.BlockSpec((tokens, width), lambda i, place_ref: (0, 0), pipeline_mode=pl.Buffered(1)),
+                pl.BlockSpec((tokens, block), column),
+            ],
+            out_specs=[out_spec(c) for c in range(count)],
+        ),
+        out_shape=[jax.ShapeDtypeStruct((2, 8, eighth, block), LOW)] * count,
+        compiler_params=pltpu.CompilerParams(vmem_limit_bytes=32 << 20),
+        cost_estimate=pl.CostEstimate(
+            flops=count * 4 * tokens * width * block, bytes_accessed=8 << 20, transcendentals=0
+        ),
+        name=name,
+    )(place, left, right)
+
+
+def mixer_backward(project_grad, in_weight, hidden, residual_grad, sums, scales):
+    tokens, width = hidden.shape
+    tile = 256
+    steps = tokens // tile
+
+    def kernel(grad_ref, in_ref, hidden_ref, residual_ref, sums_ref, scale_ref, input_out, sums_out):
+        @pl.when(pl.program_id(0) == 0)
+        def _():
+            sums_out[...] = sums_ref[...]
+
+        normed_grad = contract_cols(grad_ref[...], in_ref[...])
+        source = hidden_ref[...].astype(FULL)
+        inverse = lax.rsqrt(jnp.mean(source * source, axis=1, keepdims=True) + EPS)
+        sums_out[0:1, :] += jnp.sum(normed_grad * (source * inverse), axis=0, keepdims=True)
+        scaled = scale_ref[0:1, :] * normed_grad
+        lean = (inverse * inverse * inverse) * jnp.mean(scaled * source, axis=1, keepdims=True)
+        input_out[...] = narrow(residual_ref[...] + inverse * scaled - source * lean)
+
+    def rows(last):
+        return pl.BlockSpec((tile, last), lambda i: (i, 0))
+
+    small = pl.BlockSpec((8, width), lambda i: (0, 0))
+    return pl.pallas_call(
+        kernel,
+        grid=(steps,),
+        in_specs=[rows(3 * width), whole(in_weight.shape), rows(width), rows(width), small, whole(scales.shape)],
+        out_specs=[rows(width), small],
+        out_shape=[jax.ShapeDtypeStruct((tokens, width), LOW), jax.ShapeDtypeStruct((8, width), FULL)],
+        compiler_params=pltpu.CompilerParams(vmem_limit_bytes=32 << 20),
+        cost_estimate=pl.CostEstimate(flops=6 * tokens * width * width, bytes_accessed=20 << 20, transcendentals=0),
+        name="mixer_backward",
+    )(project_grad, in_weight, hidden, residual_grad, sums, scales)
+
+
 def plain(
     hidden_in,
     mixer_gain,
@@ -490,15 +753,17 @@
     )
 
 
+LINKS = {"x": ("row", 2), "y": ("seq", 1), "z0": ("seq", 2), "z1": ("seq", 4)}
+
+
 def settle(value, order):
-    names = ["x", "z1", "z0", "y"]
-    links = {"x": ("row", 2), "y": ("seq", 1), "z0": ("seq", 2), "z1": ("seq", 4)}
-    for name in order:
+    names = [name for name in ("x", "z1", "z0", "y") if name in order[len(order) - value.ndim + 2 :]]
+    for name in order[len(order) - len(names) :]:
         at = names.index(name)
         names.remove(name)
         give = lax.index_in_dim(value, 0, at, keepdims=False)
         keep = lax.index_in_dim(value, 1, at, keepdims=False)
-        value = wide(keep, swapped(narrow(give), *links[name]))
+        value = wide(keep, swapped(narrow(give), *LINKS[name]))
         if names:
             value = narrow(value)
     return value
@@ -532,87 +797,150 @@
         [row ^ 2, row]
         + [i ^ seq ^ 7 for i in range(8)]
         + [1 - row_x, row_x, 1 - ((1 - row_x) ^ seq_z1), 1 - (row_x ^ seq_z1)]
+        + [row ^ 3, row ^ 1, row ^ 2, row]
     ).astype(jnp.int32)
-    offset = seq * span_length
-    positions = offset + jnp.arange(span_length, dtype=jnp.int32)
+    positions = seq * span_length + jnp.arange(span_length, dtype=jnp.int32)
     starts = jnp.cumsum(document_lengths, axis=1) - document_lengths
-    is_start = jnp.any(positions[None, :, None] == starts[:, None, :], axis=2)
-    before = jnp.any((positions - 1)[None, :, None] == starts[:, None, :], axis=2)
-    keep_one = (1.0 - is_start.astype(jnp.float32))[:, :, None]
-    keep_two = keep_one * (1.0 - before.astype(jnp.float32))[:, :, None]
-    valid_mask = (
-        (positions[None, :] < valid_tokens[:, None]).astype(jnp.float32).reshape(token_count, 1)
-    )
-    mixer_scale = mixer_gain.astype(jnp.float32)
-    feed_scale = feed_gain.astype(jnp.float32)
-    kernel = conv_kernel.astype(jnp.float32)
-    upstream = cotangent.astype(jnp.float32).reshape(token_count, model_width)
-    feed_grad = narrow(valid_mask * upstream)
+
+    def unstarted(shift):
+        return 1.0 - jnp.any((positions + shift)[None, :, None] == starts[:, None, :], axis=2).astype(FULL)
+
+    here, last, one_on, two_on = (unstarted(shift) for shift in (0, -1, 1, 2))
+    valid = (positions[None, :] < valid_tokens[:, None]).astype(FULL)
+    blank = jnp.zeros_like(valid)
+    marks = jnp.stack([here, here * last, valid, one_on, two_on * one_on, blank, blank, blank], axis=2).reshape(
+        token_count, 8
+    )
+    valid_mask = marks[:, 2:3]
+    scales = jnp.concatenate(
+        [mixer_gain[None], feed_gain[None], conv_kernel.T, jnp.zeros((3, model_width), conv_kernel.dtype)]
+    ).astype(FULL)
+    hidden = hidden_in.reshape(token_count, model_width)
+    upstream = cotangent.reshape(token_count, model_width)
+    rim = passed_along(hidden_in[:, span_length - 2 :, :], "seq", 1)
+    rim = jnp.pad(rim, ((0, 0), (MARGIN - 2, 0), (0, 0))).reshape(row_count * MARGIN, model_width)
+    feed_grad = narrow(valid_mask * upstream.astype(FULL))
     other_grad = swapped(feed_grad, "row", 1)
-
-    source = hidden_in.astype(jnp.float32).reshape(token_count, model_width)
-    inverse_one = lax.rsqrt(jnp.mean(source * source, axis=1, keepdims=True) + EPS)
-    normed = (source * inverse_one * mixer_scale).astype(jnp.bfloat16)
-    project = jnp.dot(normed, in_weight, preferred_element_type=jnp.float32)
-    input_gate = project[:, :model_width]
-    output_gate = project[:, model_width : 2 * model_width]
-    values = project[:, 2 * model_width :]
-    product = (
-        (input_gate * values).astype(jnp.bfloat16).reshape(row_count, span_length, model_width)
-    )
-    rim_values = passed_along(product[:, span_length - 2 :, :], "seq", 1)
-    extended = jnp.concatenate([rim_values, product], axis=1).astype(jnp.float32)
-    tap_zero = extended[:, 2:, :]
-    tap_one = keep_one * extended[:, 1:-1, :]
-    tap_two = keep_two * extended[:, :-2, :]
-    conv_out = (kernel[:, 0] * tap_zero + kernel[:, 1] * tap_one + kernel[:, 2] * tap_two).reshape(
-        token_count, model_width
-    )
-    mixed_in = (output_gate * conv_out).astype(jnp.bfloat16)
-    mixer_out = jnp.dot(mixed_in, out_weight, preferred_element_type=jnp.float32)
-    residual = source + valid_mask * mixer_out
-    inverse_two = lax.rsqrt(jnp.mean(residual * residual, axis=1, keepdims=True) + EPS)
-    normed_two = (residual * inverse_two * feed_scale).astype(jnp.bfloat16)
+    normed, input_gate, output_gate, values, product, mixed_in, residual, normed_two, before = mixer_forward(
+        marks, hidden, rim, in_weight, out_weight, scales
+    )
     other_normed = swapped(normed_two, "row", 1)
 
-    acts, gates, ups, gate_parts, up_parts, down_parts = [], [], [], [], [], []
-    for chunk in range(chunks):
-        act, gate_grad, up_grad, gs, gk, us, uk, ds, dk = feed_chunk(
-            place, normed_two, other_normed, feed_grad, other_grad, gate_weight, up_weight, down_weight, chunk, chunks
+    def chunk_grads(start, chunk):
+        return feed_chunk(
+            start, normed_two, other_normed, feed_grad, other_grad, gate_weight, up_weight, down_weight, chunk, chunks
         )
-        acts.append(act)
-        gates.append(gate_grad)
-        ups.append(up_grad)
-        gate = narrow(wide(gk, swapped(gs, "seq", 2)))
-        gate = narrow(wide(gate[1], swapped(gate[0], "row", 2)))
-        gate_parts.append(gate)
-        up = narrow(wide(uk, swapped(us, "seq", 1)))
-        up = narrow(wide(up[1], swapped(up[0], "row", 2)))
-        up_parts.append(up)
-        down_parts.append(narrow(wide(dk, swapped(ds, "row", 2))))
-    own_ntg, give_ntg = feed_sum(place, [gates, ups], [gate_weight, up_weight], True, block, "normed_two_grad")
+
+    def sent(made):
+        gs, us, ds = made[3], made[5], made[7]
+        return swapped(gs, "seq", 2), swapped(us, "seq", 1), swapped(ds, "row", 2)
+
+    def first_sums(made, taken, behind):
+        (gk, uk, dk, taken), _ = lax.optimization_barrier(((made[4], made[6], made[8], taken), behind))
+        gate, up, down = (wide(keep, take) for keep, take in zip((gk, uk, dk), taken))
+        return narrow(gate[0]), narrow(gate[1]), narrow(up[0]), narrow(up[1]), narrow(down)
+
+    def follow(value, *ahead):
+        return lax.optimization_barrier((value,) + ahead)[0]
+
+    made0 = chunk_grads(place, 0)
+    taken0 = sent(made0)
+    made1 = chunk_grads(follow(place, made0[0]), 1)
+    taken1 = sent(made1)
+    sums0 = first_sums(made0, taken0, made1[0])
+    gate0, up0 = swapped(sums0[0], "row", 2), swapped(sums0[2], "row", 2)
+    made2 = chunk_grads(follow(place, sums0), 2)
+    taken2 = sent(made2)
+    sums1 = first_sums(made1, taken1, made2[0])
+    gate1, up1 = swapped(sums1[0], "row", 2), swapped(sums1[2], "row", 2)
+    made = (made0, made1, made2)
+    acts, gates, ups = ([one[i] for one in made] for i in range(3))
+    own_ntg, give_ntg = feed_sum(
+        follow(place, sums1), [gates, ups], [gate_weight, up_weight], True, block, "normed_two_grad"
+    )
     take_ntg = swapped(give_ntg, "row", 1)
-    own_feed, give_feed = feed_sum(place, [acts], [down_weight], False, block, "feed_out")
+    sums2 = first_sums(made2, taken2, own_ntg)
+    gate2, up2 = swapped(sums2[0], "row", 2), swapped(sums2[2], "row", 2)
+    down = jnp.concatenate([sums0[4], sums1[4], sums2[4]], axis=1)
+    low_half, high_half = down[:, : block // 2], down[:, block // 2 :]
+    down_keep = jnp.where(seq_y == 0, low_half, high_half)
+    down_take = swapped(jnp.where(seq_y == 0, high_half, low_half), "seq", 1)
+    own_feed, give_feed = feed_sum(
+        follow(place, sums2), [acts], [down_weight], False, block, "feed_out"
+    )
     take_feed = swapped(give_feed, "row", 1)
+
+    residual_grad, mixer_grad, open_grad, conv_grad, sums = mixer_middle(
+        follow(marks, own_feed), own_ntg, take_ntg, residual, upstream, product, before, output_gate, out_weight, scales
+    )
+    after = passed_along(conv_grad.reshape(row_count, span_length, model_width)[:, :2, :], "seq", -1)
+    after = jnp.pad(after, ((0, 0), (0, 6), (0, 0))).reshape(row_count * 8, model_width)
+
+    (gate_take, up_take), _ = lax.optimization_barrier((([gate0, gate1, gate2], [up0, up1, up2]), mixer_grad))
+    sums_all = (sums0, sums1, sums2)
+    gate = jnp.stack([wide(one[1], take) for one, take in zip(sums_all, gate_take)])
+    gate_keep, gate_give = narrow(gate[:, :, 1]), narrow(gate[:, :, 0])
+    up = jnp.stack(
+        [wide(one[3], take).reshape(2, 2, model_width // 8, part) for one, take in zip(sums_all, up_take)]
+    )
+    up_keep, up_give = narrow(up[:, :, 1]), narrow(up[:, :, 0])
+    gate_take = swapped(gate_give, "seq", 1)
+    up_take = swapped(up_give, "seq", 2)
+
+    project_grad = project_grads(
+        follow(marks, gate_give, up_give), conv_grad, after, input_gate, values, open_grad, scales
+    )
+    (in_give,) = pair_grads(place, normed, project_grad, (0,), "in_grads_give")
+    in_take = swapped(in_give, "row", 1)
+    (in_keep,) = pair_grads(follow(place, in_give), normed, project_grad, (1,), "in_grads_keep")
+    out_give, out_keep = pair_grads(follow(place, in_keep), mixed_in, mixer_grad, (0, 1), "out_grads")
+
+    def sided(value):
+        return value.reshape(2, 2, 2, 2, value.shape[-2], value.shape[-1])
+
+    orders = (("x", "y", "z0", "z1"), ("y", "x", "z0", "z1"), ("z0", "x", "y", "z1"))
+    (in_keep, in_take), _ = lax.optimization_barrier(((in_keep, in_take), out_keep))
+    in_sum = sided(narrow(wide(in_keep, in_take)))
+    third = in_sum.shape[-1] // 3
+    names = ["x", "z1", "z0", "y"]
+    firsts = []
+    for i, order in enumerate(orders):
+        piece = in_sum[..., i * third : (i + 1) * third]
+        at = names.index(order[0])
+        firsts.append((lax.index_in_dim(piece, 1, at, False), lax.index_in_dim(piece, 0, at, False)))
+    in_moved = [swapped(give, *LINKS[order[0]]) for (_, give), order in zip(firsts, orders)]
+    out_take = swapped(out_give, "row", 1)
+    down = narrow(wide(down_keep, down_take))
+    down_keep, down_give = down[1], down[0]
+    down_take = swapped(down_give, "seq", 4)
+
+    input_grad, small = mixer_backward(
+        follow(project_grad, [give for _, give in firsts], down_give), in_weight, hidden, residual_grad, sums, scales
+    )
+    in_moved, _ = lax.optimization_barrier((in_moved, input_grad))
+    input_grad = input_grad.reshape(row_count, span_length, model_width)
+    in_part = jnp.concatenate(
+        [
+            settle(narrow(wide(keep, take)), order)
+            for (keep, _), take, order in zip(firsts, in_moved, orders)
+        ],
+        axis=1,
+    )
+    out_part = settle(sided(narrow(wide(out_keep, out_take))), ("y", "z0", "x", "z1"))
+    for axis, bit in (("row", 1), ("row", 2), ("seq", 1), ("seq", 2), ("seq", 4)):
+        small = small + swapped(small, axis, bit)
+    small = lax.dynamic_slice_in_dim(small, seq * (model_width // 8), model_width // 8, 1)
+
     output = narrow(residual + valid_mask * wide(own_feed, take_feed)).reshape(row_count, span_length, model_width)
-
-    gate = jnp.stack(gate_parts)
-    gate = narrow(wide(gate[:, :, 1], swapped(gate[:, :, 0], "seq", 1)))
-    gate = wide(gate[:, 1], swapped(gate[:, 0], "seq", 4))
+    (gate_take, up_take), _ = lax.optimization_barrier(((gate_take, up_take), input_grad))
+    gate = wide(gate_keep, gate_take)
+    gate = wide(narrow(gate[:, 1]), swapped(narrow(gate[:, 0]), "seq", 4))
     gate_part = jnp.concatenate([gate[i] for i in range(chunks)], axis=1)
-    up = jnp.stack(up_parts).reshape(chunks, 2, 2, model_width // 8, part)
-    up = narrow(wide(up[:, :, 1], swapped(up[:, :, 0], "seq", 2)))
-    up = wide(up[:, 1], swapped(up[:, 0], "seq", 4))
+    up = wide(up_keep, up_take)
+    up = wide(narrow(up[:, 1]), swapped(narrow(up[:, 0]), "seq", 4))
     up_part = jnp.concatenate([up[i] for i in range(chunks)], axis=1)
-    down = jnp.concatenate(down_parts, axis=1)
-    low_half, high_half = down[:, : block // 2], down[:, block // 2 :]
-    down = narrow(
-        wide(
-            jnp.where(seq_y == 0, low_half, high_half),
-            swapped(jnp.where(seq_y == 0, high_half, low_half), "seq", 1),
-        )
-    )
-    down = narrow(wide(down[1], swapped(down[0], "seq", 4)))
+    down_take, _ = lax.optimization_barrier((down_take, input_grad))
+    down = narrow(wide(down_keep, down_take))
     holder = [[(r & 1) == ((s >> 1) & 1) for r in range(4)] for s in range(8)]
     down = wide(
         down,
@@ -631,100 +959,12 @@
         [(s * 4 + r, s * 4 + (r ^ 1)) for s in range(8) for r in range(4) if holder[s][r]],
     )
     down_part = jnp.where(core == seq_z0, down_own, down_other.astype(jnp.float32))
-
-    normed_two_grad = wide(own_ntg, take_ntg)
-    feed_gain_grad = jnp.sum(normed_two_grad * residual * inverse_two, axis=0)
-    scaled_two = feed_scale * normed_two_grad
-    residual_grad = (
-        upstream
-        + inverse_two * scaled_two
-        - residual
-        * (inverse_two * inverse_two * inverse_two)
-        * jnp.mean(scaled_two * residual, axis=1, keepdims=True)
-    )
-    mixer_grad = (valid_mask * residual_grad).astype(jnp.bfloat16)
-
-    def by_seq(value):
-        width = value.shape[1] // 8
-        return jnp.concatenate(
-            [lax.dynamic_slice_in_dim(value, (p ^ seq ^ 7) * width, width, 1) for p in range(8)], axis=1
-        )
-
-    def by_row(value, core_at):
-        width = value.shape[1] // 4
-        return jnp.concatenate(
-            [
-                lax.dynamic_slice_in_dim(value, ((row ^ 3) ^ (2 * x + core_at)) * width, width, 1)
-                for x in range(2)
-            ],
-            axis=1,
-        )
-
-    def pair_summed(left, right):
-        give = contract_rows(left, by_row(right, 0))
-        keep = contract_rows(left, by_row(right, 1))
-        both = narrow(keep + swapped(narrow(give), "row", 1).astype(jnp.float32))
-        width = both.shape[1] // 2
-        return jnp.stack(
-            [both[:, i * width : (i + 1) * width].reshape(2, 2, 2, model_width // 8, width) for i in range(2)]
-        )
-
-    out_sum = pair_summed(by_seq(mixed_in), mixer_grad)
-    mixed_grad = contract_cols(mixer_grad, out_weight)
-    output_gate_grad = mixed_grad * conv_out
-    conv_grad = (mixed_grad * output_gate).reshape(row_count, span_length, model_width)
-    kernel_grad = [
-        jnp.sum(conv_grad * tap_zero, axis=(0, 1)),
-        jnp.sum(conv_grad * tap_one, axis=(0, 1)),
-        jnp.sum(conv_grad * tap_two, axis=(0, 1)),
-    ]
-    grad_zero = kernel[:, 0] * conv_grad
-    grad_one = keep_one * kernel[:, 1] * conv_grad
-    grad_two = keep_two * kernel[:, 2] * conv_grad
-    extended_grad = (
-        jnp.pad(grad_zero, ((0, 0), (2, 0), (0, 0)))
-        + jnp.pad(grad_one, ((0, 0), (1, 1), (0, 0)))
-        + jnp.pad(grad_two, ((0, 0), (0, 2), (0, 0)))
-    )
-    returned = passed_along(extended_grad[:, :2, :], "seq", -1)
-    product_grad = extended_grad[:, 2:, :] + jnp.pad(
-        returned, ((0, 0), (span_length - 2, 0), (0, 0))
-    )
-    flat_grad = product_grad.reshape(token_count, model_width)
-    project_grad = jnp.concatenate(
-        [flat_grad * values, output_gate_grad, flat_grad * input_gate], axis=1
-    ).astype(jnp.bfloat16)
-    in_sum = pair_summed(by_seq(normed), project_grad)
-    third = in_sum.shape[-1] // 3
-    in_part = jnp.concatenate(
-        [
-            settle(in_sum[..., i * third : (i + 1) * third], order)
-            for i, order in enumerate((("x", "y", "z0", "z1"), ("y", "x", "z0", "z1"), ("z0", "x", "y", "z1")))
-        ],
-        axis=1,
-    )
-    out_part = settle(out_sum, ("y", "z0", "x", "z1"))
-    normed_grad = contract_cols(project_grad, in_weight)
-    mixer_gain_grad = jnp.sum(normed_grad * source * inverse_one, axis=0)
-    scaled_one = mixer_scale * normed_grad
-    input_grad = (
-        residual_grad
-        + inverse_one * scaled_one
-        - source
-        * (inverse_one * inverse_one * inverse_one)
-        * jnp.mean(scaled_one * source, axis=1, keepdims=True)
-    )
-    input_grad = input_grad.astype(jnp.bfloat16).reshape(row_count, span_length, model_width)
-    small = jnp.stack([mixer_gain_grad, feed_gain_grad] + kernel_grad)
-    for axis, bit in (("row", 1), ("row", 2), ("seq", 1), ("seq", 2), ("seq", 4)):
-        small = small + swapped(small, axis, bit)
-    small = lax.dynamic_slice_in_dim(small, seq * (model_width // 8), model_width // 8, 1)
     return (
         output,
         input_grad,
         small[0],
         in_part,
-        small[2:].T,
+        small[2:5].T,
         out_part,
         small[1],
         gate_part,

time: 479 us -> 447 us (0.933)
  Pallas kernels: 127 us -> 190 us
  matrix products: 42.4 us -> 0 us
  other arithmetic: 70.8 us -> 38.7 us
  waiting for transfers between devices: 142 us -> 120 us
  local copies, waits for them, and re-layouts: 30.5 us -> 35.3 us
    pallas_call x0 -> x7, Pallas kernels: none -> 62.9 us  [the longest x3 21.8 us: pair_grads(): pl.pallas_call(kernel, grid_spec=pltpu.PrefetchScalarGridSpec(num_scalar_...]
    dot_general x8 -> x0, matrix products: 42.4 us -> none  [the longest x2 19.8 us: contract_cols(): lax.dot_general(left, right, (((1,), (1,)), ((), ())), preferred_element_...]
    ppermute x48, waiting for transfers between devices: 140 us -> 117 us  [swapped(): return lax.ppermute(value, axis, [(i, i ^ bit) for i in range(length)])]
    convert_element_type x9 -> x3, other arithmetic: 16.2 us -> 0.09 us  [the longest x1 0.08 us: fast(): scales = jnp.concatenate([mixer_gain[None], feed_gain[None], conv_kernel....]
    add x4 -> x2, other arithmetic: 15.1 us -> 0.01 us  [the longest x1 0.01 us: fast(): positions = seq * span_length + jnp.arange(span_length, dtype=jnp.int32)]
    convert_element_type x30 -> x23, other arithmetic: 15.9 us -> 22 us  [narrow(): return value.astype(jnp.bfloat16)]
    convert_element_type x0 -> x9, local copies, waits for them, and re-layouts: none -> 5.03 us  [narrow(): return value.astype(jnp.bfloat16)]
    unnamed x142 -> x158, local copies, waits for them, and re-layouts: 23.7 us -> 24.8 us
  transfers between devices with their start and end apart: 52 -> 52, of which waited for: 26 -> 23; matrix products, arithmetic and copies ran while one was open for 25% -> 9% of each run, Pallas kernels for 21% -> 31%
where the time goes in v2:
time: 447 us; the launch traced here: 442 us
  Pallas kernels  190 us (43%)
  waiting for transfers between devices  120 us (27%)
  starting transfers between devices  55.4 us (12%)
  other arithmetic  38.7 us (9%)
  local copies, waits for them, and re-layouts  35.3 us (8%)
    ppermute x48, waiting for transfers between devices, swapped(): return lax.ppermute(value, axis, [(i, i ^ bit) for i in range(length)])  117 us
    pallas_call x3, Pallas kernels, feed_chunk(): pl.pallas_call(kernel, out_shape=[jax.ShapeDtypeStruct((both, span), low)...  83.7 us
    ppermute x48, starting transfers between devices, swapped(): return lax.ppermute(value, axis, [(i, i ^ bit) for i in range(length)])  46.6 us
    pallas_call x2, Pallas kernels, feed_sum(): pl.pallas_call(kernel, out_shape=[jax.ShapeDtypeStruct((tokens, width), l...  43.6 us
    unnamed x158, local copies, waits for them, and re-layouts  24.8 us
    convert_element_type x23, other arithmetic, narrow(): return value.astype(jnp.bfloat16)  22 us
    pallas_call x3, Pallas kernels, pair_grads(): pl.pallas_call(kernel, grid_spec=pltpu.PrefetchScalarGridSpec(num_scalar_...  21.8 us
    pallas_call x1, Pallas kernels, mixer_forward(): pl.pallas_call(kernel, grid=(steps,), in_specs=[rows(8), rows(width), row...  16.4 us
  transfers between devices with their start and end apart: 52, of which 23 were waited for; matrix products, arithmetic and copies ran while one was open for 9% of the time, Pallas kernels for 31%

profile of v2, /device:TPU:0, one launch (start us, length us, event | category | flops | bytes accessed | tf_op | source)
XLA Modules:
  0.0 442.3 jit_solution(2695874778646548661)
XLA Ops:
  1.4 4.9 %collective-permute-start = (bf16[2,2,1024]{2,1,0:T(2,128)(2,1)S(1)}, bf16[2,2,1024]{2,1,0:T(2,128)(2,1)S(1)}, u32[]{:S(2)}, u32[]{:S(2)}) collective-permute-start(bf16[2,2,1024]{2,1,0:T(2,128)(2,1)S(1)} %slice.241), channel_id=1, source_target_pairs={{0,4},{4,8},{8,12},{12,16},{16,20},{20,24},{24,28},{1,5},{5,9},{9,... | collective-permute-start | bytes 24584 | tf_op jit(solution)/shard_map/ppermute | solution.py:14
  7.1 3.4 multiply_convert_fusion.own_grad_ref
  11.6 16.4 %mixer_forward.1 = (bf16[1024,1024]{1,0:T(8,128)(2,1)S(1)}, bf16[1024,1024]{1,0:T(8,128)(2,1)S(1)}, bf16[1024,1024]{1,0:T(8,128)(2,1)S(1)}, bf16[1024,1024]{1,0:...) custom-call(f32[1024,8]{1,0:T(8,128)S(1)} %copy.72.marks_ref, ...), custom_call_target="tpu_custom_call" | custom-call | flops 8589934592 | bytes 29360128 | tf_op jit(solution)/shard_map/mixer_forward/pallas_call | solution.py:367
  33.0 3.5 collective-permute-done.1.other_ref
  36.5 27.8 %feed_0.1 = (bf16[2048,768]{1,0:T(8,128)(2,1)}, bf16[2048,768]{1,0:T(8,128)(2,1)}, bf16[2048,768]{1,0:T(8,128)(2,1)}, bf16[2,2,2,128,384]{4,3,2,1,0:T(8,128)(2,1...) custom-call(s32[18]{0:T(128)} %stack.97.place_ref, ...), custom_call_target="tpu_custom_call" | custom-call | flops 19327352832 | bytes 25165824 | tf_op jit(solution)/shard_map/feed_0/pallas_call | solution.py:168
  68.9 28.1 %feed_1.1 = (bf16[2048,768]{1,0:T(8,128)(2,1)}, bf16[2048,768]{1,0:T(8,128)(2,1)}, bf16[2048,768]{1,0:T(8,128)(2,1)}, bf16[2,2,2,128,384]{4,3,2,1,0:T(8,128)(2,1...) custom-call(s32[18]{0:T(128)} %stack.97.place_ref, ...), custom_call_target="tpu_custom_call" | custom-call | flops 19327352832 | bytes 25165824 | tf_op jit(solution)/shard_map/feed_1/pallas_call | solution.py:168
  104.7 27.9 %feed_2.1 = (bf16[2048,768]{1,0:T(8,128)(2,1)}, bf16[2048,768]{1,0:T(8,128)(2,1)}, bf16[2048,768]{1,0:T(8,128)(2,1)}, bf16[2,2,2,128,384]{4,3,2,1,0:T(8,128)(2,1...) custom-call(s32[18]{0:T(128)} %stack.97.place_ref, ...), custom_call_target="tpu_custom_call" | custom-call | flops 19327352832 | bytes 25165824 | tf_op jit(solution)/shard_map/feed_2/pallas_call | solution.py:168
  141.0 26.6 %normed_two_grad.1 = (bf16[1024,1024]{1,0:T(8,128)(2,1)S(1)}, bf16[1024,1024]{1,0:T(8,128)(2,1)S(1)}) custom-call(s32[18]{0:T(128)S(1)} %copy-done.15, bf16[2048,768]{1,0:T(8,128)(2,1)} %get-tuple-element.138.refs_0_, bf16[2048,768]{1,0:T(8,128)(2,1)} %get-tuple-element.139.refs_1_, bf16[2048,768]{1,0:T(8,128)(2,1)} %get-tuple-element.140.refs_2_, ...), custom_call_target="tpu_custom_call" | custom-call | flops 19327352832 | bytes 25165824 | tf_op jit(solution)/shard_map/normed_two_grad/pallas_call | solution.py:280
  175.2 4.5 %collective-permute-done.13 = bf16[2,2,128,384]{3,2,1,0:T(8,128)(2,1)S(1)} collective-permute-done((bf16[2,2,128,384]{3,2,1,0:T(8,128)(2,1)S(1)}, bf16[2,2,128,384]{3,2,1,0:T(8,128)(2,1)S(1)}, u32[]{:S(2)}, u32[]{:S(2)}) %collective-permute-start.13) | collective-permute-done | bytes 393248 | tf_op jit(solution)/shard_map/ppermute | solution.py:31
  183.1 17.0 %feed_out.1 = (bf16[1024,1024]{1,0:T(8,128)(2,1)S(1)}, bf16[1024,1024]{1,0:T(8,128)(2,1)}) custom-call(s32[18]{0:T(128)S(1)} %copy-done.15, bf16[2048,768]{1,0:T(8,128)(2,1)} %get-tuple-element.108.refs_0_, bf16[2048,768]{1,0:T(8,128)(2,1)} %get-tuple-element.110.refs_1_, bf16[2048,768]{1,0:T(8,128)(2,1)} %get-tuple-element.130.refs_2_, ...), custom_call_target="tpu_custom_call" | custom-call | flops 9663676416 | bytes 25165824 | tf_op jit(solution)/shard_map/feed_out/pallas_call | solution.py:280
  204.9 12.7 %mixer_middle.1 = (f32[1024,1024]{1,0:T(8,128)}, bf16[1024,1024]{1,0:T(8,128)(2,1)S(1)}, bf16[1024,1024]{1,0:T(8,128)(2,1)S(1)}, f32[1024,1024]{1,0:T(8,128)}, f32[8,1024]{1,0:T(8,128)S(1)}) custom-call(f32[1024,8]{1,0:T(8,128)S(1)} %copy.73.marks_ref, bf16[1024,1024]{1,0:T(8,128)(2,1)S(1)} %copy-done.8, bf16[1024,1024]{1,0:T(8,128)(2,1)S(1)} %copy-done.10, ...), custom_call_target="tpu_custom_call" | custom-call | flops 2147483648 | bytes 33554432 | tf_op jit(solution)/shard_map/mixer_middle/pallas_call | solution.py:433
  219.0 2.5 collective-permute-done.18
  239.6 2.8 project_grads.1.right_ref.grad_ref
  242.4 8.8 %in_grads_give.1 = bf16[2,8,128,768]{3,2,1,0:T(8,128)(2,1)} custom-call(s32[18]{0:T(128)S(1)} %copy-done.15, bf16[1024,1024]{1,0:T(8,128)(2,1)S(1)} %copy-done.21, bf16[1024,3072]{1,0:T(8,128)(2,1)S(1)} %project_grads.1.right_ref.grad_ref), custom_call_target="tpu_custom_call" | custom-call | flops 3221225472 | bytes 8388608 | tf_op jit(solution)/shard_map/in_grads_give/pallas_call | solution.py:515
  251.2 7.7 %in_grads_keep.1 = bf16[2,8,128,768]{3,2,1,0:T(8,128)(2,1)S(1)} custom-call(s32[18]{0:T(128)S(1)} %copy-done.15, bf16[1024,1024]{1,0:T(8,128)(2,1)S(1)} %copy-done.21, bf16[1024,3072]{1,0:T(8,128)(2,1)S(1)} %project_grads.1.right_ref.grad_ref), custom_call_target="tpu_custom_call" | custom-call | flops 3221225472 | bytes 8388608 | tf_op jit(solution)/shard_map/in_grads_keep/pallas_call | solution.py:515
  258.9 5.3 %out_grads.1 = (bf16[2,8,128,256]{3,2,1,0:T(8,128)(2,1)}, bf16[2,8,128,256]{3,2,1,0:T(8,128)(2,1)S(1)}) custom-call(s32[18]{0:T(128)S(1)} %copy-done.15, bf16[1024,1024]{1,0:T(8,128)(2,1)S(1)} %copy-done.22, bf16[1024,1024]{1,0:T(8,128)(2,1)S(1)} %copy-done.19), custom_call_target="tpu_custom_call" | custom-call | flops 2147483648 | bytes 8388608 | tf_op jit(solution)/shard_map/out_grads/pallas_call | solution.py:515
  265.3 3.0 broadcast_select_fusion
  274.1 34.1 %collective-permute-done.41 = bf16[2,2,2,128,256]{4,3,1,0,2:T(8,128)(2,1)} collective-permute-done((bf16[2,2,2,128,256]{4,3,1,0,2:T(8,128)(2,1)}, bf16[2,2,2,128,256]{4,3,1,0,2:T(8,128)(2,1)}, u32[]{:S(2)}, u32[]{:S(2)}) %collective-permute-start.41) | collective-permute-done | bytes 524320 | tf_op jit(solution)/shard_map/ppermute | solution.py:31
  312.7 4.8 %collective-permute-done.42 = bf16[2,2,128,256]{3,2,1,0:T(8,128)(2,1)S(1)} collective-permute-done((bf16[2,2,128,256]{3,2,1,0:T(8,128)(2,1)S(1)}, bf16[2,2,128,256]{3,2,1,0:T(8,128)(2,1)S(1)}, u32[]{:S(2)}, u32[]{:S(2)}) %collective-permute-start.42) | collective-permute-done | bytes 262176 | tf_op jit(solution)/shard_map/ppermute | solution.py:31
  318.3 2.6 collective-permute-start.49
  324.1 2.6 collective-permute-start.44
  326.8 3.8 add_convert_fusion.1
  330.6 18.0 %collective-permute-done.44 = bf16[128,256]{1,0:T(8,128)(2,1)S(1)} collective-permute-done((bf16[128,256]{1,0:T(8,128)(2,1)S(1)}, bf16[128,256]{1,0:T(8,128)(2,1)S(1)}, u32[]{:S(2)}, u32[]{:S(2)}) %collective-permute-start.44) | collective-permute-done | bytes 65568 | tf_op jit(solution)/shard_map/ppermute | solution.py:31
  349.3 3.0 add_convert_fusion
  356.4 9.3 %mixer_backward.1 = (bf16[1024,1024]{1,0:T(8,128)(2,1)}, f32[8,1024]{1,0:T(8,128)S(1)}) custom-call(bf16[1024,3072]{1,0:T(8,128)(2,1)S(1)} %bitcast.284, bf16[1024,3072]{1,0:T(8,128)(2,1)S(1)} %bitcast.290, bf16[1024,1024]{1,0:T(8,128)(2,1)S(1)} %bitcast.288, f32[1024,1024]{1,0:T(8,128)S(1)} %copy-done.17, f32[8,1024]{1,0:T(8,128)S(1)} %get-tuple-element.180.sums_ref, ...), custom_call_target="tpu_custom_call" | custom-call | flops 6442450944 | bytes 20971520 | tf_op jit(solution)/shard_map/mixer_backward/pallas_call | solution.py:557
  373.3 7.7 %collective-permute-done.25 = f32[8,1024]{1,0:T(8,128)S(1)} collective-permute-done((f32[8,1024]{1,0:T(8,128)S(1)}, f32[8,1024]{1,0:T(8,128)S(1)}, u32[]{:S(2)}, u32[]{:S(2)}) %collective-permute-start.25) | collective-permute-done | bytes 32800 | tf_op jit(solution)/shard_map/ppermute | solution.py:31
  381.1 3.8 collective-permute-done.26
  387.9 11.8 %collective-permute-done.27 = f32[8,1024]{1,0:T(8,128)S(1)} collective-permute-done((f32[8,1024]{1,0:T(8,128)S(1)}, f32[8,1024]{1,0:T(8,128)S(1)}, u32[]{:S(2)}, u32[]{:S(2)}) %collective-permute-start.27) | collective-permute-done | bytes 32800 | tf_op jit(solution)/shard_map/ppermute | solution.py:31
  400.8 8.4 %collective-permute-done.48 = bf16[3,128,384]{2,1,0:T(8,128)(2,1)S(1)} collective-permute-done((bf16[3,128,384]{2,1,0:T(8,128)(2,1)S(1)}, bf16[3,128,384]{2,1,0:T(8,128)(2,1)S(1)}, u32[]{:S(2)}, u32[]{:S(2)}) %collective-permute-start.48) | collective-permute-done | bytes 294944 | tf_op jit(solution)/shard_map/ppermute | solution.py:31
  410.6 3.5 collective-permute-done.47
  422.5 3.0 collective-permute-done.37
  436.5 2.4 collective-permute-done.39
  (358 shorter events, 118.1 us)
Async XLA Ops:
  10.5 22.5 %collective-permute-start.2 = (bf16[1024,1024]{1,0:T(8,128)(2,1)}, bf16[1024,1024]{1,0:T(8,128)(2,1)}, u32[]{:S(2)}, u32[]{:S(2)}) collective-permute-start(bf16[1024,1024]{1,0:T(8,128)(2,1)} %multiply_convert_fusion.own_grad_ref), channel_id=1, source_target_pairs={{0,1},{1,0},{2,3},{3,2},{4,5},{5,4},{6,7},{7,6},{8,9},{9,8},{10,11... | collective-permute-start | bytes 6291464 | tf_op jit(solution)/shard_map/ppermute | solution.py:31
  64.3 33.8 %collective-permute-start.3 = (bf16[2,2,2,128,384]{4,3,2,1,0:T(8,128)(2,1)}, bf16[2,2,2,128,384]{4,3,2,1,0:T(8,128)(2,1)S(1)}, u32[]{:S(2)}, u32[]{:S(2)}) collective-permute-start(bf16[2,2,2,128,384]{4,3,2,1,0:T(8,128)(2,1)} %get-tuple-element.105), channel_id=1, source_target_pairs={{0,8},{4,12},{8,0},{12,4},{16,24},{20,28},{24,16},{28,20},{1,9},{5... | collective-permute-start | bytes 2359304 | tf_op jit(solution)/shard_map/ppermute | solution.py:31
  65.9 32.7 %collective-permute-start.4 = (bf16[2,4,128,384]{3,2,1,0:T(8,128)(2,1)}, bf16[2,4,128,384]{3,2,1,0:T(8,128)(2,1)S(1)}, u32[]{:S(2)}, u32[]{:S(2)}) collective-permute-start(bf16[2,4,128,384]{3,2,1,0:T(8,128)(2,1)} %get-tuple-element.106), channel_id=1, source_target_pairs={{0,4},{4,0},{8,12},{12,8},{16,20},{20,16},{24,28},{28,24},{1,5},{5... | collective-permute-start | bytes 2359304 | tf_op jit(solution)/shard_map/ppermute | solution.py:31
  67.4 31.1 %collective-permute-start.5 = (bf16[2,384,512]{2,1,0:T(8,128)(2,1)}, bf16[2,384,512]{2,1,0:T(8,128)(2,1)}, u32[]{:S(2)}, u32[]{:S(2)}) collective-permute-start(bf16[2,384,512]{2,1,0:T(8,128)(2,1)} %get-tuple-element.107), channel_id=1, source_target_pairs={{0,2},{1,3},{2,0},{3,1},{4,6},{5,7},{6,4},{7,5},{8,10},{9,11},{10,... | collective-permute-start | bytes 2359304 | tf_op jit(solution)/shard_map/ppermute | solution.py:31
  97.0 35.5 %collective-permute-start.9 = (bf16[2,2,2,128,384]{4,3,2,1,0:T(8,128)(2,1)}, bf16[2,2,2,128,384]{4,3,2,1,0:T(8,128)(2,1)S(1)}, u32[]{:S(2)}, u32[]{:S(2)}) collective-permute-start(bf16[2,2,2,128,384]{4,3,2,1,0:T(8,128)(2,1)} %get-tuple-element.127), channel_id=1, source_target_pairs={{0,8},{4,12},{8,0},{12,4},{16,24},{20,28},{24,16},{28,20},{1,9},{5... | collective-permute-start | bytes 2359304 | tf_op jit(solution)/shard_map/ppermute | solution.py:31
  97.5 35.0 %collective-permute-start.10 = (bf16[2,4,128,384]{3,2,1,0:T(8,128)(2,1)}, bf16[2,4,128,384]{3,2,1,0:T(8,128)(2,1)S(1)}, u32[]{:S(2)}, u32[]{:S(2)}) collective-permute-start(bf16[2,4,128,384]{3,2,1,0:T(8,128)(2,1)} %get-tuple-element.128), channel_id=1, source_target_pairs={{0,4},{4,0},{8,12},{12,8},{16,20},{20,16},{24,28},{28,24},{1,5},{5... | collective-permute-start | bytes 2359304 | tf_op jit(solution)/shard_map/ppermute | solution.py:31
  98.0 34.5 %collective-permute-start.11 = (bf16[2,384,512]{2,1,0:T(8,128)(2,1)}, bf16[2,384,512]{2,1,0:T(8,128)(2,1)S(1)}, u32[]{:S(2)}, u32[]{:S(2)}) collective-permute-start(bf16[2,384,512]{2,1,0:T(8,128)(2,1)} %get-tuple-element.129), channel_id=1, source_target_pairs={{0,2},{1,3},{2,0},{3,1},{4,6},{5,7},{6,4},{7,5},{8,10},{9,11},{10,... | collective-permute-start | bytes 2359304 | tf_op jit(solution)/shard_map/ppermute | solution.py:31
  136.4 31.9 %collective-permute-start.6 = (bf16[2,2,2,128,384]{4,3,2,1,0:T(8,128)(2,1)S(1)}, bf16[2,2,2,128,384]{4,3,2,1,0:T(8,128)(2,1)S(1)}, u32[]{:S(2)}, u32[]{:S(2)}) collective-permute-start(bf16[2,2,2,128,384]{4,3,2,1,0:T(8,128)(2,1)S(1)} %copy-done.67), channel_id=1, source_target_pairs={{0,8},{4,12},{8,0},{12,4},{16,24},{20,28},{24,16},{28,20},{1,9},{5... | collective-permute-start | bytes 2359304 | tf_op jit(solution)/shard_map/ppermute | solution.py:31
  138.0 31.8 %collective-permute-start.7 = (bf16[2,4,128,384]{3,2,1,0:T(8,128)(2,1)S(1)}, bf16[2,4,128,384]{3,2,1,0:T(8,128)(2,1)S(1)}, u32[]{:S(2)}, u32[]{:S(2)}) collective-permute-start(bf16[2,4,128,384]{3,2,1,0:T(8,128)(2,1)S(1)} %copy-done.66), channel_id=1, source_target_pairs={{0,4},{4,0},{8,12},{12,8},{16,20},{20,16},{24,28},{28,24},{1,5},{5... | collective-permute-start | bytes 2359304 | tf_op jit(solution)/shard_map/ppermute | solution.py:31
  139.5 30.8 %collective-permute-start.8 = (bf16[2,384,512]{2,1,0:T(8,128)(2,1)S(1)}, bf16[2,384,512]{2,1,0:T(8,128)(2,1)S(1)}, u32[]{:S(2)}, u32[]{:S(2)}) collective-permute-start(bf16[2,384,512]{2,1,0:T(8,128)(2,1)S(1)} %copy-done.65), channel_id=1, source_target_pairs={{0,2},{1,3},{2,0},{3,1},{4,6},{5,7},{6,4},{7,5},{8,10},{9,11},{10,... | collective-permute-start | bytes 2359304 | tf_op jit(solution)/shard_map/ppermute | solution.py:31
  167.6 12.7 %collective-permute-start.19 = (bf16[1024,1024]{1,0:T(8,128)(2,1)S(1)}, bf16[1024,1024]{1,0:T(8,128)(2,1)S(1)}, u32[]{:S(2)}, u32[]{:S(2)}) collective-permute-start(bf16[1024,1024]{1,0:T(8,128)(2,1)S(1)} %get-tuple-element.155), channel_id=1, source_target_pairs={{0,1},{1,0},{2,3},{3,2},{4,5},{5,4},{6,7},{7,6},{8,9},{9,8},{10,11... | collective-permute-start | bytes 6291464 | tf_op jit(solution)/shard_map/ppermute | solution.py:31
  167.7 12.1 %collective-permute-start.13 = (bf16[2,2,128,384]{3,2,1,0:T(8,128)(2,1)S(1)}, bf16[2,2,128,384]{3,2,1,0:T(8,128)(2,1)S(1)}, u32[]{:S(2)}, u32[]{:S(2)}) collective-permute-start(bf16[2,2,128,384]{3,2,1,0:T(8,128)(2,1)S(1)} %slice_bitcast_fusion.17), channel_id=1, source_target_pairs={{0,2},{1,3},{2,0},{3,1},{4,6},{5,7},{6,4},{7,5},{8,10},{9,11},{10,... | collective-permute-start | bytes 1179656 | tf_op jit(solution)/shard_map/ppermute | solution.py:31
  168.4 50.6 %collective-permute-start.16 = (bf16[4,128,384]{2,1,0:T(8,128)(2,1)}, bf16[4,128,384]{2,1,0:T(8,128)(2,1)}, u32[]{:S(2)}, u32[]{:S(2)}) collective-permute-start(bf16[4,128,384]{2,1,0:T(8,128)(2,1)} %slice_bitcast_fusion.15), channel_id=1, source_target_pairs={{0,2},{1,3},{2,0},{3,1},{4,6},{5,7},{6,4},{7,5},{8,10},{9,11},{10,... | collective-permute-start | bytes 1179656 | tf_op jit(solution)/shard_map/ppermute | solution.py:31
  169.8 49.1 %collective-permute-start.14 = (bf16[2,2,128,384]{3,2,1,0:T(8,128)(2,1)}, bf16[2,2,128,384]{3,2,1,0:T(8,128)(2,1)}, u32[]{:S(2)}, u32[]{:S(2)}) collective-permute-start(bf16[2,2,128,384]{3,2,1,0:T(8,128)(2,1)} %slice_bitcast_fusion.13), channel_id=1, source_target_pairs={{0,2},{1,3},{2,0},{3,1},{4,6},{5,7},{6,4},{7,5},{8,10},{9,11},{10,... | collective-permute-start | bytes 1179656 | tf_op jit(solution)/shard_map/ppermute | solution.py:31
  170.4 48.6 %collective-permute-start.17 = (bf16[4,128,384]{2,1,0:T(8,128)(2,1)}, bf16[4,128,384]{2,1,0:T(8,128)(2,1)}, u32[]{:S(2)}, u32[]{:S(2)}) collective-permute-start(bf16[4,128,384]{2,1,0:T(8,128)(2,1)} %slice_bitcast_fusion.11), channel_id=1, source_target_pairs={{0,2},{1,3},{2,0},{3,1},{4,6},{5,7},{6,4},{7,5},{8,10},{9,11},{10,... | collective-permute-start | bytes 1179656 | tf_op jit(solution)/shard_map/ppermute | solution.py:31
  179.8 39.2 %collective-permute-start.15 = (bf16[2,2,128,384]{3,2,1,0:T(8,128)(2,1)}, bf16[2,2,128,384]{3,2,1,0:T(8,128)(2,1)}, u32[]{:S(2)}, u32[]{:S(2)}) collective-permute-start(bf16[2,2,128,384]{3,2,1,0:T(8,128)(2,1)} %slice_bitcast_fusion.9), channel_id=1, source_target_pairs={{0,2},{1,3},{2,0},{3,1},{4,6},{5,7},{6,4},{7,5},{8,10},{9,11},{10,... | collective-permute-start | bytes 1179656 | tf_op jit(solution)/shard_map/ppermute | solution.py:31
  181.7 39.8 %collective-permute-start.18 = (bf16[4,128,384]{2,1,0:T(8,128)(2,1)}, bf16[4,128,384]{2,1,0:T(8,128)(2,1)}, u32[]{:S(2)}, u32[]{:S(2)}) collective-permute-start(bf16[4,128,384]{2,1,0:T(8,128)(2,1)} %slice_bitcast_fusion.7), channel_id=1, source_target_pairs={{0,2},{1,3},{2,0},{3,1},{4,6},{5,7},{6,4},{7,5},{8,10},{9,11},{10,... | collective-permute-start | bytes 1179656 | tf_op jit(solution)/shard_map/ppermute | solution.py:31
  268.3 42.2 %collective-permute-start.22 = (bf16[2,576,512]{2,1,0:T(8,128)(2,1)}, bf16[2,576,512]{2,1,0:T(8,128)(2,1)}, u32[]{:S(2)}, u32[]{:S(2)}) collective-permute-start(bf16[2,576,512]{2,1,0:T(8,128)(2,1)} %broadcast_select_fusion), channel_id=1, source_target_pairs={{0,4},{4,0},{8,12},{12,8},{16,20},{20,16},{24,28},{28,24},{1,5},{5... | collective-permute-start | bytes 3538952 | tf_op jit(solution)/shard_map/ppermute | solution.py:31
  273.0 35.2 %collective-permute-start.41 = (bf16[2,2,2,128,256]{4,3,1,0,2:T(8,128)(2,1)}, bf16[2,2,2,128,256]{4,3,1,0,2:T(8,128)(2,1)}, u32[]{:S(2)}, u32[]{:S(2)}) collective-permute-start(bf16[2,2,2,128,256]{4,3,1,0,2:T(8,128)(2,1)} %bitcast.279), channel_id=1, source_target_pairs={{0,4},{4,0},{8,12},{12,8},{16,20},{20,16},{24,28},{28,24},{1,5},{5... | collective-permute-start | bytes 1572872 | tf_op jit(solution)/shard_map/ppermute | solution.py:31
  273.6 75.7 %collective-permute-start.21 = (bf16[2,8,128,768]{3,2,1,0:T(8,128)(2,1)}, bf16[2,8,128,768]{3,2,1,0:T(8,128)(2,1)}, u32[]{:S(2)}, u32[]{:S(2)}) collective-permute-start(bf16[2,8,128,768]{3,2,1,0:T(8,128)(2,1)} %in_grads_give.1), channel_id=1, source_target_pairs={{0,1},{1,0},{2,3},{3,2},{4,5},{5,4},{6,7},{7,6},{8,9},{9,8},{10,11... | collective-permute-start | bytes 9437192 | tf_op jit(solution)/shard_map/ppermute | solution.py:31
  273.6 50.5 %collective-permute-start.12 = (bf16[1024,1024]{1,0:T(8,128)(2,1)}, bf16[1024,1024]{1,0:T(8,128)(2,1)}, u32[]{:S(2)}, u32[]{:S(2)}) collective-permute-start(bf16[1024,1024]{1,0:T(8,128)(2,1)} %get-tuple-element.153), channel_id=1, source_target_pairs={{0,1},{1,0},{2,3},{3,2},{4,5},{5,4},{6,7},{7,6},{8,9},{9,8},{10,11... | collective-permute-start | bytes 6291464 | tf_op jit(solution)/shard_map/ppermute | solution.py:31
  318.3 47.4 %collective-permute-start.49 = (bf16[576,512]{1,0:T(8,128)(2,1)S(1)}, bf16[576,512]{1,0:T(8,128)(2,1)S(1)}, u32[]{:S(2)}, u32[]{:S(2)}) collective-permute-start(bf16[576,512]{1,0:T(8,128)(2,1)S(1)} %slice_bitcast_fusion.3), channel_id=1, source_target_pairs={{0,16},{4,20},{8,24},{12,28},{16,0},{20,4},{24,8},{28,12},{1,17},{... | collective-permute-start | bytes 1769480 | tf_op jit(solution)/shard_map/ppermute | solution.py:31
  320.9 45.0 %collective-permute-start.46 = (bf16[3,2,128,384]{3,2,0,1:T(8,128)(2,1)S(1)}, bf16[3,2,128,384]{3,2,0,1:T(8,128)(2,1)}, u32[]{:S(2)}, u32[]{:S(2)}) collective-permute-start(bf16[3,2,128,384]{3,2,0,1:T(8,128)(2,1)S(1)} %copy-done.57), channel_id=1, source_target_pairs={{0,8},{4,12},{8,0},{12,4},{16,24},{20,28},{24,16},{28,20},{1,9},{5... | collective-permute-start | bytes 1769480 | tf_op jit(solution)/shard_map/ppermute | solution.py:31
  322.6 44.5 %collective-permute-start.45 = (bf16[3,2,128,384]{3,2,1,0:T(8,128)(2,1)S(1)}, bf16[3,2,128,384]{3,2,1,0:T(8,128)(2,1)S(1)}, u32[]{:S(2)}, u32[]{:S(2)}) collective-permute-start(bf16[3,2,128,384]{3,2,1,0:T(8,128)(2,1)S(1)} %copy-done.58), channel_id=1, source_target_pairs={{0,4},{4,0},{8,12},{12,8},{16,20},{20,16},{24,28},{28,24},{1,5},{5... | collective-permute-start | bytes 1769480 | tf_op jit(solution)/shard_map/ppermute | solution.py:31
  324.1 24.5 %collective-permute-start.44 = (bf16[128,256]{1,0:T(8,128)(2,1)S(1)}, bf16[128,256]{1,0:T(8,128)(2,1)S(1)}, u32[]{:S(2)}, u32[]{:S(2)}) collective-permute-start(bf16[128,256]{1,0:T(8,128)(2,1)S(1)} %slice_bitcast_fusion.44), channel_id=1, source_target_pairs={{0,16},{4,20},{8,24},{12,28},{16,0},{20,4},{24,8},{28,12},{1,17},{... | collective-permute-start | bytes 196616 | tf_op jit(solution)/shard_map/ppermute | solution.py:31
  352.7 63.3 %collective-permute-start.30 = (bf16[2,2,2,128,256]{4,3,1,2,0:T(8,128)(2,1)S(1)}, bf16[2,2,2,128,256]{4,3,1,2,0:T(8,128)(2,1)S(1)}, u32[]{:S(2)}, u32[]{:S(2)}) collective-permute-start(bf16[2,2,2,128,256]{4,3,1,2,0:T(8,128)(2,1)S(1)} %bitcast.304), channel_id=1, source_target_pairs={{0,8},{4,12},{8,0},{12,4},{16,24},{20,28},{24,16},{28,20},{1,9},{5... | collective-permute-start | bytes 1572872 | tf_op jit(solution)/shard_map/ppermute | solution.py:31
  352.8 63.1 %collective-permute-start.28 = (bf16[2,2,2,128,256]{4,3,0,1,2:T(8,128)(2,1)S(1)}, bf16[2,2,2,128,256]{4,3,0,1,2:T(8,128)(2,1)S(1)}, u32[]{:S(2)}, u32[]{:S(2)}) collective-permute-start(bf16[2,2,2,128,256]{4,3,0,1,2:T(8,128)(2,1)S(1)} %bitcast.305), channel_id=1, source_target_pairs={{0,2},{1,3},{2,0},{3,1},{4,6},{5,7},{6,4},{7,5},{8,10},{9,11},{10,... | collective-permute-start | bytes 1572872 | tf_op jit(solution)/shard_map/ppermute | solution.py:31
  365.9 50.1 %collective-permute-start.29 = (bf16[2,2,2,128,256]{4,3,1,2,0:T(8,128)(2,1)S(1)}, bf16[2,2,2,128,256]{4,3,1,2,0:T(8,128)(2,1)S(1)}, u32[]{:S(2)}, u32[]{:S(2)}) collective-permute-start(bf16[2,2,2,128,256]{4,3,1,2,0:T(8,128)(2,1)S(1)} %bitcast.303), channel_id=1, source_target_pairs={{0,4},{4,0},{8,12},{12,8},{16,20},{20,16},{24,28},{28,24},{1,5},{5... | collective-permute-start | bytes 1572872 | tf_op jit(solution)/shard_map/ppermute | solution.py:31
  384.9 14.8 %collective-permute-start.27 = (f32[8,1024]{1,0:T(8,128)S(1)}, f32[8,1024]{1,0:T(8,128)S(1)}, u32[]{:S(2)}, u32[]{:S(2)}) collective-permute-start(f32[8,1024]{1,0:T(8,128)S(1)} %add.245), channel_id=1, source_target_pairs={{0,16},{4,20},{8,24},{12,28},{16,0},{20,4},{24,8},{28,12},{1,17},{... | collective-permute-start | bytes 98312 | tf_op jit(solution)/shard_map/ppermute | solution.py:31
  386.3 22.9 %collective-permute-start.48 = (bf16[3,128,384]{2,1,0:T(8,128)(2,1)S(1)}, bf16[3,128,384]{2,1,0:T(8,128)(2,1)S(1)}, u32[]{:S(2)}, u32[]{:S(2)}) collective-permute-start(bf16[3,128,384]{2,1,0:T(8,128)(2,1)S(1)} %slice_bitcast_fusion.18), channel_id=1, source_target_pairs={{0,16},{4,20},{8,24},{12,28},{16,0},{20,4},{24,8},{28,12},{1,17},{... | collective-permute-start | bytes 884744 | tf_op jit(solution)/shard_map/ppermute | solution.py:31
  399.7 14.4 %collective-permute-start.47 = (bf16[3,128,384]{2,1,0:T(8,128)(2,1)S(1)}, bf16[3,128,384]{2,1,0:T(8,128)(2,1)S(1)}, u32[]{:S(2)}, u32[]{:S(2)}) collective-permute-start(bf16[3,128,384]{2,1,0:T(8,128)(2,1)S(1)} %slice_bitcast_fusion.20), channel_id=1, source_target_pairs={{0,16},{4,20},{8,24},{12,28},{16,0},{20,4},{24,8},{28,12},{1,17},{... | collective-permute-start | bytes 884744 | tf_op jit(solution)/shard_map/ppermute | solution.py:31
  409.2 11.8 %collective-permute-start.50 = (bf16[576,512]{1,0:T(8,128)(2,1)S(1)}, bf16[576,512]{1,0:T(8,128)(2,1)S(1)}, u32[]{:S(2)}, u32[]{:S(2)}) collective-permute-start(bf16[576,512]{1,0:T(8,128)(2,1)S(1)} %fusion), channel_id=1, source_target_pairs={{1,9},{3,11},{5,13},{7,15},{8,0},{10,2},{12,4},{14,6},{17,25},{19,... | collective-permute-start | bytes 1769480 | tf_op jit(solution)/shard_map/ppermute | solution.py:947
  (92 other events, 652.8 us)

commit v3 on v2

--- a/solution.py
+++ b/solution.py
@@ -133,17 +133,18 @@
                         buf[col // part, spot, :, pl.ds(col % part, 128)] = rows_i[:, c * 128 : (c + 1) * 128]
             if buf is gw:
                 pairs = [
-                    (gw.at[j, pl.ds(4 * h + 2 * z, 2)], out.at[j, h], grad_sem.at[8 + 4 * z + 2 * j + h])
+                    (gw.at[j, pl.ds(4 * h + 2 * z, 2)], out.at[:, j, h], grad_sem.at[8 + 4 * z + 2 * j + h])
                     for z, out in enumerate((gate_send, gate_keep))
                     for j in range(2)
                     for h in range(2)
                 ]
             else:
                 pairs = [
-                    (uw.at[j, 2 * h + y], out.at[j, h], grad_sem.at[16 + 8 * y + 4 * j + h])
+                    (uw.at[j, 4 * h + 2 * z + y], out.at[z, j, h], grad_sem.at[16 + 8 * y + 4 * z + 2 * j + h])
                     for y, out in enumerate((up_send, up_keep))
+                    for z in range(2)
                     for j in range(2)
-                    for h in range(4)
+                    for h in range(2)
                 ]
             for src, out, sem in pairs:
                 copy = pltpu.make_async_copy(src, out, sem)
@@ -168,8 +169,7 @@
     return pl.pallas_call(
         kernel,
         out_shape=[jax.ShapeDtypeStruct((both, span), low)] * 3
-        + [jax.ShapeDtypeStruct((2, 2, 2, eighth, part), low)] * 2
-        + [jax.ShapeDtypeStruct((2, 4, eighth, part), low)] * 2
+        + [jax.ShapeDtypeStruct((2, 2, 2, eighth, part), low)] * 4
         + [jax.ShapeDtypeStruct((2, part, width // 2), low)] * 2,
         grid_spec=pltpu.PrefetchScalarGridSpec(
             num_scalar_prefetch=1,
@@ -753,20 +753,65 @@
     )
 
 
-LINKS = {"x": ("row", 2), "y": ("seq", 1), "z0": ("seq", 2), "z1": ("seq", 4)}
-
-
-def settle(value, order):
-    names = [name for name in ("x", "z1", "z0", "y") if name in order[len(order) - value.ndim + 2 :]]
-    for name in order[len(order) - len(names) :]:
-        at = names.index(name)
-        names.remove(name)
-        give = lax.index_in_dim(value, 0, at, keepdims=False)
-        keep = lax.index_in_dim(value, 1, at, keepdims=False)
-        value = wide(keep, swapped(narrow(give), *LINKS[name]))
-        if names:
-            value = narrow(value)
-    return value
+def joined(keeps, takes, name):
+    count = len(keeps)
+    shape = (count,) + keeps[0].shape[1:]
+
+    def kernel(*refs):
+        for n in range(count):
+            for side in range(2):
+                refs[2 * count + side][n] = narrow(wide(refs[n][side], refs[count + n][side]))
+
+    return pl.pallas_call(
+        kernel,
+        out_shape=[jax.ShapeDtypeStruct(shape, LOW)] * 2,
+        compiler_params=pltpu.CompilerParams(vmem_limit_bytes=32 << 20),
+        name=name,
+    )(*keeps, *takes)
+
+
+def side_by_side(keeps, takes):
+    count = len(keeps)
+    widths = [keep.shape[-1] for keep in keeps]
+    shape = (2, keeps[0].shape[-2], sum(widths))
+
+    def kernel(*refs):
+        for n in range(count):
+            at = pl.ds(sum(widths[:n]), widths[n])
+            for side in range(2):
+                for h in range(2):
+                    refs[2 * count + side][h, :, at] = narrow(
+                        wide(refs[n][2 * h + side], refs[count + n][2 * h + side])
+                    )
+
+    return pl.pallas_call(
+        kernel,
+        out_shape=[jax.ShapeDtypeStruct(shape, LOW)] * 2,
+        compiler_params=pltpu.CompilerParams(vmem_limit_bytes=32 << 20),
+        name="side_by_side",
+    )(*keeps, *takes)
+
+
+def last_sums(keeps, takes):
+    counts = [keep.shape[0] for keep in keeps]
+    height, part = keeps[0].shape[1:]
+    shape = (height, sum(counts) // 2 * part)
+
+    def kernel(*refs):
+        n = 0
+        for i, count in enumerate(counts):
+            for k in range(count):
+                refs[2 * len(counts) + n % 2][:, pl.ds(n // 2 * part, part)] = wide(
+                    refs[i][k], refs[len(counts) + i][k]
+                )
+                n += 1
+
+    return pl.pallas_call(
+        kernel,
+        out_shape=[jax.ShapeDtypeStruct(shape, FULL)] * 2,
+        compiler_params=pltpu.CompilerParams(vmem_limit_bytes=32 << 20),
+        name="last_sums",
+    )(*keeps, *takes)
 
 
 def fast(
@@ -835,121 +880,169 @@
         gs, us, ds = made[3], made[5], made[7]
         return swapped(gs, "seq", 2), swapped(us, "seq", 1), swapped(ds, "row", 2)
 
-    def first_sums(made, taken, behind):
-        (gk, uk, dk, taken), _ = lax.optimization_barrier(((made[4], made[6], made[8], taken), behind))
-        gate, up, down = (wide(keep, take) for keep, take in zip((gk, uk, dk), taken))
-        return narrow(gate[0]), narrow(gate[1]), narrow(up[0]), narrow(up[1]), narrow(down)
+    def together(*values):
+        return lax.optimization_barrier(values)
 
     def follow(value, *ahead):
         return lax.optimization_barrier((value,) + ahead)[0]
 
+    def first_sums(made, taken):
+        pairs = ((made[4], taken[0]), (made[6], taken[1]))
+        halves = [narrow(wide(keep[i], take[i])) for keep, take in pairs for i in range(2)]
+        return halves + [narrow(wide(made[8], taken[2]))]
+
+    def second(sums):
+        return swapped(sums[0], "seq", 1), swapped(sums[2], "seq", 2)
+
+    def split(keep, take, at):
+        return [
+            narrow(wide(lax.index_in_dim(keep, i, at, False), lax.index_in_dim(take, i, at, False))) for i in range(2)
+        ]
+
     made0 = chunk_grads(place, 0)
     taken0 = sent(made0)
-    made1 = chunk_grads(follow(place, made0[0]), 1)
+    made1, taken0 = together(chunk_grads(follow(place, made0[0]), 1), taken0)
     taken1 = sent(made1)
-    sums0 = first_sums(made0, taken0, made1[0])
-    gate0, up0 = swapped(sums0[0], "row", 2), swapped(sums0[2], "row", 2)
-    made2 = chunk_grads(follow(place, sums0), 2)
+    sums0 = first_sums(made0, taken0)
+    second0 = second(sums0)
+    made2, taken1, second0 = together(chunk_grads(follow(place, sums0), 2), taken1, second0)
     taken2 = sent(made2)
-    sums1 = first_sums(made1, taken1, made2[0])
-    gate1, up1 = swapped(sums1[0], "row", 2), swapped(sums1[2], "row", 2)
-    made = (made0, made1, made2)
-    acts, gates, ups = ([one[i] for one in made] for i in range(3))
-    own_ntg, give_ntg = feed_sum(
-        follow(place, sums1), [gates, ups], [gate_weight, up_weight], True, block, "normed_two_grad"
+    sums1 = first_sums(made1, taken1)
+    second1 = second(sums1)
+    acts, gates, ups = ([one[i] for one in (made0, made1, made2)] for i in range(3))
+    (own_ntg, give_ntg), taken2, second1 = together(
+        feed_sum(follow(place, sums1), [gates, ups], [gate_weight, up_weight], True, block, "normed_two_grad"),
+        taken2,
+        second1,
     )
     take_ntg = swapped(give_ntg, "row", 1)
-    sums2 = first_sums(made2, taken2, own_ntg)
-    gate2, up2 = swapped(sums2[0], "row", 2), swapped(sums2[2], "row", 2)
-    down = jnp.concatenate([sums0[4], sums1[4], sums2[4]], axis=1)
+    sums2 = first_sums(made2, taken2)
+    second2 = second(sums2)
+    third_give, third_keep = joined([sums0[1], sums0[3], sums1[1], sums1[3]], second0 + second1, "third_sums")
+    third_take = swapped(third_give, "row", 2)
+
+    (residual_grad, mixer_grad, open_grad, conv_grad, sums), second2 = together(
+        mixer_middle(
+            follow(marks, sums2, third_keep), own_ntg, take_ntg, residual, upstream, product, before, output_gate,
+            out_weight, scales,
+        ),
+        second2,
+    )
+    after = passed_along(conv_grad.reshape(row_count, span_length, model_width)[:, :2, :], "seq", -1)
+    late_give, late_keep = joined([sums2[1], sums2[3]], second2, "late_sums")
+    late_take = swapped(late_give, "row", 2)
+    down = jnp.concatenate(follow([sums0[4], sums1[4], sums2[4]], mixer_grad), axis=1)
     low_half, high_half = down[:, : block // 2], down[:, block // 2 :]
     down_keep = jnp.where(seq_y == 0, low_half, high_half)
-    down_take = swapped(jnp.where(seq_y == 0, high_half, low_half), "seq", 1)
-    own_feed, give_feed = feed_sum(
-        follow(place, sums2), [acts], [down_weight], False, block, "feed_out"
-    )
+    down_give = jnp.where(seq_y == 0, high_half, low_half)
+
+    (out_give, out_keep), after, third_take, down_give = together(
+        pair_grads(follow(place, late_keep, down_keep, down_give), mixed_in, mixer_grad, (0, 1), "out_grads"),
+        after,
+        third_take,
+        down_give,
+    )
+    down_takes = [swapped(down_give[0], "seq", 1)]
+    out_take = swapped(out_give, "row", 1)
+    after = jnp.pad(after, ((0, 0), (0, 6), (0, 0))).reshape(row_count * 8, model_width)
+    fourth_give, fourth_keep = split(third_keep, third_take, 1)
+    fourth_takes = [swapped(fourth_give[:2], "seq", 4)]
+
+    project_grad = project_grads(
+        follow(marks, out_keep, fourth_give, fourth_keep), conv_grad, after, input_gate, values, open_grad, scales
+    )
+    (in_give,), out_take, late_take, down_takes, fourth_takes = together(
+        pair_grads(place, normed, project_grad, (0,), "in_grads_give"), out_take, late_take, down_takes, fourth_takes
+    )
+    in_take = swapped(in_give, "row", 1)
+    out_give, out_keep = split(out_keep, out_take, 0)
+    out_take = swapped(out_give, "row", 2)
+    down_takes.append(swapped(follow(down_give[1], out_give), "seq", 1))
+    fourth_takes.append(swapped(follow(fourth_give[2:], out_give), "seq", 4))
+    late_give, late_keep = split(late_keep, late_take, 1)
+
+    (in_keep,), in_take, out_take, down_takes, fourth_takes, late_give = together(
+        pair_grads(
+            follow(place, in_give, out_give, out_keep, late_give, late_keep), normed, project_grad, (1,), "in_grads_keep"
+        ),
+        in_take,
+        out_take,
+        down_takes,
+        fourth_takes,
+        late_give,
+    )
+    late_take = swapped(late_give, "seq", 4)
+    half = in_keep.shape[-1] // 2
+    left_give, left_keep = split(in_keep[..., :half], in_take[..., :half], 0)
+    left_take = swapped(left_give, "row", 2)
+    eighths = (2, 4, 2, model_width // 8, half)
+    right_give, right_keep = split(in_keep[..., half:].reshape(eighths), in_take[..., half:].reshape(eighths), 2)
+    right_take = swapped(right_give, "seq", 1)
+    eighths = (4, 2, model_width // 8, out_keep.shape[-1])
+    out_give, out_keep = split(out_keep.reshape(eighths), out_take.reshape(eighths), 1)
+    down_give, down_keep = (narrow(wide(down_keep[i], down_takes[i])) for i in range(2))
+
+    (input_grad, small), late_take, out_give, down_give = together(
+        mixer_backward(
+            follow(
+                project_grad, left_give, left_keep, right_give, right_keep, out_give, out_keep, down_give, down_keep,
+            ),
+            in_weight, hidden, residual_grad, sums, scales,
+        ),
+        late_take,
+        out_give,
+        down_give,
+    )
+    small_take = swapped(small, "row", 1)
+    out_take = swapped(out_give, "seq", 1)
+    quarter = down_give.shape[0] // 2
+    down_takes = [swapped(down_give[:quarter], "seq", 4)]
+    (own_feed, give_feed), left_take, right_take, out_take, small_take, down_takes = together(
+        feed_sum(follow(place, input_grad), [acts], [down_weight], False, block, "feed_out"),
+        left_take,
+        right_take,
+        out_take,
+        small_take,
+        down_takes,
+    )
+    down_takes.append(swapped(follow(down_give[quarter:], own_feed), "seq", 4))
     take_feed = swapped(give_feed, "row", 1)
-
-    residual_grad, mixer_grad, open_grad, conv_grad, sums = mixer_middle(
-        follow(marks, own_feed), own_ntg, take_ntg, residual, upstream, product, before, output_gate, out_weight, scales
-    )
-    after = passed_along(conv_grad.reshape(row_count, span_length, model_width)[:, :2, :], "seq", -1)
-    after = jnp.pad(after, ((0, 0), (0, 6), (0, 0))).reshape(row_count * 8, model_width)
-
-    (gate_take, up_take), _ = lax.optimization_barrier((([gate0, gate1, gate2], [up0, up1, up2]), mixer_grad))
-    sums_all = (sums0, sums1, sums2)
-    gate = jnp.stack([wide(one[1], take) for one, take in zip(sums_all, gate_take)])
-    gate_keep, gate_give = narrow(gate[:, :, 1]), narrow(gate[:, :, 0])
-    up = jnp.stack(
-        [wide(one[3], take).reshape(2, 2, model_width // 8, part) for one, take in zip(sums_all, up_take)]
-    )
-    up_keep, up_give = narrow(up[:, :, 1]), narrow(up[:, :, 0])
-    gate_take = swapped(gate_give, "seq", 1)
-    up_take = swapped(up_give, "seq", 2)
-
-    project_grad = project_grads(
-        follow(marks, gate_give, up_give), conv_grad, after, input_gate, values, open_grad, scales
-    )
-    (in_give,) = pair_grads(place, normed, project_grad, (0,), "in_grads_give")
-    in_take = swapped(in_give, "row", 1)
-    (in_keep,) = pair_grads(follow(place, in_give), normed, project_grad, (1,), "in_grads_keep")
-    out_give, out_keep = pair_grads(follow(place, in_keep), mixed_in, mixer_grad, (0, 1), "out_grads")
-
-    def sided(value):
-        return value.reshape(2, 2, 2, 2, value.shape[-2], value.shape[-1])
-
-    orders = (("x", "y", "z0", "z1"), ("y", "x", "z0", "z1"), ("z0", "x", "y", "z1"))
-    (in_keep, in_take), _ = lax.optimization_barrier(((in_keep, in_take), out_keep))
-    in_sum = sided(narrow(wide(in_keep, in_take)))
-    third = in_sum.shape[-1] // 3
-    names = ["x", "z1", "z0", "y"]
-    firsts = []
-    for i, order in enumerate(orders):
-        piece = in_sum[..., i * third : (i + 1) * third]
-        at = names.index(order[0])
-        firsts.append((lax.index_in_dim(piece, 1, at, False), lax.index_in_dim(piece, 0, at, False)))
-    in_moved = [swapped(give, *LINKS[order[0]]) for (_, give), order in zip(firsts, orders)]
-    out_take = swapped(out_give, "row", 1)
-    down = narrow(wide(down_keep, down_take))
-    down_keep, down_give = down[1], down[0]
-    down_take = swapped(down_give, "seq", 4)
-
-    input_grad, small = mixer_backward(
-        follow(project_grad, [give for _, give in firsts], down_give), in_weight, hidden, residual_grad, sums, scales
-    )
-    in_moved, _ = lax.optimization_barrier((in_moved, input_grad))
-    input_grad = input_grad.reshape(row_count, span_length, model_width)
-    in_part = jnp.concatenate(
-        [
-            settle(narrow(wide(keep, take)), order)
-            for (keep, _), take, order in zip(firsts, in_moved, orders)
-        ],
-        axis=1,
-    )
-    out_part = settle(sided(narrow(wide(out_keep, out_take))), ("y", "z0", "x", "z1"))
-    for axis, bit in (("row", 1), ("row", 2), ("seq", 1), ("seq", 2), ("seq", 4)):
-        small = small + swapped(small, axis, bit)
-    small = lax.dynamic_slice_in_dim(small, seq * (model_width // 8), model_width // 8, 1)
-
-    output = narrow(residual + valid_mask * wide(own_feed, take_feed)).reshape(row_count, span_length, model_width)
-    (gate_take, up_take), _ = lax.optimization_barrier(((gate_take, up_take), input_grad))
-    gate = wide(gate_keep, gate_take)
-    gate = wide(narrow(gate[:, 1]), swapped(narrow(gate[:, 0]), "seq", 4))
-    gate_part = jnp.concatenate([gate[i] for i in range(chunks)], axis=1)
-    up = wide(up_keep, up_take)
-    up = wide(narrow(up[:, 1]), swapped(narrow(up[:, 0]), "seq", 4))
-    up_part = jnp.concatenate([up[i] for i in range(chunks)], axis=1)
-    down_take, _ = lax.optimization_barrier((down_take, input_grad))
-    down = narrow(wide(down_keep, down_take))
+    eighths = (4, 2, model_width // 8, half)
+    left_give, left_keep = split(left_keep.reshape(eighths), left_take.reshape(eighths), 1)
+    left_take = swapped(left_give, "seq", 1)
+    right_give, right_keep = split(right_keep, right_take, 0)
+    right_take = swapped(right_give, "row", 2)
+    small = small + small_take
+    small_take = swapped(small, "row", 2)
+    (gate_part, up_part), left_take, right_take, take_feed, small_take = together(
+        last_sums(*follow(([fourth_keep[:2], fourth_keep[2:], late_keep], fourth_takes + [late_take]), left_give, right_give, small)),
+        left_take,
+        right_take,
+        take_feed,
+        small_take,
+    )
+    give, keep = side_by_side([left_keep, right_keep, out_keep], [left_take, right_take, out_take])
+    take = swapped(give, "seq", 2)
+    small = small + small_take
+    small_take = swapped(small, "seq", 1)
+    output = narrow(residual + valid_mask * wide(own_feed, follow(take_feed, give)))
+    output, small_take, down_takes = together(output, small_take, down_takes)
+    output = output.reshape(row_count, span_length, model_width)
+    down = narrow(wide(down_keep, jnp.concatenate(down_takes)))
+    small = small + small_take
+    small_take = swapped(small, "seq", 2)
     holder = [[(r & 1) == ((s >> 1) & 1) for r in range(4)] for s in range(8)]
-    down = wide(
+    down_take = lax.ppermute(
         down,
-        lax.ppermute(
-            down,
-            ("seq", "row"),
-            [(s * 4 + r, (s ^ 2) * 4 + r) for s in range(8) for r in range(4) if not holder[s][r]],
-        ),
-    )
+        ("seq", "row"),
+        [(s * 4 + r, (s ^ 2) * 4 + r) for s in range(8) for r in range(4) if not holder[s][r]],
+    )
+    take, small_take = together(take, small_take)
+    give, keep = split(keep, take, 0)
+    take = swapped(give, "seq", 4)
+    small = small + small_take
+    small_take = swapped(small, "seq", 4)
+    down = wide(down, follow(down_take, give))
     quarter = model_width // 4
     down_own = jnp.where(core == 0, down[:, :quarter], down[:, quarter:])
     down_other = narrow(jnp.where(core == 0, down[:, quarter:], down[:, :quarter]))
@@ -959,6 +1052,11 @@
         [(s * 4 + r, s * 4 + (r ^ 1)) for s in range(8) for r in range(4) if holder[s][r]],
     )
     down_part = jnp.where(core == seq_z0, down_own, down_other.astype(jnp.float32))
+    input_grad = input_grad.reshape(row_count, span_length, model_width)
+    both_part = wide(keep, take)
+    in_part, out_part = both_part[:, : 2 * half], both_part[:, 2 * half :]
+    small = small + small_take
+    small = lax.dynamic_slice_in_dim(small, seq * (model_width // 8), model_width // 8, 1)
     return (
         output,
         input_grad,

time: 447 us -> 354 us (0.79)
  waiting for transfers between devices: 120 us -> 38.5 us
  starting transfers between devices: 55.4 us -> 49.6 us
  local copies, waits for them, and re-layouts: 35.3 us -> 30.3 us
    ppermute x48 -> x43, waiting for transfers between devices: 117 us -> 38.4 us  [swapped(): return lax.ppermute(value, axis, [(i, i ^ bit) for i in range(length)])]
    convert_element_type x23 -> x24, other arithmetic: 22 us -> 31.1 us  [narrow(): return value.astype(jnp.bfloat16)]
    ppermute x48 -> x43, starting transfers between devices: 46.6 us -> 40.8 us  [swapped(): return lax.ppermute(value, axis, [(i, i ^ bit) for i in range(length)])]
    another operation x12 -> x0, other arithmetic: 5.16 us -> none
    convert_element_type x9 -> x0, local copies, waits for them, and re-layouts: 5.03 us -> none  [narrow(): return value.astype(jnp.bfloat16)]
    unnamed x158 -> x128, local copies, waits for them, and re-layouts: 24.8 us -> 20.7 us
  transfers between devices with their start and end apart: 52 -> 47, of which waited for: 23 -> 10; matrix products, arithmetic and copies ran while one was open for 9% -> 11% of each run, Pallas kernels for 31% -> 48%
where the time goes in v3:
time: 354 us; the launch traced here: 349 us
  Pallas kernels  194 us (55%)
  starting transfers between devices  49.6 us (14%)
  waiting for transfers between devices  38.5 us (11%)
  other arithmetic  34.3 us (10%)
  local copies, waits for them, and re-layouts  30.3 us (9%)
    pallas_call x3, Pallas kernels, feed_chunk(): pl.pallas_call(kernel, out_shape=[jax.ShapeDtypeStruct((both, span), low)...  84.9 us
    pallas_call x2, Pallas kernels, feed_sum(): pl.pallas_call(kernel, out_shape=[jax.ShapeDtypeStruct((tokens, width), l...  43.6 us
    ppermute x43, starting transfers between devices, swapped(): return lax.ppermute(value, axis, [(i, i ^ bit) for i in range(length)])  40.8 us
    ppermute x43, waiting for transfers between devices, swapped(): return lax.ppermute(value, axis, [(i, i ^ bit) for i in range(length)])  38.4 us
    convert_element_type x24, other arithmetic, narrow(): return value.astype(jnp.bfloat16)  31.1 us
    unnamed x128, local copies, waits for them, and re-layouts  20.7 us
    pallas_call x3, Pallas kernels, pair_grads(): pl.pallas_call(kernel, grid_spec=pltpu.PrefetchScalarGridSpec(num_scalar_...  20.6 us
    pallas_call x1, Pallas kernels, mixer_forward(): pl.pallas_call(kernel, grid=(steps,), in_specs=[rows(8), rows(width), row...  16.3 us
  transfers between devices with their start and end apart: 47, of which 10 were waited for; matrix products, arithmetic and copies ran while one was open for 11% of the time, Pallas kernels for 48%

profile of v3, /device:TPU:0, one launch (start us, length us, event | category | flops | bytes accessed | tf_op | source)
XLA Modules:
  0.0 349.0 jit_solution(10565713959962185729)
XLA Ops:
  1.4 4.9 %collective-permute-start = (bf16[2,2,1024]{2,1,0:T(2,128)(2,1)S(1)}, bf16[2,2,1024]{2,1,0:T(2,128)(2,1)S(1)}, u32[]{:S(2)}, u32[]{:S(2)}) collective-permute-start(bf16[2,2,1024]{2,1,0:T(2,128)(2,1)S(1)} %slice.274), channel_id=1, source_target_pairs={{0,4},{4,8},{8,12},{12,16},{16,20},{20,24},{24,28},{1,5},{5,9},{9,... | collective-permute-start | bytes 24584 | tf_op jit(solution)/shard_map/ppermute | solution.py:14
  7.1 3.4 multiply_convert_fusion.own_grad_ref
  11.6 16.3 %mixer_forward.1 = (bf16[1024,1024]{1,0:T(8,128)(2,1)S(1)}, bf16[1024,1024]{1,0:T(8,128)(2,1)S(1)}, bf16[1024,1024]{1,0:T(8,128)(2,1)S(1)}, bf16[1024,1024]{1,0:...) custom-call(f32[1024,8]{1,0:T(8,128)S(1)} %copy.75.marks_ref, ...), custom_call_target="tpu_custom_call" | custom-call | flops 8589934592 | bytes 29360128 | tf_op jit(solution)/shard_map/mixer_forward/pallas_call | solution.py:367
  33.0 3.5 %collective-permute-done.1.other_ref = bf16[1024,1024]{1,0:T(8,128)(2,1)} collective-permute-done((bf16[1024,1024]{1,0:T(8,128)(2,1)}, bf16[1024,1024]{1,0:T(8,128)(2,1)}, u32[]{:S(2)}, u32[]{:S(2)}) %collective-permute-start.1) | collective-permute-done | bytes 2097184 | tf_op jit(solution)/shard_map/ppermute | solution.py:31
  36.5 28.2 %feed_0.1 = (bf16[2048,768]{1,0:T(8,128)(2,1)}, bf16[2048,768]{1,0:T(8,128)(2,1)}, bf16[2048,768]{1,0:T(8,128)(2,1)}, bf16[2,2,2,128,384]{4,3,2,1,0:T(8,128)(2,1...) custom-call(s32[18]{0:T(128)} %stack.82.place_ref, ...), custom_call_target="tpu_custom_call" | custom-call | flops 19327352832 | bytes 25165824 | tf_op jit(solution)/shard_map/feed_0/pallas_call | solution.py:169
  69.4 28.5 %feed_1.1 = (bf16[2048,768]{1,0:T(8,128)(2,1)}, bf16[2048,768]{1,0:T(8,128)(2,1)}, bf16[2048,768]{1,0:T(8,128)(2,1)}, bf16[2,2,2,128,384]{4,3,2,1,0:T(8,128)(2,1...) custom-call(s32[18]{0:T(128)} %stack.82.place_ref, ...), custom_call_target="tpu_custom_call" | custom-call | flops 19327352832 | bytes 25165824 | tf_op jit(solution)/shard_map/feed_1/pallas_call | solution.py:169
  104.9 28.1 %feed_2.1 = (bf16[2048,768]{1,0:T(8,128)(2,1)}, bf16[2048,768]{1,0:T(8,128)(2,1)}, bf16[2048,768]{1,0:T(8,128)(2,1)}, bf16[2,2,2,128,384]{4,3,2,1,0:T(8,128)(2,1...) custom-call(s32[18]{0:T(128)} %stack.82.place_ref, ...), custom_call_target="tpu_custom_call" | custom-call | flops 19327352832 | bytes 25165824 | tf_op jit(solution)/shard_map/feed_2/pallas_call | solution.py:169
  142.9 27.5 %normed_two_grad.1 = (bf16[1024,1024]{1,0:T(8,128)(2,1)S(1)}, bf16[1024,1024]{1,0:T(8,128)(2,1)}) custom-call(s32[18]{0:T(128)S(1)} %copy-done.23, bf16[2048,768]{1,0:T(8,128)(2,1)} %get-tuple-element.215.refs_0_, bf16[2048,768]{1,0:T(8,128)(2,1)} %get-tuple-element.216.refs_1_, bf16[2048,768]{1,0:T(8,128)(2,1)} %get-tuple-element.217.refs_2_, ...), custom_call_target="tpu_custom_call" | custom-call | flops 19327352832 | bytes 25165824 | tf_op jit(solution)/shard_map/normed_two_grad/pallas_call | solution.py:280
  179.7 2.1 fusion.18
  182.6 2.1 fusion.17
  185.8 2.3 add_convert_fusion.5
  189.8 12.8 %mixer_middle.1 = (f32[1024,1024]{1,0:T(8,128)}, bf16[1024,1024]{1,0:T(8,128)(2,1)S(1)}, bf16[1024,1024]{1,0:T(8,128)(2,1)S(1)}, f32[1024,1024]{1,0:T(8,128)}, f32[8,1024]{1,0:T(8,128)S(1)}) custom-call(f32[1024,8]{1,0:T(8,128)S(1)} %copy.76.marks_ref, bf16[1024,1024]{1,0:T(8,128)(2,1)S(1)} %copy-done.5, ...), custom_call_target="tpu_custom_call" | custom-call | flops 2147483648 | bytes 33554432 | tf_op jit(solution)/shard_map/mixer_middle/pallas_call | solution.py:433
  202.7 2.1 late_sums.1
  210.5 5.3 %out_grads.1 = (bf16[2,8,128,256]{3,2,1,0:T(8,128)(2,1)}, bf16[2,8,128,256]{3,2,1,0:T(8,128)(2,1)S(1)}) custom-call(s32[18]{0:T(128)S(1)} %copy-done.23, bf16[1024,1024]{1,0:T(8,128)(2,1)S(1)} %copy-done.28, bf16[1024,1024]{1,0:T(8,128)(2,1)S(1)} %get-tuple-element.250.right_ref), custom_call_target="tpu_custom_call" | custom-call | flops 2147483648 | bytes 8388608 | tf_op jit(solution)/shard_map/out_grads/pallas_call | solution.py:515
  217.0 2.6 collective-permute-start.23
  219.6 2.1 add_convert_fusion.14
  222.5 2.6 collective-permute-start.24
  225.3 2.2 copy-done
  230.6 2.8 project_grads.1.right_ref.grad_ref
  233.5 7.7 %in_grads_give.1 = bf16[2,8,128,768]{3,2,1,0:T(8,128)(2,1)S(1)} custom-call(s32[18]{0:T(128)S(1)} %copy-done.23, bf16[1024,1024]{1,0:T(8,128)(2,1)S(1)} %copy-done.27, bf16[1024,3072]{1,0:T(8,128)(2,1)S(1)} %project_grads.1.right_ref.grad_ref), custom_call_target="tpu_custom_call" | custom-call | flops 3221225472 | bytes 8388608 | tf_op jit(solution)/shard_map/in_grads_give/pallas_call | solution.py:515
  245.9 7.7 %in_grads_keep.1 = bf16[2,8,128,768]{3,2,1,0:T(8,128)(2,1)S(1)} custom-call(s32[18]{0:T(128)S(1)} %copy-done.23, bf16[1024,1024]{1,0:T(8,128)(2,1)S(1)} %copy-done.27, bf16[1024,3072]{1,0:T(8,128)(2,1)S(1)} %project_grads.1.right_ref.grad_ref), custom_call_target="tpu_custom_call" | custom-call | flops 3221225472 | bytes 8388608 | tf_op jit(solution)/shard_map/in_grads_keep/pallas_call | solution.py:515
  253.6 4.0 %collective-permute-done.28.refs_4_ = bf16[2,128,384]{2,1,0:T(8,128)(2,1)S(1)} collective-permute-done((bf16[2,128,384]{2,1,0:T(8,128)(2,1)S(1)}, bf16[2,128,384]{2,1,0:T(8,128)(2,1)S(1)}, u32[]{:S(2)}, u32[]{:S(2)}) %collective-permute-start.28) | collective-permute-done | bytes 196640 | tf_op jit(solution)/shard_map/ppermute | solution.py:31
  265.8 9.5 %mixer_backward.1 = (bf16[1024,1024]{1,0:T(8,128)(2,1)}, f32[8,1024]{1,0:T(8,128)S(1)}) custom-call(bf16[1024,3072]{1,0:T(8,128)(2,1)S(1)} %project_grads.1.right_ref.grad_ref, bf16[1024,3072]{1,0:T(8,128)(2,1)S(1)} %bitcast.213, bf16[1024,1024]{1,0:T(8,128)(2,1)S(1)} %bitcast.211, f32[1024,1024]{1,0:T(8,128)S(1)} %copy-done.25, ...), custom_call_target="tpu_custom_call" | custom-call | flops 6442450944 | bytes 20971520 | tf_op jit(solution)/shard_map/mixer_backward/pallas_call | solution.py:557
  277.3 2.6 collective-permute-start.34
  279.9 16.1 %feed_out.1 = (bf16[1024,1024]{1,0:T(8,128)(2,1)S(1)}, bf16[1024,1024]{1,0:T(8,128)(2,1)S(1)}) custom-call(s32[18]{0:T(128)S(1)} %copy-done.23, bf16[2048,768]{1,0:T(8,128)(2,1)} %get-tuple-element.175.refs_0_, bf16[2048,768]{1,0:T(8,128)(2,1)} %get-tuple-element.292.refs_1_, bf16[2048,768]{1,0:T(8,128)(2,1)} %get-tuple-element.293.refs_2_, ...), custom_call_target="tpu_custom_call" | custom-call | flops 9663676416 | bytes 25165824 | tf_op jit(solution)/shard_map/feed_out/pallas_call | solution.py:280
  303.8 6.2 %collective-permute-done.38 = f32[8,1024]{1,0:T(8,128)S(1)} collective-permute-done((f32[8,1024]{1,0:T(8,128)S(1)}, f32[8,1024]{1,0:T(8,128)S(1)}, u32[]{:S(2)}, u32[]{:S(2)}) %collective-permute-start.38) | collective-permute-done | bytes 32800 | tf_op jit(solution)/shard_map/ppermute | solution.py:31
  310.1 1.8 collective-permute-done.35.refs_3_
  314.9 2.2 add_convert_fusion
  320.2 10.2 %collective-permute-done.42 = f32[8,1024]{1,0:T(8,128)S(1)} collective-permute-done((f32[8,1024]{1,0:T(8,128)S(1)}, f32[8,1024]{1,0:T(8,128)S(1)}, u32[]{:S(2)}, u32[]{:S(2)}) %collective-permute-start.42) | collective-permute-done | bytes 32800 | tf_op jit(solution)/shard_map/ppermute | solution.py:31
  330.6 3.0 collective-permute-start.44
  333.6 7.7 %collective-permute-done.43 = f32[8,1024]{1,0:T(8,128)S(1)} collective-permute-done((f32[8,1024]{1,0:T(8,128)S(1)}, f32[8,1024]{1,0:T(8,128)S(1)}, u32[]{:S(2)}, u32[]{:S(2)}) %collective-permute-start.43) | collective-permute-done | bytes 32800 | tf_op jit(solution)/shard_map/ppermute | solution.py:31
  343.9 2.3 collective-permute-done.44
  (281 shorter events, 86.6 us)
Async XLA Ops:
  10.5 22.5 %collective-permute-start.2 = (bf16[1024,1024]{1,0:T(8,128)(2,1)}, bf16[1024,1024]{1,0:T(8,128)(2,1)}, u32[]{:S(2)}, u32[]{:S(2)}) collective-permute-start(bf16[1024,1024]{1,0:T(8,128)(2,1)} %multiply_convert_fusion.own_grad_ref), channel_id=1, source_target_pairs={{0,1},{1,0},{2,3},{3,2},{4,5},{5,4},{6,7},{7,6},{8,9},{9,8},{10,11... | collective-permute-start | bytes 6291464 | tf_op jit(solution)/shard_map/ppermute | solution.py:31
  64.7 33.2 %collective-permute-start.3 = (bf16[2,2,2,128,384]{4,3,2,1,0:T(8,128)(2,1)}, bf16[2,2,2,128,384]{4,3,2,1,0:T(8,128)(2,1)S(1)}, u32[]{:S(2)}, u32[]{:S(2)}) collective-permute-start(bf16[2,2,2,128,384]{4,3,2,1,0:T(8,128)(2,1)} %get-tuple-element.186), channel_id=1, source_target_pairs={{0,8},{4,12},{8,0},{12,4},{16,24},{20,28},{24,16},{28,20},{1,9},{5... | collective-permute-start | bytes 2359304 | tf_op jit(solution)/shard_map/ppermute | solution.py:31
  66.4 31.5 %collective-permute-start.4 = (bf16[2,2,2,128,384]{4,3,2,1,0:T(8,128)(2,1)}, bf16[2,2,2,128,384]{4,3,2,1,0:T(8,128)(2,1)S(1)}, u32[]{:S(2)}, u32[]{:S(2)}) collective-permute-start(bf16[2,2,2,128,384]{4,3,2,1,0:T(8,128)(2,1)} %get-tuple-element.187), channel_id=1, source_target_pairs={{0,4},{4,0},{8,12},{12,8},{16,20},{20,16},{24,28},{28,24},{1,5},{5... | collective-permute-start | bytes 2359304 | tf_op jit(solution)/shard_map/ppermute | solution.py:31
  67.9 30.0 %collective-permute-start.5 = (bf16[2,384,512]{2,1,0:T(8,128)(2,1)}, bf16[2,384,512]{2,1,0:T(8,128)(2,1)S(1)}, u32[]{:S(2)}, u32[]{:S(2)}) collective-permute-start(bf16[2,384,512]{2,1,0:T(8,128)(2,1)} %get-tuple-element.188), channel_id=1, source_target_pairs={{0,2},{1,3},{2,0},{3,1},{4,6},{5,7},{6,4},{7,5},{8,10},{9,11},{10,... | collective-permute-start | bytes 2359304 | tf_op jit(solution)/shard_map/ppermute | solution.py:31
  98.2 34.9 %collective-permute-start.10 = (bf16[2,2,128,384]{3,2,1,0:T(8,128)(2,1)S(1)}, bf16[2,2,128,384]{3,2,1,0:T(8,128)(2,1)S(1)}, u32[]{:S(2)}, u32[]{:S(2)}) collective-permute-start(bf16[2,2,128,384]{3,2,1,0:T(8,128)(2,1)S(1)} %get-tuple-element.358), channel_id=1, source_target_pairs={{0,8},{4,12},{8,0},{12,4},{16,24},{20,28},{24,16},{28,20},{1,9},{5... | collective-permute-start | bytes 1179656 | tf_op jit(solution)/shard_map/ppermute | solution.py:31
  100.0 33.2 %collective-permute-start.9 = (bf16[2,2,128,384]{3,2,1,0:T(8,128)(2,1)}, bf16[2,2,128,384]{3,2,1,0:T(8,128)(2,1)S(1)}, u32[]{:S(2)}, u32[]{:S(2)}) collective-permute-start(bf16[2,2,128,384]{3,2,1,0:T(8,128)(2,1)} %get-tuple-element.360), channel_id=1, source_target_pairs={{0,4},{4,0},{8,12},{12,8},{16,20},{20,16},{24,28},{28,24},{1,5},{5... | collective-permute-start | bytes 1179656 | tf_op jit(solution)/shard_map/ppermute | solution.py:31
  101.6 31.5 %collective-permute-start.6 = (bf16[2,2,2,128,384]{4,3,2,1,0:T(8,128)(2,1)}, bf16[2,2,2,128,384]{4,3,2,1,0:T(8,128)(2,1)S(1)}, u32[]{:S(2)}, u32[]{:S(2)}) collective-permute-start(bf16[2,2,2,128,384]{4,3,2,1,0:T(8,128)(2,1)} %get-tuple-element.204), channel_id=1, source_target_pairs={{0,8},{4,12},{8,0},{12,4},{16,24},{20,28},{24,16},{28,20},{1,9},{5... | collective-permute-start | bytes 2359304 | tf_op jit(solution)/shard_map/ppermute | solution.py:31
  102.9 30.3 %collective-permute-start.7 = (bf16[2,2,2,128,384]{4,3,2,1,0:T(8,128)(2,1)}, bf16[2,2,2,128,384]{4,3,2,1,0:T(8,128)(2,1)}, u32[]{:S(2)}, u32[]{:S(2)}) collective-permute-start(bf16[2,2,2,128,384]{4,3,2,1,0:T(8,128)(2,1)} %get-tuple-element.205), channel_id=1, source_target_pairs={{0,4},{4,0},{8,12},{12,8},{16,20},{20,16},{24,28},{28,24},{1,5},{5... | collective-permute-start | bytes 2359304 | tf_op jit(solution)/shard_map/ppermute | solution.py:31
  104.4 28.8 %collective-permute-start.8 = (bf16[2,384,512]{2,1,0:T(8,128)(2,1)}, bf16[2,384,512]{2,1,0:T(8,128)(2,1)S(1)}, u32[]{:S(2)}, u32[]{:S(2)}) collective-permute-start(bf16[2,384,512]{2,1,0:T(8,128)(2,1)} %get-tuple-element.206), channel_id=1, source_target_pairs={{0,2},{1,3},{2,0},{3,1},{4,6},{5,7},{6,4},{7,5},{8,10},{9,11},{10,... | collective-permute-start | bytes 2359304 | tf_op jit(solution)/shard_map/ppermute | solution.py:31
  134.9 36.9 %collective-permute-start.15 = (bf16[2,2,128,384]{3,2,1,0:T(8,128)(2,1)S(1)}, bf16[2,2,128,384]{3,2,1,0:T(8,128)(2,1)S(1)}, u32[]{:S(2)}, u32[]{:S(2)}) collective-permute-start(bf16[2,2,128,384]{3,2,1,0:T(8,128)(2,1)S(1)} %get-tuple-element.354), channel_id=1, source_target_pairs={{0,8},{4,12},{8,0},{12,4},{16,24},{20,28},{24,16},{28,20},{1,9},{5... | collective-permute-start | bytes 1179656 | tf_op jit(solution)/shard_map/ppermute | solution.py:31
  136.7 35.8 %collective-permute-start.14 = (bf16[2,2,128,384]{3,2,1,0:T(8,128)(2,1)S(1)}, bf16[2,2,128,384]{3,2,1,0:T(8,128)(2,1)S(1)}, u32[]{:S(2)}, u32[]{:S(2)}) collective-permute-start(bf16[2,2,128,384]{3,2,1,0:T(8,128)(2,1)S(1)} %get-tuple-element.356), channel_id=1, source_target_pairs={{0,4},{4,0},{8,12},{12,8},{16,20},{20,16},{24,28},{28,24},{1,5},{5... | collective-permute-start | bytes 1179656 | tf_op jit(solution)/shard_map/ppermute | solution.py:31
  138.7 34.5 %collective-permute-start.11 = (bf16[2,2,2,128,384]{4,3,2,1,0:T(8,128)(2,1)S(1)}, bf16[2,2,2,128,384]{4,3,2,1,0:T(8,128)(2,1)}, u32[]{:S(2)}, u32[]{:S(2)}) collective-permute-start(bf16[2,2,2,128,384]{4,3,2,1,0:T(8,128)(2,1)S(1)} %copy-done.56), channel_id=1, source_target_pairs={{0,8},{4,12},{8,0},{12,4},{16,24},{20,28},{24,16},{28,20},{1,9},{5... | collective-permute-start | bytes 2359304 | tf_op jit(solution)/shard_map/ppermute | solution.py:31
  140.0 33.3 %collective-permute-start.12 = (bf16[2,2,2,128,384]{4,3,2,1,0:T(8,128)(2,1)S(1)}, bf16[2,2,2,128,384]{4,3,2,1,0:T(8,128)(2,1)}, u32[]{:S(2)}, u32[]{:S(2)}) collective-permute-start(bf16[2,2,2,128,384]{4,3,2,1,0:T(8,128)(2,1)S(1)} %copy-done.55), channel_id=1, source_target_pairs={{0,4},{4,0},{8,12},{12,8},{16,20},{20,16},{24,28},{28,24},{1,5},{5... | collective-permute-start | bytes 2359304 | tf_op jit(solution)/shard_map/ppermute | solution.py:31
  141.5 31.8 %collective-permute-start.13 = (bf16[2,384,512]{2,1,0:T(8,128)(2,1)S(1)}, bf16[2,384,512]{2,1,0:T(8,128)(2,1)}, u32[]{:S(2)}, u32[]{:S(2)}) collective-permute-start(bf16[2,384,512]{2,1,0:T(8,128)(2,1)S(1)} %copy-done.54), channel_id=1, source_target_pairs={{0,2},{1,3},{2,0},{3,1},{4,6},{5,7},{6,4},{7,5},{8,10},{9,11},{10,... | collective-permute-start | bytes 2359304 | tf_op jit(solution)/shard_map/ppermute | solution.py:31
  181.8 20.9 %collective-permute-start.18 = (bf16[2,2,128,384]{3,2,1,0:T(8,128)(2,1)}, bf16[2,2,128,384]{3,2,1,0:T(8,128)(2,1)}, u32[]{:S(2)}, u32[]{:S(2)}) collective-permute-start(bf16[2,2,128,384]{3,2,1,0:T(8,128)(2,1)} %get-tuple-element.350), channel_id=1, source_target_pairs={{0,8},{4,12},{8,0},{12,4},{16,24},{20,28},{24,16},{28,20},{1,9},{5... | collective-permute-start | bytes 1179656 | tf_op jit(solution)/shard_map/ppermute | solution.py:31
  184.7 18.0 %collective-permute-start.17 = (bf16[2,2,128,384]{3,2,1,0:T(8,128)(2,1)}, bf16[2,2,128,384]{3,2,1,0:T(8,128)(2,1)}, u32[]{:S(2)}, u32[]{:S(2)}) collective-permute-start(bf16[2,2,128,384]{3,2,1,0:T(8,128)(2,1)} %get-tuple-element.352), channel_id=1, source_target_pairs={{0,4},{4,0},{8,12},{12,8},{16,20},{20,16},{24,28},{28,24},{1,5},{5... | collective-permute-start | bytes 1179656 | tf_op jit(solution)/shard_map/ppermute | solution.py:31
  185.2 30.6 %collective-permute-start.20 = (bf16[4,2,128,384]{3,2,0,1:T(8,128)(2,1)}, bf16[4,2,128,384]{3,2,0,1:T(8,128)(2,1)}, u32[]{:S(2)}, u32[]{:S(2)}) collective-permute-start(bf16[4,2,128,384]{3,2,0,1:T(8,128)(2,1)} %copy.77), channel_id=1, source_target_pairs={{0,2},{1,3},{2,0},{3,1},{4,6},{5,7},{6,4},{7,5},{8,10},{9,11},{10,... | collective-permute-start | bytes 2359304 | tf_op jit(solution)/shard_map/ppermute | solution.py:31
  209.0 32.2 %collective-permute-start.22 = (bf16[2,2,128,384]{3,2,0,1:T(8,128)(2,1)S(1)}, bf16[2,2,128,384]{3,2,0,1:T(8,128)(2,1)}, u32[]{:S(2)}, u32[]{:S(2)}) collective-permute-start(bf16[2,2,128,384]{3,2,0,1:T(8,128)(2,1)S(1)} %copy.79), channel_id=1, source_target_pairs={{0,2},{1,3},{2,0},{3,1},{4,6},{5,7},{6,4},{7,5},{8,10},{9,11},{10,... | collective-permute-start | bytes 1179656 | tf_op jit(solution)/shard_map/ppermute | solution.py:31
  215.8 25.4 %collective-permute-start.21 = (bf16[2,8,128,256]{3,2,1,0:T(8,128)(2,1)}, bf16[2,8,128,256]{3,2,1,0:T(8,128)(2,1)}, u32[]{:S(2)}, u32[]{:S(2)}) collective-permute-start(bf16[2,8,128,256]{3,2,1,0:T(8,128)(2,1)} %get-tuple-element.267), channel_id=1, source_target_pairs={{0,1},{1,0},{2,3},{3,2},{4,5},{5,4},{6,7},{7,6},{8,9},{9,8},{10,11... | collective-permute-start | bytes 3145736 | tf_op jit(solution)/shard_map/ppermute | solution.py:31
  217.0 24.2 %collective-permute-start.23 = (bf16[576,512]{1,0:T(8,128)(2,1)}, bf16[576,512]{1,0:T(8,128)(2,1)}, u32[]{:S(2)}, u32[]{:S(2)}) collective-permute-start(bf16[576,512]{1,0:T(8,128)(2,1)} %get-tuple-element.365), channel_id=1, source_target_pairs={{0,4},{4,0},{8,12},{12,8},{16,20},{20,16},{24,28},{28,24},{1,5},{5... | collective-permute-start | bytes 1769480 | tf_op jit(solution)/shard_map/ppermute | solution.py:31
  222.5 18.7 %collective-permute-start.24 = (bf16[2,128,384]{2,1,0:T(8,128)(2,1)}, bf16[2,128,384]{2,1,0:T(8,128)(2,1)S(1)}, u32[]{:S(2)}, u32[]{:S(2)}) collective-permute-start(bf16[2,128,384]{2,1,0:T(8,128)(2,1)} %get-tuple-element.373), channel_id=1, source_target_pairs={{0,16},{4,20},{8,24},{12,28},{16,0},{20,4},{24,8},{28,12},{1,17},{... | collective-permute-start | bytes 589832 | tf_op jit(solution)/shard_map/ppermute | solution.py:31
  241.2 17.4 %collective-permute-start.25 = (bf16[2,8,128,768]{3,2,1,0:T(8,128)(2,1)S(1)}, bf16[2,8,128,768]{3,2,1,0:T(8,128)(2,1)S(1)}, u32[]{:S(2)}, u32[]{:S(2)}) collective-permute-start(bf16[2,8,128,768]{3,2,1,0:T(8,128)(2,1)S(1)} %in_grads_give.1), channel_id=1, source_target_pairs={{0,1},{1,0},{2,3},{3,2},{4,5},{5,4},{6,7},{7,6},{8,9},{9,8},{10,11... | collective-permute-start | bytes 9437192 | tf_op jit(solution)/shard_map/ppermute | solution.py:31
  242.9 15.7 %collective-permute-start.27 = (bf16[576,512]{1,0:T(8,128)(2,1)S(1)}, bf16[576,512]{1,0:T(8,128)(2,1)S(1)}, u32[]{:S(2)}, u32[]{:S(2)}) collective-permute-start(bf16[576,512]{1,0:T(8,128)(2,1)S(1)} %copy-done.44), channel_id=1, source_target_pairs={{0,4},{4,0},{8,12},{12,8},{16,20},{20,16},{24,28},{28,24},{1,5},{5... | collective-permute-start | bytes 1769480 | tf_op jit(solution)/shard_map/ppermute | solution.py:31
  261.9 34.2 %collective-permute-start.31 = (bf16[2,4,128,384]{3,2,1,0:T(8,128)(2,1)}, bf16[2,4,128,384]{3,2,1,0:T(8,128)(2,1)}, u32[]{:S(2)}, u32[]{:S(2)}) collective-permute-start(bf16[2,4,128,384]{3,2,1,0:T(8,128)(2,1)} %fusion.3), channel_id=1, source_target_pairs={{0,4},{4,0},{8,12},{12,8},{16,20},{20,16},{24,28},{28,24},{1,5},{5... | collective-permute-start | bytes 2359304 | tf_op jit(solution)/shard_map/ppermute | solution.py:31
  262.6 33.5 %collective-permute-start.30 = (bf16[8,128,384]{2,1,0:T(8,128)(2,1)}, bf16[8,128,384]{2,1,0:T(8,128)(2,1)}, u32[]{:S(2)}, u32[]{:S(2)}) collective-permute-start(bf16[8,128,384]{2,1,0:T(8,128)(2,1)} %get-tuple-element.339), channel_id=1, source_target_pairs={{0,2},{1,3},{2,0},{3,1},{4,6},{5,7},{6,4},{7,5},{8,10},{9,11},{10,... | collective-permute-start | bytes 2359304 | tf_op jit(solution)/shard_map/ppermute | solution.py:31
  275.3 20.7 %collective-permute-start.33 = (f32[8,1024]{1,0:T(8,128)S(1)}, f32[8,1024]{1,0:T(8,128)S(1)}, u32[]{:S(2)}, u32[]{:S(2)}) collective-permute-start(f32[8,1024]{1,0:T(8,128)S(1)} %get-tuple-element.297), channel_id=1, source_target_pairs={{0,1},{1,0},{2,3},{3,2},{4,5},{5,4},{6,7},{7,6},{8,9},{9,8},{10,11... | collective-permute-start | bytes 98312 | tf_op jit(solution)/shard_map/ppermute | solution.py:31
  275.3 20.7 %collective-permute-start.32 = (bf16[4,128,256]{2,1,0:T(8,128)(2,1)}, bf16[4,128,256]{2,1,0:T(8,128)(2,1)S(1)}, u32[]{:S(2)}, u32[]{:S(2)}) collective-permute-start(bf16[4,128,256]{2,1,0:T(8,128)(2,1)} %get-tuple-element.296), channel_id=1, source_target_pairs={{0,4},{4,0},{8,12},{12,8},{16,20},{20,16},{24,28},{28,24},{1,5},{5... | collective-permute-start | bytes 786440 | tf_op jit(solution)/shard_map/ppermute | solution.py:31
  277.3 18.7 %collective-permute-start.34 = (bf16[288,512]{1,0:T(8,128)(2,1)S(1)}, bf16[288,512]{1,0:T(8,128)(2,1)S(1)}, u32[]{:S(2)}, u32[]{:S(2)}) collective-permute-start(bf16[288,512]{1,0:T(8,128)(2,1)S(1)} %get-tuple-element.371), channel_id=1, source_target_pairs={{0,16},{4,20},{8,24},{12,28},{16,0},{20,4},{24,8},{28,12},{1,17},{... | collective-permute-start | bytes 884744 | tf_op jit(solution)/shard_map/ppermute | solution.py:31
  296.1 15.8 %collective-permute-start.37 = (bf16[1024,1024]{1,0:T(8,128)(2,1)S(1)}, bf16[1024,1024]{1,0:T(8,128)(2,1)S(1)}, u32[]{:S(2)}, u32[]{:S(2)}) collective-permute-start(bf16[1024,1024]{1,0:T(8,128)(2,1)S(1)} %get-tuple-element.314), channel_id=1, source_target_pairs={{0,1},{1,0},{2,3},{3,2},{4,5},{5,4},{6,7},{7,6},{8,9},{9,8},{10,11... | collective-permute-start | bytes 6291464 | tf_op jit(solution)/shard_map/ppermute | solution.py:31
  302.4 16.2 %collective-permute-start.40 = (bf16[288,512]{1,0:T(8,128)(2,1)}, bf16[288,512]{1,0:T(8,128)(2,1)S(1)}, u32[]{:S(2)}, u32[]{:S(2)}) collective-permute-start(bf16[288,512]{1,0:T(8,128)(2,1)} %get-tuple-element.323), channel_id=1, source_target_pairs={{0,16},{4,20},{8,24},{12,28},{16,0},{20,4},{24,8},{28,12},{1,17},{... | collective-permute-start | bytes 884744 | tf_op jit(solution)/shard_map/ppermute | solution.py:31
  312.2 18.3 %collective-permute-start.41 = (bf16[2,128,1024]{2,1,0:T(8,128)(2,1)S(1)}, bf16[2,128,1024]{2,1,0:T(8,128)(2,1)S(1)}, u32[]{:S(2)}, u32[]{:S(2)}) collective-permute-start(bf16[2,128,1024]{2,1,0:T(8,128)(2,1)S(1)} %get-tuple-element.319), channel_id=1, source_target_pairs={{0,8},{4,12},{8,0},{12,4},{16,24},{20,28},{24,16},{28,20},{1,9},{5... | collective-permute-start | bytes 1572872 | tf_op jit(solution)/shard_map/ppermute | solution.py:31
  318.8 23.0 %collective-permute-start.45 = (bf16[576,512]{1,0:T(8,128)(2,1)S(1)}, bf16[576,512]{1,0:T(8,128)(2,1)S(1)}, u32[]{:S(2)}, u32[]{:S(2)}) collective-permute-start(bf16[576,512]{1,0:T(8,128)(2,1)S(1)} %add_convert_fusion.8), channel_id=1, source_target_pairs={{1,9},{3,11},{5,13},{7,15},{8,0},{10,2},{12,4},{14,6},{17,25},{19,... | collective-permute-start | bytes 1769480 | tf_op jit(solution)/shard_map/ppermute | solution.py:1035
  (74 other events, 597.7 us)

commit v4 on v3

--- a/solution.py
+++ b/solution.py
@@ -24,6 +24,10 @@
     return lax.dot_general(
         left, right, (((1,), (1,)), ((), ())), preferred_element_type=jnp.float32
     )
+
+
+def far(*values):
+    return [pltpu.with_memory_space_constraint(value, pltpu.HBM) for value in values]
 
 
 def swapped(value, axis, bit):
@@ -55,7 +59,7 @@
     def kernel(
         place_ref, own_ref, other_ref, own_grad_ref, other_grad_ref, gate_ref, up_ref, down_ref,
         act_out, gate_out, up_out, gate_send, gate_keep, up_send, up_keep, down_send, down_keep,
-        tok, grd, wg, wu, wd, act, gg, ug, gw, uw, dw, in_sem, w_sem, out_sem, grad_sem,
+        tok, grd, wg, wu, wd, act, gg, ug, gw, uw, dw, tok_t, act_t, in_sem, w_sem, out_sem, grad_sem,
     ):
         def token_copy(t, which):
             buf = (tok, grd)[which]
@@ -106,6 +110,7 @@
             if t == 0:
                 for copy in weight_copies[2]:
                     copy.wait()
+            tok_t[:, at] = tok[at, :].T
             for n in range(span // step):
                 cols = pl.ds(n * step, step)
                 gate = jnp.dot(tok[at, :], wg[:, cols], preferred_element_type=jnp.float32)
@@ -113,7 +118,9 @@
                 grad = contract_cols(grd[at, :], wd[cols, :])
                 sig = jax.nn.sigmoid(gate)
                 gate_sig = gate * sig
-                act[at, cols] = narrow(gate_sig * up)
+                made = narrow(gate_sig * up)
+                act[at, cols] = made
+                act_t[cols, at] = made.T
                 ug[at, cols] = narrow(grad * gate_sig)
                 gg[at, cols] = narrow(grad * up * (sig + gate_sig * (1.0 - sig)))
             for n, (buf, out) in enumerate(((act, act_out), (gg, gate_out), (ug, up_out))):
@@ -124,7 +131,7 @@
         for buf, grad in ((gw, gg), (uw, ug)):
             for n in range(span // step):
                 cols = pl.ds(n * step, step)
-                total = narrow(contract_rows(tok[...], grad[:, cols]))
+                total = narrow(jnp.dot(tok_t[...], grad[:, cols], preferred_element_type=jnp.float32))
                 for i in range(8):
                     spot = place_ref[2 + i]
                     rows_i = total[i * eighth : (i + 1) * eighth]
@@ -153,7 +160,7 @@
         for side in range(2):
             for n in range(2):
                 cols = pl.ds(pl.multiple_of(place_ref[10 + side] * (width // 2) + n * (width // 4), 128), width // 4)
-                total = narrow(contract_rows(act[...], grd[:, cols]))
+                total = narrow(jnp.dot(act_t[...], grd[:, cols], preferred_element_type=jnp.float32))
                 for j in range(2):
                     dw[side, place_ref[12 + j], :, pl.ds(n * (width // 4), width // 4)] = total[j * part : (j + 1) * part]
             copy = pltpu.make_async_copy(dw.at[side], (down_send, down_keep)[side], grad_sem.at[side])
@@ -188,6 +195,8 @@
                 pltpu.VMEM((2, 8, eighth, part), low),
                 pltpu.VMEM((2, 8, eighth, part), low),
                 pltpu.VMEM((2, 2, part, width // 2), low),
+                pltpu.VMEM((width, both), low),
+                pltpu.VMEM((span, both), low),
                 pltpu.SemaphoreType.DMA((2, tiles)),
                 pltpu.SemaphoreType.DMA((3, 2)),
                 pltpu.SemaphoreType.DMA((3, tiles)),
@@ -200,21 +209,22 @@
     )(place, own_in, other_in, own_grad, other_grad, gate_weight, up_weight, down_weight)
 
 
-def feed_sum(place, groups, weights, across, block, name):
+def feed_sum(place, groups, weights, across, block, name, sides=(0, 1)):
     chunks = len(groups[0])
     both, span = groups[0][0].shape
     part = span // 2
     width = weights[0].shape[0] if across else weights[0].shape[1]
     tokens = both // 2
     tile = min(512, tokens)
-    tiles = both // tile
-    half_tiles = tiles // 2
+    half_tiles = tokens // tile
+    tiles = len(sides) * half_tiles
     kinds = len(groups)
 
     def kernel(place_ref, *refs):
         lefts = [refs[g * chunks : (g + 1) * chunks] for g in range(kinds)]
         rights = refs[kinds * chunks : kinds * chunks + kinds]
-        own_out, other_out, lbuf, wbuf, total, obuf, l_sem, w_sem, o_sem = refs[kinds * chunks + kinds :]
+        sums_out = refs[kinds * chunks + kinds : kinds * chunks + kinds + len(sides)]
+        lbuf, wbuf, total, obuf, l_sem, w_sem, o_sem = refs[kinds * chunks + kinds + len(sides) :]
 
         def weight_copies(k):
             slot = k % 2
@@ -230,13 +240,14 @@
             return copies
 
         def left_copies(k, t, slot):
+            row = (sides[t // half_tiles] * half_tiles + t % half_tiles) * tile
             return [
-                pltpu.make_async_copy(lefts[g][k].at[pl.ds(t * tile, tile)], lbuf.at[slot, g], l_sem.at[slot, g])
+                pltpu.make_async_copy(lefts[g][k].at[pl.ds(row, tile)], lbuf.at[slot, g], l_sem.at[slot, g])
                 for g in range(kinds)
             ]
 
         def out_copy(t, slot):
-            ref = own_out if t < half_tiles else other_out
+            ref = sums_out[t // half_tiles]
             return pltpu.make_async_copy(
                 obuf.at[slot], ref.at[pl.ds((t % half_tiles) * tile, tile)], o_sem.at[slot]
             )
@@ -279,12 +290,12 @@
     wshape = (width, span) if across else (span, width)
     return pl.pallas_call(
         kernel,
-        out_shape=[jax.ShapeDtypeStruct((tokens, width), low)] * 2,
+        out_shape=[jax.ShapeDtypeStruct((tokens, width), low)] * len(sides),
         grid_spec=pltpu.PrefetchScalarGridSpec(
             num_scalar_prefetch=1,
             grid=(1,),
             in_specs=[any_spec] * (kinds * chunks + kinds),
-            out_specs=[any_spec] * 2,
+            out_specs=[any_spec] * len(sides),
             scratch_shapes=[
                 pltpu.VMEM((2, kinds, tile, span), low),
                 pltpu.VMEM((2, kinds) + wshape, low),
@@ -369,9 +380,9 @@
         grid=(steps,),
         in_specs=[rows(8), rows(width), row_spec, whole(in_weight.shape), whole(out_weight.shape), whole(scales.shape)],
         out_specs=[rows(width)] * 8 + [row_spec],
-        out_shape=[jax.ShapeDtypeStruct((tokens, width), LOW)] * 6
-        + [jax.ShapeDtypeStruct((tokens, width), FULL), jax.ShapeDtypeStruct((tokens, width), LOW)]
-        + [jax.ShapeDtypeStruct((2 * MARGIN, width), LOW)],
+        out_shape=[pltpu.HBM((tokens, width), LOW)] * 6
+        + [pltpu.HBM((tokens, width), FULL), pltpu.HBM((tokens, width), LOW)]
+        + [pltpu.HBM((2 * MARGIN, width), LOW)],
         scratch_shapes=[pltpu.VMEM((tile + MARGIN, width), FULL), pltpu.VMEM((MARGIN, width), FULL)],
         compiler_params=pltpu.CompilerParams(vmem_limit_bytes=44 << 20),
         cost_estimate=pl.CostEstimate(flops=8 * tokens * width * width, bytes_accessed=28 << 20, transcendentals=0),
@@ -762,12 +773,18 @@
             for side in range(2):
                 refs[2 * count + side][n] = narrow(wide(refs[n][side], refs[count + n][side]))
 
+    def spec(first):
+        return pl.BlockSpec((first, 1) + shape[2:], lambda i: (0, i, 0, 0))
+
     return pl.pallas_call(
         kernel,
-        out_shape=[jax.ShapeDtypeStruct(shape, LOW)] * 2,
+        grid=(shape[1],),
+        in_specs=[spec(2)] * (2 * count),
+        out_specs=[spec(count)] * 2,
+        out_shape=[pltpu.HBM(shape, LOW)] * 2,
         compiler_params=pltpu.CompilerParams(vmem_limit_bytes=32 << 20),
         name=name,
-    )(*keeps, *takes)
+    )(*far(*keeps, *takes))
 
 
 def side_by_side(keeps, takes):
@@ -779,17 +796,20 @@
         for n in range(count):
             at = pl.ds(sum(widths[:n]), widths[n])
             for side in range(2):
-                for h in range(2):
-                    refs[2 * count + side][h, :, at] = narrow(
-                        wide(refs[n][2 * h + side], refs[count + n][2 * h + side])
-                    )
+                refs[2 * count + side][0, :, at] = narrow(wide(refs[n][side], refs[count + n][side]))
+
+    def spec(first, last):
+        return pl.BlockSpec((first, shape[1], last), lambda i: (i, 0, 0))
 
     return pl.pallas_call(
         kernel,
-        out_shape=[jax.ShapeDtypeStruct(shape, LOW)] * 2,
+        grid=(2,),
+        in_specs=[spec(2, size) for size in widths] * 2,
+        out_specs=[spec(1, shape[2])] * 2,
+        out_shape=[pltpu.HBM(shape, LOW)] * 2,
         compiler_params=pltpu.CompilerParams(vmem_limit_bytes=32 << 20),
         name="side_by_side",
-    )(*keeps, *takes)
+    )(*far(*keeps, *takes))
 
 
 def last_sums(keeps, takes):
@@ -806,12 +826,16 @@
                 )
                 n += 1
 
+    rows = height // 2
     return pl.pallas_call(
         kernel,
-        out_shape=[jax.ShapeDtypeStruct(shape, FULL)] * 2,
+        grid=(2,),
+        in_specs=[pl.BlockSpec((count, rows, part), lambda i: (0, i, 0)) for count in counts] * 2,
+        out_specs=[pl.BlockSpec((rows, shape[1]), lambda i: (i, 0))] * 2,
+        out_shape=[pltpu.HBM(shape, FULL)] * 2,
         compiler_params=pltpu.CompilerParams(vmem_limit_bytes=32 << 20),
         name="last_sums",
-    )(*keeps, *takes)
+    )(*far(*keeps, *takes))
 
 
 def fast(
@@ -946,32 +970,30 @@
     out_take = swapped(out_give, "row", 1)
     after = jnp.pad(after, ((0, 0), (0, 6), (0, 0))).reshape(row_count * 8, model_width)
     fourth_give, fourth_keep = split(third_keep, third_take, 1)
-    fourth_takes = [swapped(fourth_give[:2], "seq", 4)]
+    fourth_take = swapped(fourth_give, "seq", 4)
 
     project_grad = project_grads(
         follow(marks, out_keep, fourth_give, fourth_keep), conv_grad, after, input_gate, values, open_grad, scales
     )
-    (in_give,), out_take, late_take, down_takes, fourth_takes = together(
-        pair_grads(place, normed, project_grad, (0,), "in_grads_give"), out_take, late_take, down_takes, fourth_takes
+    (in_give,), out_take, late_take, down_takes, fourth_take = together(
+        pair_grads(place, normed, project_grad, (0,), "in_grads_give"), out_take, late_take, down_takes, fourth_take
     )
     in_take = swapped(in_give, "row", 1)
     out_give, out_keep = split(out_keep, out_take, 0)
     out_take = swapped(out_give, "row", 2)
     down_takes.append(swapped(follow(down_give[1], out_give), "seq", 1))
-    fourth_takes.append(swapped(follow(fourth_give[2:], out_give), "seq", 4))
     late_give, late_keep = split(late_keep, late_take, 1)
-
-    (in_keep,), in_take, out_take, down_takes, fourth_takes, late_give = together(
+    late_take = swapped(late_give, "seq", 4)
+
+    (in_keep,), in_take, out_take, down_takes, late_take = together(
         pair_grads(
             follow(place, in_give, out_give, out_keep, late_give, late_keep), normed, project_grad, (1,), "in_grads_keep"
         ),
         in_take,
         out_take,
         down_takes,
-        fourth_takes,
-        late_give,
-    )
-    late_take = swapped(late_give, "seq", 4)
+        late_take,
+    )
     half = in_keep.shape[-1] // 2
     left_give, left_keep = split(in_keep[..., :half], in_take[..., :half], 0)
     left_take = swapped(left_give, "row", 2)
@@ -981,68 +1003,69 @@
     eighths = (4, 2, model_width // 8, out_keep.shape[-1])
     out_give, out_keep = split(out_keep.reshape(eighths), out_take.reshape(eighths), 1)
     down_give, down_keep = (narrow(wide(down_keep[i], down_takes[i])) for i in range(2))
-
-    (input_grad, small), late_take, out_give, down_give = together(
+    quarter = down_give.shape[0] // 2
+    down_takes = [swapped(down_give[:quarter], "seq", 4)]
+
+    (input_grad, small), left_take, right_take, down_takes, out_give, down_give = together(
         mixer_backward(
             follow(
                 project_grad, left_give, left_keep, right_give, right_keep, out_give, out_keep, down_give, down_keep,
             ),
             in_weight, hidden, residual_grad, sums, scales,
         ),
-        late_take,
+        left_take,
+        right_take,
+        down_takes,
         out_give,
         down_give,
     )
+    eighths = (4, 2, model_width // 8, half)
+    left_give, left_keep = split(left_keep.reshape(eighths), left_take.reshape(eighths), 1)
+    left_take = swapped(left_give, "seq", 1)
+    right_give, right_keep = split(right_keep, right_take, 0)
+    right_take = swapped(right_give, "row", 2)
     small_take = swapped(small, "row", 1)
-    out_take = swapped(out_give, "seq", 1)
-    quarter = down_give.shape[0] // 2
-    down_takes = [swapped(down_give[:quarter], "seq", 4)]
-    (own_feed, give_feed), left_take, right_take, out_take, small_take, down_takes = together(
-        feed_sum(follow(place, input_grad), [acts], [down_weight], False, block, "feed_out"),
+    down_takes.append(swapped(down_give[quarter:], "seq", 4))
+    out_take = swapped(follow(out_give, left_give), "seq", 1)
+
+    (give_feed,), left_take, right_take, out_take, small_take, down_takes = together(
+        feed_sum(
+            follow(place, left_give, left_keep, right_give, right_keep),
+            [acts], [down_weight], False, block, "feed_out_give", (1,),
+        ),
         left_take,
         right_take,
         out_take,
         small_take,
         down_takes,
     )
-    down_takes.append(swapped(follow(down_give[quarter:], own_feed), "seq", 4))
+    give, keep = side_by_side([left_keep, right_keep, out_keep], [left_take, right_take, out_take])
+    take = swapped(give, "seq", 2)
     take_feed = swapped(give_feed, "row", 1)
-    eighths = (4, 2, model_width // 8, half)
-    left_give, left_keep = split(left_keep.reshape(eighths), left_take.reshape(eighths), 1)
-    left_take = swapped(left_give, "seq", 1)
-    right_give, right_keep = split(right_keep, right_take, 0)
-    right_take = swapped(right_give, "row", 2)
     small = small + small_take
     small_take = swapped(small, "row", 2)
-    (gate_part, up_part), left_take, right_take, take_feed, small_take = together(
-        last_sums(*follow(([fourth_keep[:2], fourth_keep[2:], late_keep], fourth_takes + [late_take]), left_give, right_give, small)),
-        left_take,
-        right_take,
-        take_feed,
-        small_take,
-    )
-    give, keep = side_by_side([left_keep, right_keep, out_keep], [left_take, right_take, out_take])
-    take = swapped(give, "seq", 2)
-    small = small + small_take
-    small_take = swapped(small, "seq", 1)
-    output = narrow(residual + valid_mask * wide(own_feed, follow(take_feed, give)))
-    output, small_take, down_takes = together(output, small_take, down_takes)
-    output = output.reshape(row_count, span_length, model_width)
-    down = narrow(wide(down_keep, jnp.concatenate(down_takes)))
-    small = small + small_take
-    small_take = swapped(small, "seq", 2)
+    down = narrow(wide(down_keep, jnp.concatenate(follow(down_takes, give))))
     holder = [[(r & 1) == ((s >> 1) & 1) for r in range(4)] for s in range(8)]
     down_take = lax.ppermute(
         down,
         ("seq", "row"),
         [(s * 4 + r, (s ^ 2) * 4 + r) for s in range(8) for r in range(4) if not holder[s][r]],
     )
-    take, small_take = together(take, small_take)
+
+    (own_feed,), take, take_feed, small_take, down_take = together(
+        feed_sum(
+            follow(place, give, keep, small, down), [acts], [down_weight], False, block, "feed_out_keep", (0,)
+        ),
+        take,
+        take_feed,
+        small_take,
+        down_take,
+    )
     give, keep = split(keep, take, 0)
     take = swapped(give, "seq", 4)
     small = small + small_take
-    small_take = swapped(small, "seq", 4)
-    down = wide(down, follow(down_take, give))
+    small_take = swapped(small, "seq", 1)
+    down = wide(down, down_take)
     quarter = model_width // 4
     down_own = jnp.where(core == 0, down[:, :quarter], down[:, quarter:])
     down_other = narrow(jnp.where(core == 0, down[:, quarter:], down[:, :quarter]))
@@ -1051,6 +1074,16 @@
         ("seq", "row"),
         [(s * 4 + r, s * 4 + (r ^ 1)) for s in range(8) for r in range(4) if holder[s][r]],
     )
+    (gate_part, up_part), small_take = together(
+        last_sums(*follow(([fourth_keep, late_keep], [fourth_take, late_take]), give)), small_take
+    )
+    small = small + small_take
+    small_take = swapped(small, "seq", 2)
+    output = narrow(residual + valid_mask * wide(own_feed, follow(take_feed, small)))
+    output, small_take = together(output, small_take)
+    output = output.reshape(row_count, span_length, model_width)
+    small = small + small_take
+    small_take = swapped(small, "seq", 4)
     down_part = jnp.where(core == seq_z0, down_own, down_other.astype(jnp.float32))
     input_grad = input_grad.reshape(row_count, span_length, model_width)
     both_part = wide(keep, take)

time: 354 us -> 345 us (0.975)
  Pallas kernels: 194 us -> 203 us
  local copies, waits for them, and re-layouts: 30.3 us -> 22.2 us
  waiting for transfers between devices: 38.5 us -> 30.8 us
    ppermute x43 -> x42, waiting for transfers between devices: 38.4 us -> 24.5 us  [swapped(): return lax.ppermute(value, axis, [(i, i ^ bit) for i in range(length)])]
    unnamed x128 -> x126, local copies, waits for them, and re-layouts: 20.7 us -> 12.2 us
    pallas_call x4, Pallas kernels: 3.79 us -> 11.3 us  [the longest x2 6.2 us: joined(): pl.pallas_call(kernel, grid=(shape[1],), in_specs=[spec(2)] * (2 * count)...]
    ppermute x1, waiting for transfers between devices: 0.01 us -> 6.32 us  [fast(): lax.ppermute(down, ('seq', 'row'), [(s * 4 + r, (s ^ 2) * 4 + r) for s in...]
    pallas_call x2 -> x3, Pallas kernels: 43.6 us -> 45.4 us  [feed_sum(): pl.pallas_call(kernel, out_shape=[jax.ShapeDtypeStruct((tokens, width), l...]
    ppermute x43 -> x42, starting transfers between devices: 40.8 us -> 40.5 us  [swapped(): return lax.ppermute(value, axis, [(i, i ^ bit) for i in range(length)])]
  transfers between devices with their start and end apart: 47 -> 46, of which waited for: 10 -> 13; matrix products, arithmetic and copies ran while one was open for 11% -> 11% of each run, Pallas kernels for 48% -> 51%
where the time goes in v4:
time: 345 us; the launch traced here: 340 us
  Pallas kernels  203 us (59%)
  starting transfers between devices  49.3 us (14%)
  other arithmetic  32.8 us (10%)
  waiting for transfers between devices  30.8 us (9%)
  local copies, waits for them, and re-layouts  22.2 us (6%)
    pallas_call x3, Pallas kernels, feed_chunk(): pl.pallas_call(kernel, out_shape=[jax.ShapeDtypeStruct((both, span), low)...  84.2 us
    pallas_call x3, Pallas kernels, feed_sum(): pl.pallas_call(kernel, out_shape=[jax.ShapeDtypeStruct((tokens, width), l...  45.4 us
    ppermute x42, starting transfers between devices, swapped(): return lax.ppermute(value, axis, [(i, i ^ bit) for i in range(length)])  40.5 us
    convert_element_type x24, other arithmetic, narrow(): return value.astype(jnp.bfloat16)  29.7 us
    ppermute x42, waiting for transfers between devices, swapped(): return lax.ppermute(value, axis, [(i, i ^ bit) for i in range(length)])  24.5 us
    pallas_call x3, Pallas kernels, pair_grads(): pl.pallas_call(kernel, grid_spec=pltpu.PrefetchScalarGridSpec(num_scalar_...  20.6 us
    pallas_call x1, Pallas kernels, mixer_forward(): pl.pallas_call(kernel, grid=(steps,), in_specs=[rows(8), rows(width), row...  16.3 us
    pallas_call x1, Pallas kernels, mixer_middle(): pl.pallas_call(kernel, grid=(steps,), in_specs=[rows(8)] + [rows(width)]...  13 us
  transfers between devices with their start and end apart: 46, of which 13 were waited for; matrix products, arithmetic and copies ran while one was open for 11% of the time, Pallas kernels for 51%

profile of v4, /device:TPU:0, one launch (start us, length us, event | category | flops | bytes accessed | tf_op | source)
XLA Modules:
  0.0 340.3 jit_solution(14048355718759634013)
XLA Ops:
  1.4 4.9 %collective-permute-start = (bf16[2,2,1024]{2,1,0:T(2,128)(2,1)S(1)}, bf16[2,2,1024]{2,1,0:T(2,128)(2,1)S(1)}, u32[]{:S(2)}, u32[]{:S(2)}) collective-permute-start(bf16[2,2,1024]{2,1,0:T(2,128)(2,1)S(1)} %slice.250), channel_id=1, source_target_pairs={{0,4},{4,8},{8,12},{12,16},{16,20},{20,24},{24,28},{1,5},{5,9},{9,... | collective-permute-start | bytes 24584 | tf_op jit(solution)/shard_map/ppermute | solution.py:14
  7.2 3.5 %multiply_convert_fusion.own_grad_ref = bf16[1024,1024]{1,0:T(8,128)(2,1)} fusion(f32[1024]{0:T(1024)S(1)} %compare_convert_fusion.1, bf16[2,512,1024]{2,1,0:T(8,128)(2,1)} %param.23), kind=kLoop, calls=%fused_computation.1 | loop fusion | flops 3145728 | bytes 4198400 | tf_op jit(solution)/shard_map/convert_element_type | solution.py:43
  13.3 16.3 %mixer_forward.1 = (bf16[1024,1024]{1,0:T(8,128)(2,1)}, bf16[1024,1024]{1,0:T(8,128)(2,1)}, bf16[1024,1024]{1,0:T(8,128)(2,1)}, bf16[1024,1024]{1,0:T(8,128)(2,1...) custom-call(f32[1024,8]{1,0:T(8,128)S(1)} %copy.75.marks_ref, ...), custom_call_target="tpu_custom_call" | custom-call | flops 8589934592 | bytes 29360128 | tf_op jit(solution)/shard_map/mixer_forward/pallas_call | solution.py:378
  30.9 3.4 collective-permute-done.1.other_ref
  35.6 27.9 %feed_0.1 = (bf16[2048,768]{1,0:T(8,128)(2,1)}, bf16[2048,768]{1,0:T(8,128)(2,1)}, bf16[2048,768]{1,0:T(8,128)(2,1)}, bf16[2,2,2,128,384]{4,3,2,1,0:T(8,128)(2,1...) custom-call(s32[18]{0:T(128)} %stack.82.place_ref, ...), custom_call_target="tpu_custom_call" | custom-call | flops 19327352832 | bytes 25165824 | tf_op jit(solution)/shard_map/feed_0/pallas_call | solution.py:176
  68.1 28.1 %feed_1.1 = (bf16[2048,768]{1,0:T(8,128)(2,1)}, bf16[2048,768]{1,0:T(8,128)(2,1)}, bf16[2048,768]{1,0:T(8,128)(2,1)}, bf16[2,2,2,128,384]{4,3,2,1,0:T(8,128)(2,1...) custom-call(s32[18]{0:T(128)} %stack.82.place_ref, ...), custom_call_target="tpu_custom_call" | custom-call | flops 19327352832 | bytes 25165824 | tf_op jit(solution)/shard_map/feed_1/pallas_call | solution.py:176
  103.1 28.1 %feed_2.1 = (bf16[2048,768]{1,0:T(8,128)(2,1)}, bf16[2048,768]{1,0:T(8,128)(2,1)}, bf16[2048,768]{1,0:T(8,128)(2,1)}, bf16[2,2,2,128,384]{4,3,2,1,0:T(8,128)(2,1...) custom-call(s32[18]{0:T(128)} %stack.82.place_ref, ...), custom_call_target="tpu_custom_call" | custom-call | flops 19327352832 | bytes 25165824 | tf_op jit(solution)/shard_map/feed_2/pallas_call | solution.py:176
  140.0 27.7 %normed_two_grad.1 = (bf16[1024,1024]{1,0:T(8,128)(2,1)S(1)}, bf16[1024,1024]{1,0:T(8,128)(2,1)}) custom-call(s32[18]{0:T(128)S(1)} %copy-done.9, bf16[2048,768]{1,0:T(8,128)(2,1)} %get-tuple-element.211.refs_0_, bf16[2048,768]{1,0:T(8,128)(2,1)} %get-tuple-element.212.refs_1_, bf16[2048,768]{1,0:T(8,128)(2,1)} %get-tuple-element.213.refs_2_, ...), custom_call_target="tpu_custom_call" | custom-call | flops 19327352832 | bytes 25165824 | tf_op jit(solution)/shard_map/normed_two_grad/pallas_call | solution.py:291
  168.5 3.1 third_sums.1
  173.8 2.3 fusion.18
  179.7 2.2 add_convert_fusion.5
  182.1 13.0 %mixer_middle.1 = (f32[1024,1024]{1,0:T(8,128)}, bf16[1024,1024]{1,0:T(8,128)(2,1)S(1)}, bf16[1024,1024]{1,0:T(8,128)(2,1)S(1)}, f32[1024,1024]{1,0:T(8,128)}, f32[8,1024]{1,0:T(8,128)S(1)}) custom-call(f32[1024,8]{1,0:T(8,128)S(1)} %copy.76.marks_ref, bf16[1024,1024]{1,0:T(8,128)(2,1)S(1)} %get-tuple-element.233.own_ref, ...), custom_call_target="tpu_custom_call" | custom-call | flops 2147483648 | bytes 33554432 | tf_op jit(solution)/shard_map/mixer_middle/pallas_call | solution.py:444
  195.1 3.1 late_sums.1
  201.9 5.3 %out_grads.1 = (bf16[2,8,128,256]{3,2,1,0:T(8,128)(2,1)}, bf16[2,8,128,256]{3,2,1,0:T(8,128)(2,1)S(1)}) custom-call(s32[18]{0:T(128)S(1)} %copy-done.9, bf16[1024,1024]{1,0:T(8,128)(2,1)S(1)} %copy-done.14, bf16[1024,1024]{1,0:T(8,128)(2,1)S(1)} %get-tuple-element.246.right_ref), custom_call_target="tpu_custom_call" | custom-call | flops 2147483648 | bytes 8388608 | tf_op jit(solution)/shard_map/out_grads/pallas_call | solution.py:526
  210.6 2.6 collective-permute-start.23
  215.5 2.6 collective-permute-start.24
  223.7 2.9 project_grads.1.right_ref.grad_ref
  226.6 7.7 %in_grads_give.1 = bf16[2,8,128,768]{3,2,1,0:T(8,128)(2,1)S(1)} custom-call(s32[18]{0:T(128)S(1)} %copy-done.9, bf16[1024,1024]{1,0:T(8,128)(2,1)S(1)} %copy-done.13, bf16[1024,3072]{1,0:T(8,128)(2,1)S(1)} %project_grads.1.right_ref.grad_ref), custom_call_target="tpu_custom_call" | custom-call | flops 3221225472 | bytes 8388608 | tf_op jit(solution)/shard_map/in_grads_give/pallas_call | solution.py:526
  241.4 7.7 %in_grads_keep.1 = bf16[2,8,128,768]{3,2,1,0:T(8,128)(2,1)S(1)} custom-call(s32[18]{0:T(128)S(1)} %copy-done.9, bf16[1024,1024]{1,0:T(8,128)(2,1)S(1)} %copy-done.13, bf16[1024,3072]{1,0:T(8,128)(2,1)S(1)} %project_grads.1.right_ref.grad_ref), custom_call_target="tpu_custom_call" | custom-call | flops 3221225472 | bytes 8388608 | tf_op jit(solution)/shard_map/in_grads_keep/pallas_call | solution.py:526
  249.1 4.2 %collective-permute-done.28.refs_3_ = bf16[2,128,384]{2,1,0:T(8,128)(2,1)S(1)} collective-permute-done((bf16[2,128,384]{2,1,0:T(8,128)(2,1)S(1)}, bf16[2,128,384]{2,1,0:T(8,128)(2,1)S(1)}, u32[]{:S(2)}, u32[]{:S(2)}) %collective-permute-start.28) | collective-permute-done | bytes 196640 | tf_op jit(solution)/shard_map/ppermute | solution.py:35
  259.8 9.5 %mixer_backward.1 = (bf16[1024,1024]{1,0:T(8,128)(2,1)}, f32[8,1024]{1,0:T(8,128)S(1)}) custom-call(bf16[1024,3072]{1,0:T(8,128)(2,1)S(1)} %project_grads.1.right_ref.grad_ref, bf16[1024,3072]{1,0:T(8,128)(2,1)S(1)} %bitcast.209, bf16[1024,1024]{1,0:T(8,128)(2,1)S(1)} %bitcast.207, f32[1024,1024]{1,0:T(8,128)S(1)} %copy-done.12, ...), custom_call_target="tpu_custom_call" | custom-call | flops 6442450944 | bytes 20971520 | tf_op jit(solution)/shard_map/mixer_backward/pallas_call | solution.py:568
  269.5 2.2 collective-permute-done.31
  271.7 3.6 %collective-permute-done.30 = bf16[2,4,128,384]{3,2,1,0:T(8,128)(2,1)S(1)} collective-permute-done((bf16[2,4,128,384]{3,2,1,0:T(8,128)(2,1)S(1)}, bf16[2,4,128,384]{3,2,1,0:T(8,128)(2,1)S(1)}, u32[]{:S(2)}, u32[]{:S(2)}) %collective-permute-start.30) | collective-permute-done | bytes 786464 | tf_op jit(solution)/shard_map/ppermute | solution.py:35
  281.2 2.7 collective-permute-start.36
  283.9 8.9 %feed_out_give.1 = bf16[1024,1024]{1,0:T(8,128)(2,1)S(1)} custom-call(s32[18]{0:T(128)S(1)} %copy-done.9, bf16[2048,768]{1,0:T(8,128)(2,1)S(1)} %copy-done.15, bf16[2048,768]{1,0:T(8,128)(2,1)} %get-tuple-element.285.refs_1_, bf16[2048,768]{1,0:T(8,128)(2,1)} %get-tuple-element.286.refs_2_, bf16[4608,1024]{1,0:T(8,128)(2,1)} %refs_3_.3), custom_call_target="tpu_custom_call" | custom-call | flops 9663676416 | bytes 25165824 | tf_op jit(solution)/shard_map/feed_out_give/pallas_call | solution.py:291
  293.5 4.2 %collective-permute-done.36 = bf16[288,512]{1,0:T(8,128)(2,1)} collective-permute-done((bf16[288,512]{1,0:T(8,128)(2,1)S(1)}, bf16[288,512]{1,0:T(8,128)(2,1)}, u32[]{:S(2)}, u32[]{:S(2)}) %collective-permute-start.36) | collective-permute-done | bytes 294944 | tf_op jit(solution)/shard_map/ppermute | solution.py:35
  298.4 2.8 side_by_side.1
  305.5 8.9 %feed_out_keep.1 = bf16[1024,1024]{1,0:T(8,128)(2,1)S(1)} custom-call(s32[18]{0:T(128)S(1)} %copy-done.9, bf16[2048,768]{1,0:T(8,128)(2,1)S(1)} %copy-done.16, bf16[2048,768]{1,0:T(8,128)(2,1)} %get-tuple-element.285.refs_1_, bf16[2048,768]{1,0:T(8,128)(2,1)} %get-tuple-element.286.refs_2_, bf16[4608,1024]{1,0:T(8,128)(2,1)} %refs_3_.3), custom_call_target="tpu_custom_call" | custom-call | flops 9663676416 | bytes 25165824 | tf_op jit(solution)/shard_map/feed_out_keep/pallas_call | solution.py:291
  315.0 6.3 %collective-permute-done.40 = bf16[576,512]{1,0:T(8,128)(2,1)S(1)} collective-permute-done((bf16[576,512]{1,0:T(8,128)(2,1)S(1)}, bf16[576,512]{1,0:T(8,128)(2,1)S(1)}, u32[]{:S(2)}, u32[]{:S(2)}) %collective-permute-start.40) | collective-permute-done | bytes 589856 | tf_op jit(solution)/shard_map/ppermute | solution.py:1049
  324.4 2.2 last_sums.1
  326.8 3.7 %add_convert_fusion = bf16[1024,1024]{1,0:T(8,128)(2,1)} fusion(f32[1024,1024]{1,0:T(8,128)S(1)} %copy-done.17, bf16[1024,1024]{1,0:T(8,128)(2,1)} %collective-permute-done.38, bf16[1024,1024]{1,0:T(8,128)(2,1)S(1)} %feed_out_keep.1, f32[1024]{0:T(1024)S(1)} %copy-done.45), kind=kLoop, calls=%fused_computation | loop fusion | flops 6291456 | bytes 10489856 | tf_op jit(solution)/shard_map/convert_element_type | solution.py:43
  334.1 2.4 collective-permute-done.43
  (277 shorter events, 84.3 us)
Async XLA Ops:
  10.7 20.2 %collective-permute-start.2 = (bf16[1024,1024]{1,0:T(8,128)(2,1)}, bf16[1024,1024]{1,0:T(8,128)(2,1)}, u32[]{:S(2)}, u32[]{:S(2)}) collective-permute-start(bf16[1024,1024]{1,0:T(8,128)(2,1)} %multiply_convert_fusion.own_grad_ref), channel_id=1, source_target_pairs={{0,1},{1,0},{2,3},{3,2},{4,5},{5,4},{6,7},{7,6},{8,9},{9,8},{10,11... | collective-permute-start | bytes 6291464 | tf_op jit(solution)/shard_map/ppermute | solution.py:35
  63.5 32.8 %collective-permute-start.3 = (bf16[2,2,2,128,384]{4,3,2,1,0:T(8,128)(2,1)}, bf16[2,2,2,128,384]{4,3,2,1,0:T(8,128)(2,1)S(1)}, u32[]{:S(2)}, u32[]{:S(2)}) collective-permute-start(bf16[2,2,2,128,384]{4,3,2,1,0:T(8,128)(2,1)} %get-tuple-element.182), channel_id=1, source_target_pairs={{0,8},{4,12},{8,0},{12,4},{16,24},{20,28},{24,16},{28,20},{1,9},{5... | collective-permute-start | bytes 2359304 | tf_op jit(solution)/shard_map/ppermute | solution.py:35
  65.1 31.1 %collective-permute-start.4 = (bf16[2,2,2,128,384]{4,3,2,1,0:T(8,128)(2,1)}, bf16[2,2,2,128,384]{4,3,2,1,0:T(8,128)(2,1)S(1)}, u32[]{:S(2)}, u32[]{:S(2)}) collective-permute-start(bf16[2,2,2,128,384]{4,3,2,1,0:T(8,128)(2,1)} %get-tuple-element.183), channel_id=1, source_target_pairs={{0,4},{4,0},{8,12},{12,8},{16,20},{20,16},{24,28},{28,24},{1,5},{5... | collective-permute-start | bytes 2359304 | tf_op jit(solution)/shard_map/ppermute | solution.py:35
  66.6 29.6 %collective-permute-start.5 = (bf16[2,384,512]{2,1,0:T(8,128)(2,1)}, bf16[2,384,512]{2,1,0:T(8,128)(2,1)S(1)}, u32[]{:S(2)}, u32[]{:S(2)}) collective-permute-start(bf16[2,384,512]{2,1,0:T(8,128)(2,1)} %get-tuple-element.184), channel_id=1, source_target_pairs={{0,2},{1,3},{2,0},{3,1},{4,6},{5,7},{6,4},{7,5},{8,10},{9,11},{10,... | collective-permute-start | bytes 2359304 | tf_op jit(solution)/shard_map/ppermute | solution.py:35
  97.3 34.0 %collective-permute-start.10 = (bf16[2,2,128,384]{3,2,1,0:T(8,128)(2,1)S(1)}, bf16[2,2,128,384]{3,2,1,0:T(8,128)(2,1)S(1)}, u32[]{:S(2)}, u32[]{:S(2)}) collective-permute-start(bf16[2,2,128,384]{3,2,1,0:T(8,128)(2,1)S(1)} %get-tuple-element.349), channel_id=1, source_target_pairs={{0,8},{4,12},{8,0},{12,4},{16,24},{20,28},{24,16},{28,20},{1,9},{5... | collective-permute-start | bytes 1179656 | tf_op jit(solution)/shard_map/ppermute | solution.py:35
  98.7 32.6 %collective-permute-start.9 = (bf16[2,2,128,384]{3,2,1,0:T(8,128)(2,1)S(1)}, bf16[2,2,128,384]{3,2,1,0:T(8,128)(2,1)S(1)}, u32[]{:S(2)}, u32[]{:S(2)}) collective-permute-start(bf16[2,2,128,384]{3,2,1,0:T(8,128)(2,1)S(1)} %get-tuple-element.351), channel_id=1, source_target_pairs={{0,4},{4,0},{8,12},{12,8},{16,20},{20,16},{24,28},{28,24},{1,5},{5... | collective-permute-start | bytes 1179656 | tf_op jit(solution)/shard_map/ppermute | solution.py:35
  99.4 31.9 %collective-permute-start.6 = (bf16[2,2,2,128,384]{4,3,2,1,0:T(8,128)(2,1)}, bf16[2,2,2,128,384]{4,3,2,1,0:T(8,128)(2,1)S(1)}, u32[]{:S(2)}, u32[]{:S(2)}) collective-permute-start(bf16[2,2,2,128,384]{4,3,2,1,0:T(8,128)(2,1)} %get-tuple-element.200), channel_id=1, source_target_pairs={{0,8},{4,12},{8,0},{12,4},{16,24},{20,28},{24,16},{28,20},{1,9},{5... | collective-permute-start | bytes 2359304 | tf_op jit(solution)/shard_map/ppermute | solution.py:35
  101.0 30.3 %collective-permute-start.7 = (bf16[2,2,2,128,384]{4,3,2,1,0:T(8,128)(2,1)S(1)}, bf16[2,2,2,128,384]{4,3,2,1,0:T(8,128)(2,1)S(1)}, u32[]{:S(2)}, u32[]{:S(2)}) collective-permute-start(bf16[2,2,2,128,384]{4,3,2,1,0:T(8,128)(2,1)S(1)} %copy-done.55), channel_id=1, source_target_pairs={{0,4},{4,0},{8,12},{12,8},{16,20},{20,16},{24,28},{28,24},{1,5},{5... | collective-permute-start | bytes 2359304 | tf_op jit(solution)/shard_map/ppermute | solution.py:35
  102.6 28.8 %collective-permute-start.8 = (bf16[2,384,512]{2,1,0:T(8,128)(2,1)S(1)}, bf16[2,384,512]{2,1,0:T(8,128)(2,1)S(1)}, u32[]{:S(2)}, u32[]{:S(2)}) collective-permute-start(bf16[2,384,512]{2,1,0:T(8,128)(2,1)S(1)} %copy-done.53), channel_id=1, source_target_pairs={{0,2},{1,3},{2,0},{3,1},{4,6},{5,7},{6,4},{7,5},{8,10},{9,11},{10,... | collective-permute-start | bytes 2359304 | tf_op jit(solution)/shard_map/ppermute | solution.py:35
  132.3 35.4 %collective-permute-start.15 = (bf16[2,2,128,384]{3,2,1,0:T(8,128)(2,1)S(1)}, bf16[2,2,128,384]{3,2,1,0:T(8,128)(2,1)S(1)}, u32[]{:S(2)}, u32[]{:S(2)}) collective-permute-start(bf16[2,2,128,384]{3,2,1,0:T(8,128)(2,1)S(1)} %get-tuple-element.345), channel_id=1, source_target_pairs={{0,8},{4,12},{8,0},{12,4},{16,24},{20,28},{24,16},{28,20},{1,9},{5... | collective-permute-start | bytes 1179656 | tf_op jit(solution)/shard_map/ppermute | solution.py:35
  133.8 33.9 %collective-permute-start.14 = (bf16[2,2,128,384]{3,2,1,0:T(8,128)(2,1)S(1)}, bf16[2,2,128,384]{3,2,1,0:T(8,128)(2,1)}, u32[]{:S(2)}, u32[]{:S(2)}) collective-permute-start(bf16[2,2,128,384]{3,2,1,0:T(8,128)(2,1)S(1)} %get-tuple-element.347), channel_id=1, source_target_pairs={{0,4},{4,0},{8,12},{12,8},{16,20},{20,16},{24,28},{28,24},{1,5},{5... | collective-permute-start | bytes 1179656 | tf_op jit(solution)/shard_map/ppermute | solution.py:35
  135.4 32.3 %collective-permute-start.11 = (bf16[2,2,2,128,384]{4,3,2,1,0:T(8,128)(2,1)S(1)}, bf16[2,2,2,128,384]{4,3,2,1,0:T(8,128)(2,1)}, u32[]{:S(2)}, u32[]{:S(2)}) collective-permute-start(bf16[2,2,2,128,384]{4,3,2,1,0:T(8,128)(2,1)S(1)} %copy-done.54), channel_id=1, source_target_pairs={{0,8},{4,12},{8,0},{12,4},{16,24},{20,28},{24,16},{28,20},{1,9},{5... | collective-permute-start | bytes 2359304 | tf_op jit(solution)/shard_map/ppermute | solution.py:35
  137.0 30.7 %collective-permute-start.12 = (bf16[2,2,2,128,384]{4,3,2,1,0:T(8,128)(2,1)S(1)}, bf16[2,2,2,128,384]{4,3,2,1,0:T(8,128)(2,1)}, u32[]{:S(2)}, u32[]{:S(2)}) collective-permute-start(bf16[2,2,2,128,384]{4,3,2,1,0:T(8,128)(2,1)S(1)} %copy-done.52), channel_id=1, source_target_pairs={{0,4},{4,0},{8,12},{12,8},{16,20},{20,16},{24,28},{28,24},{1,5},{5... | collective-permute-start | bytes 2359304 | tf_op jit(solution)/shard_map/ppermute | solution.py:35
  138.5 29.2 %collective-permute-start.13 = (bf16[2,384,512]{2,1,0:T(8,128)(2,1)S(1)}, bf16[2,384,512]{2,1,0:T(8,128)(2,1)}, u32[]{:S(2)}, u32[]{:S(2)}) collective-permute-start(bf16[2,384,512]{2,1,0:T(8,128)(2,1)S(1)} %copy-done.51), channel_id=1, source_target_pairs={{0,2},{1,3},{2,0},{3,1},{4,6},{5,7},{6,4},{7,5},{8,10},{9,11},{10,... | collective-permute-start | bytes 2359304 | tf_op jit(solution)/shard_map/ppermute | solution.py:35
  176.0 19.1 %collective-permute-start.18 = (bf16[2,2,128,384]{3,2,1,0:T(8,128)(2,1)}, bf16[2,2,128,384]{3,2,1,0:T(8,128)(2,1)}, u32[]{:S(2)}, u32[]{:S(2)}) collective-permute-start(bf16[2,2,128,384]{3,2,1,0:T(8,128)(2,1)} %get-tuple-element.340), channel_id=1, source_target_pairs={{0,8},{4,12},{8,0},{12,4},{16,24},{20,28},{24,16},{28,20},{1,9},{5... | collective-permute-start | bytes 1179656 | tf_op jit(solution)/shard_map/ppermute | solution.py:35
  178.7 16.5 %collective-permute-start.17 = (bf16[2,2,128,384]{3,2,1,0:T(8,128)(2,1)}, bf16[2,2,128,384]{3,2,1,0:T(8,128)(2,1)}, u32[]{:S(2)}, u32[]{:S(2)}) collective-permute-start(bf16[2,2,128,384]{3,2,1,0:T(8,128)(2,1)} %get-tuple-element.342), channel_id=1, source_target_pairs={{0,4},{4,0},{8,12},{12,8},{16,20},{20,16},{24,28},{28,24},{1,5},{5... | collective-permute-start | bytes 1179656 | tf_op jit(solution)/shard_map/ppermute | solution.py:35
  179.2 28.0 %collective-permute-start.20 = (bf16[4,2,128,384]{3,2,0,1:T(8,128)(2,1)}, bf16[4,2,128,384]{3,2,0,1:T(8,128)(2,1)}, u32[]{:S(2)}, u32[]{:S(2)}) collective-permute-start(bf16[4,2,128,384]{3,2,0,1:T(8,128)(2,1)} %copy.77), channel_id=1, source_target_pairs={{0,2},{1,3},{2,0},{3,1},{4,6},{5,7},{6,4},{7,5},{8,10},{9,11},{10,... | collective-permute-start | bytes 2359304 | tf_op jit(solution)/shard_map/ppermute | solution.py:35
  207.2 28.9 %collective-permute-start.21 = (bf16[2,8,128,256]{3,2,1,0:T(8,128)(2,1)}, bf16[2,8,128,256]{3,2,1,0:T(8,128)(2,1)}, u32[]{:S(2)}, u32[]{:S(2)}) collective-permute-start(bf16[2,8,128,256]{3,2,1,0:T(8,128)(2,1)} %get-tuple-element.263), channel_id=1, source_target_pairs={{0,1},{1,0},{2,3},{3,2},{4,5},{5,4},{6,7},{7,6},{8,9},{9,8},{10,11... | collective-permute-start | bytes 3145736 | tf_op jit(solution)/shard_map/ppermute | solution.py:35
  208.1 26.2 %collective-permute-start.22 = (bf16[2,2,128,384]{3,2,0,1:T(8,128)(2,1)}, bf16[2,2,128,384]{3,2,0,1:T(8,128)(2,1)}, u32[]{:S(2)}, u32[]{:S(2)}) collective-permute-start(bf16[2,2,128,384]{3,2,0,1:T(8,128)(2,1)} %copy.81), channel_id=1, source_target_pairs={{0,2},{1,3},{2,0},{3,1},{4,6},{5,7},{6,4},{7,5},{8,10},{9,11},{10,... | collective-permute-start | bytes 1179656 | tf_op jit(solution)/shard_map/ppermute | solution.py:35
  210.6 25.4 %collective-permute-start.23 = (bf16[576,512]{1,0:T(8,128)(2,1)}, bf16[576,512]{1,0:T(8,128)(2,1)S(1)}, u32[]{:S(2)}, u32[]{:S(2)}) collective-permute-start(bf16[576,512]{1,0:T(8,128)(2,1)} %get-tuple-element.355), channel_id=1, source_target_pairs={{0,4},{4,0},{8,12},{12,8},{16,20},{20,16},{24,28},{28,24},{1,5},{5... | collective-permute-start | bytes 1769480 | tf_op jit(solution)/shard_map/ppermute | solution.py:35
  215.5 20.6 %collective-permute-start.24 = (bf16[4,128,384]{2,1,0:T(8,128)(2,1)}, bf16[4,128,384]{2,1,0:T(8,128)(2,1)}, u32[]{:S(2)}, u32[]{:S(2)}) collective-permute-start(bf16[4,128,384]{2,1,0:T(8,128)(2,1)} %get-tuple-element.339), channel_id=1, source_target_pairs={{0,16},{4,20},{8,24},{12,28},{16,0},{20,4},{24,8},{28,12},{1,17},{... | collective-permute-start | bytes 1179656 | tf_op jit(solution)/shard_map/ppermute | solution.py:35
  236.1 17.3 %collective-permute-start.25 = (bf16[2,8,128,768]{3,2,1,0:T(8,128)(2,1)S(1)}, bf16[2,8,128,768]{3,2,1,0:T(8,128)(2,1)S(1)}, u32[]{:S(2)}, u32[]{:S(2)}) collective-permute-start(bf16[2,8,128,768]{3,2,1,0:T(8,128)(2,1)S(1)} %in_grads_give.1), channel_id=1, source_target_pairs={{0,1},{1,0},{2,3},{3,2},{4,5},{5,4},{6,7},{7,6},{8,9},{9,8},{10,11... | collective-permute-start | bytes 9437192 | tf_op jit(solution)/shard_map/ppermute | solution.py:35
  237.6 15.8 %collective-permute-start.27 = (bf16[576,512]{1,0:T(8,128)(2,1)S(1)}, bf16[576,512]{1,0:T(8,128)(2,1)S(1)}, u32[]{:S(2)}, u32[]{:S(2)}) collective-permute-start(bf16[576,512]{1,0:T(8,128)(2,1)S(1)} %copy-done.31), channel_id=1, source_target_pairs={{0,4},{4,0},{8,12},{12,8},{16,20},{20,16},{24,28},{28,24},{1,5},{5... | collective-permute-start | bytes 1769480 | tf_op jit(solution)/shard_map/ppermute | solution.py:35
  256.4 15.3 %collective-permute-start.31 = (bf16[288,512]{1,0:T(8,128)(2,1)S(1)}, bf16[288,512]{1,0:T(8,128)(2,1)S(1)}, u32[]{:S(2)}, u32[]{:S(2)}) collective-permute-start(bf16[288,512]{1,0:T(8,128)(2,1)S(1)} %slice.343), channel_id=1, source_target_pairs={{0,16},{4,20},{8,24},{12,28},{16,0},{20,4},{24,8},{28,12},{1,17},{... | collective-permute-start | bytes 884744 | tf_op jit(solution)/shard_map/ppermute | solution.py:35
  256.7 18.6 %collective-permute-start.30 = (bf16[2,4,128,384]{3,2,1,0:T(8,128)(2,1)S(1)}, bf16[2,4,128,384]{3,2,1,0:T(8,128)(2,1)S(1)}, u32[]{:S(2)}, u32[]{:S(2)}) collective-permute-start(bf16[2,4,128,384]{3,2,1,0:T(8,128)(2,1)S(1)} %fusion.3), channel_id=1, source_target_pairs={{0,4},{4,0},{8,12},{12,8},{16,20},{20,16},{24,28},{28,24},{1,5},{5... | collective-permute-start | bytes 2359304 | tf_op jit(solution)/shard_map/ppermute | solution.py:35
  257.6 18.8 %collective-permute-start.29 = (bf16[8,128,384]{2,1,0:T(8,128)(2,1)S(1)}, bf16[8,128,384]{2,1,0:T(8,128)(2,1)S(1)}, u32[]{:S(2)}, u32[]{:S(2)}) collective-permute-start(bf16[8,128,384]{2,1,0:T(8,128)(2,1)S(1)} %get-tuple-element.329), channel_id=1, source_target_pairs={{0,2},{1,3},{2,0},{3,1},{4,6},{5,7},{6,4},{7,5},{8,10},{9,11},{10,... | collective-permute-start | bytes 2359304 | tf_op jit(solution)/shard_map/ppermute | solution.py:35
  277.4 20.3 %collective-permute-start.33 = (bf16[4,128,384]{2,1,0:T(8,128)(2,1)S(1)}, bf16[4,128,384]{2,1,0:T(8,128)(2,1)S(1)}, u32[]{:S(2)}, u32[]{:S(2)}) collective-permute-start(bf16[4,128,384]{2,1,0:T(8,128)(2,1)S(1)} %get-tuple-element.334), channel_id=1, source_target_pairs={{0,2},{1,3},{2,0},{3,1},{4,6},{5,7},{6,4},{7,5},{8,10},{9,11},{10,... | collective-permute-start | bytes 1179656 | tf_op jit(solution)/shard_map/ppermute | solution.py:35
  279.1 18.6 %collective-permute-start.32 = (bf16[4,128,384]{2,1,0:T(8,128)(2,1)S(1)}, bf16[4,128,384]{2,1,0:T(8,128)(2,1)}, u32[]{:S(2)}, u32[]{:S(2)}) collective-permute-start(bf16[4,128,384]{2,1,0:T(8,128)(2,1)S(1)} %get-tuple-element.336), channel_id=1, source_target_pairs={{0,4},{4,0},{8,12},{12,8},{16,20},{20,16},{24,28},{28,24},{1,5},{5... | collective-permute-start | bytes 1179656 | tf_op jit(solution)/shard_map/ppermute | solution.py:35
  281.2 16.5 %collective-permute-start.36 = (bf16[288,512]{1,0:T(8,128)(2,1)S(1)}, bf16[288,512]{1,0:T(8,128)(2,1)}, u32[]{:S(2)}, u32[]{:S(2)}) collective-permute-start(bf16[288,512]{1,0:T(8,128)(2,1)S(1)} %slice.317), channel_id=1, source_target_pairs={{0,16},{4,20},{8,24},{12,28},{16,0},{20,4},{24,8},{28,12},{1,17},{... | collective-permute-start | bytes 884744 | tf_op jit(solution)/shard_map/ppermute | solution.py:35
  297.7 23.6 %collective-permute-start.38 = (bf16[1024,1024]{1,0:T(8,128)(2,1)S(1)}, bf16[1024,1024]{1,0:T(8,128)(2,1)}, u32[]{:S(2)}, u32[]{:S(2)}) collective-permute-start(bf16[1024,1024]{1,0:T(8,128)(2,1)S(1)} %feed_out_give.1), channel_id=1, source_target_pairs={{0,1},{1,0},{2,3},{3,2},{4,5},{5,4},{6,7},{7,6},{8,9},{9,8},{10,11... | collective-permute-start | bytes 6291464 | tf_op jit(solution)/shard_map/ppermute | solution.py:35
  304.2 17.1 %collective-permute-start.40 = (bf16[576,512]{1,0:T(8,128)(2,1)S(1)}, bf16[576,512]{1,0:T(8,128)(2,1)S(1)}, u32[]{:S(2)}, u32[]{:S(2)}) collective-permute-start(bf16[576,512]{1,0:T(8,128)(2,1)S(1)} %add_convert_fusion.8), channel_id=1, source_target_pairs={{1,9},{3,11},{5,13},{7,15},{8,0},{10,2},{12,4},{14,6},{17,25},{19,... | collective-permute-start | bytes 1769480 | tf_op jit(solution)/shard_map/ppermute | solution.py:1049
  322.8 14.8 %collective-permute-start.44 = (bf16[128,1024]{1,0:T(8,128)(2,1)S(1)}, bf16[128,1024]{1,0:T(8,128)(2,1)S(1)}, u32[]{:S(2)}, u32[]{:S(2)}) collective-permute-start(bf16[128,1024]{1,0:T(8,128)(2,1)S(1)} %fusion.27), channel_id=1, source_target_pairs={{0,16},{4,20},{8,24},{12,28},{16,0},{20,4},{24,8},{28,12},{1,17},{... | collective-permute-start | bytes 786440 | tf_op jit(solution)/shard_map/ppermute | solution.py:35
  (72 other events, 476.5 us)

commit v5 on v4

--- a/solution.py
+++ b/solution.py
@@ -495,7 +495,7 @@
         compiler_params=pltpu.CompilerParams(vmem_limit_bytes=32 << 20),
         cost_estimate=pl.CostEstimate(flops=10 * tokens * width, bytes_accessed=16 << 20, transcendentals=0),
         name="project_grads",
-    )(marks, conv_grad, after, gate, value, open_grad, scales)
+    )(marks, *far(conv_grad, after, gate, value, open_grad), scales)
 
 
 def pair_grads(place, left, right, cores, name):
@@ -766,31 +766,28 @@
 
 def joined(keeps, takes, name):
     count = len(keeps)
-    shape = (count,) + keeps[0].shape[1:]
+    shape = (keeps[0].shape[1], count) + keeps[0].shape[2:]
 
     def kernel(*refs):
         for n in range(count):
             for side in range(2):
-                refs[2 * count + side][n] = narrow(wide(refs[n][side], refs[count + n][side]))
-
-    def spec(first):
-        return pl.BlockSpec((first, 1) + shape[2:], lambda i: (0, i, 0, 0))
+                refs[2 * count + side][0, n] = narrow(wide(refs[n][side, 0], refs[count + n][side, 0]))
 
     return pl.pallas_call(
         kernel,
-        grid=(shape[1],),
-        in_specs=[spec(2)] * (2 * count),
-        out_specs=[spec(count)] * 2,
+        grid=(shape[0],),
+        in_specs=[pl.BlockSpec((2, 1) + shape[2:], lambda i: (0, i, 0, 0))] * (2 * count),
+        out_specs=[pl.BlockSpec((1,) + shape[1:], lambda i: (i, 0, 0, 0))] * 2,
         out_shape=[pltpu.HBM(shape, LOW)] * 2,
         compiler_params=pltpu.CompilerParams(vmem_limit_bytes=32 << 20),
         name=name,
     )(*far(*keeps, *takes))
 
 
-def side_by_side(keeps, takes):
+def side_by_side(keeps, takes, name):
     count = len(keeps)
     widths = [keep.shape[-1] for keep in keeps]
-    shape = (2, keeps[0].shape[-2], sum(widths))
+    shape = (keeps[0].shape[0] // 2, keeps[0].shape[-2], sum(widths))
 
     def kernel(*refs):
         for n in range(count):
@@ -803,12 +800,12 @@
 
     return pl.pallas_call(
         kernel,
-        grid=(2,),
+        grid=(shape[0],),
         in_specs=[spec(2, size) for size in widths] * 2,
         out_specs=[spec(1, shape[2])] * 2,
         out_shape=[pltpu.HBM(shape, LOW)] * 2,
         compiler_params=pltpu.CompilerParams(vmem_limit_bytes=32 << 20),
-        name="side_by_side",
+        name=name,
     )(*far(*keeps, *takes))
 
 
@@ -966,11 +963,12 @@
         third_take,
         down_give,
     )
+    after = jnp.pad(after, ((0, 0), (0, 6), (0, 0))).reshape(row_count * 8, model_width)
+    fourth_give, fourth_keep = split(third_keep, third_take, 0)
+    fourth_take = swapped(fourth_give, "seq", 4)
+    down_give, out_give = follow((down_give, out_give), fourth_give)
     down_takes = [swapped(down_give[0], "seq", 1)]
     out_take = swapped(out_give, "row", 1)
-    after = jnp.pad(after, ((0, 0), (0, 6), (0, 0))).reshape(row_count * 8, model_width)
-    fourth_give, fourth_keep = split(third_keep, third_take, 1)
-    fourth_take = swapped(fourth_give, "seq", 4)
 
     project_grad = project_grads(
         follow(marks, out_keep, fourth_give, fourth_keep), conv_grad, after, input_gate, values, open_grad, scales
@@ -982,17 +980,17 @@
     out_give, out_keep = split(out_keep, out_take, 0)
     out_take = swapped(out_give, "row", 2)
     down_takes.append(swapped(follow(down_give[1], out_give), "seq", 1))
-    late_give, late_keep = split(late_keep, late_take, 1)
-    late_take = swapped(late_give, "seq", 4)
-
-    (in_keep,), in_take, out_take, down_takes, late_take = together(
+    late_give, late_keep = split(late_keep, late_take, 0)
+    down_first = narrow(wide(down_keep[0], down_takes[0]))
+    down_take = swapped(down_first, "seq", 4)
+
+    (in_keep,), in_take, out_take, down_takes = together(
         pair_grads(
-            follow(place, in_give, out_give, out_keep, late_give, late_keep), normed, project_grad, (1,), "in_grads_keep"
+            follow(place, in_give, out_give, out_keep, late_give, late_keep, down_first), normed, project_grad, (1,), "in_grads_keep"
         ),
         in_take,
         out_take,
         down_takes,
-        late_take,
     )
     half = in_keep.shape[-1] // 2
     left_give, left_keep = split(in_keep[..., :half], in_take[..., :half], 0)
@@ -1000,72 +998,48 @@
     eighths = (2, 4, 2, model_width // 8, half)
     right_give, right_keep = split(in_keep[..., half:].reshape(eighths), in_take[..., half:].reshape(eighths), 2)
     right_take = swapped(right_give, "seq", 1)
-    eighths = (4, 2, model_width // 8, out_keep.shape[-1])
-    out_give, out_keep = split(out_keep.reshape(eighths), out_take.reshape(eighths), 1)
-    down_give, down_keep = (narrow(wide(down_keep[i], down_takes[i])) for i in range(2))
-    quarter = down_give.shape[0] // 2
-    down_takes = [swapped(down_give[:quarter], "seq", 4)]
-
-    (input_grad, small), left_take, right_take, down_takes, out_give, down_give = together(
+    down_keep = narrow(wide(down_keep[1], down_takes[1]))
+
+    (input_grad, small), left_take, right_take, down_take = together(
         mixer_backward(
-            follow(
-                project_grad, left_give, left_keep, right_give, right_keep, out_give, out_keep, down_give, down_keep,
-            ),
+            follow(project_grad, left_give, left_keep, right_give, right_keep, down_keep),
             in_weight, hidden, residual_grad, sums, scales,
         ),
         left_take,
         right_take,
-        down_takes,
-        out_give,
-        down_give,
-    )
-    eighths = (4, 2, model_width // 8, half)
-    left_give, left_keep = split(left_keep.reshape(eighths), left_take.reshape(eighths), 1)
+        down_take,
+    )
+    left_give, left_keep = side_by_side([left_keep, out_keep], [left_take, out_take], "y_sums")
     left_take = swapped(left_give, "seq", 1)
-    right_give, right_keep = split(right_keep, right_take, 0)
+    right_give, right_keep = split(right_keep, follow(right_take, left_give), 0)
     right_take = swapped(right_give, "row", 2)
     small_take = swapped(small, "row", 1)
-    down_takes.append(swapped(down_give[quarter:], "seq", 4))
-    out_take = swapped(follow(out_give, left_give), "seq", 1)
-
-    (give_feed,), left_take, right_take, out_take, small_take, down_takes = together(
-        feed_sum(
-            follow(place, left_give, left_keep, right_give, right_keep),
-            [acts], [down_weight], False, block, "feed_out_give", (1,),
-        ),
-        left_take,
-        right_take,
-        out_take,
-        small_take,
-        down_takes,
-    )
-    give, keep = side_by_side([left_keep, right_keep, out_keep], [left_take, right_take, out_take])
-    take = swapped(give, "seq", 2)
-    take_feed = swapped(give_feed, "row", 1)
-    small = small + small_take
-    small_take = swapped(small, "row", 2)
-    down = narrow(wide(down_keep, jnp.concatenate(follow(down_takes, give))))
+    down = narrow(wide(down_keep, follow(down_take, left_give)))
     holder = [[(r & 1) == ((s >> 1) & 1) for r in range(4)] for s in range(8)]
     down_take = lax.ppermute(
         down,
         ("seq", "row"),
         [(s * 4 + r, (s ^ 2) * 4 + r) for s in range(8) for r in range(4) if not holder[s][r]],
     )
-
-    (own_feed,), take, take_feed, small_take, down_take = together(
+    late_take = swapped(follow(late_give, down), "seq", 4)
+
+    (give_feed,), left_take, right_take, small_take, down_take, late_take = together(
         feed_sum(
-            follow(place, give, keep, small, down), [acts], [down_weight], False, block, "feed_out_keep", (0,)
+            follow(place, left_give, left_keep, right_give, right_keep, down),
+            [acts], [down_weight], False, block, "feed_out_give", (1,),
         ),
-        take,
-        take_feed,
+        left_take,
+        right_take,
         small_take,
         down_take,
-    )
-    give, keep = split(keep, take, 0)
-    take = swapped(give, "seq", 4)
+        late_take,
+    )
+    give, keep = side_by_side([left_keep, right_keep], [left_take, right_take], "z_sums")
+    take = swapped(give, "seq", 2)
+    take_feed = swapped(give_feed, "row", 1)
     small = small + small_take
-    small_take = swapped(small, "seq", 1)
-    down = wide(down, down_take)
+    small_take = swapped(small, "row", 2)
+    down = wide(down, follow(down_take, give))
     quarter = model_width // 4
     down_own = jnp.where(core == 0, down[:, :quarter], down[:, quarter:])
     down_other = narrow(jnp.where(core == 0, down[:, quarter:], down[:, :quarter]))
@@ -1074,6 +1048,20 @@
         ("seq", "row"),
         [(s * 4 + r, s * 4 + (r ^ 1)) for s in range(8) for r in range(4) if holder[s][r]],
     )
+
+    (own_feed,), take, take_feed, small_take, down_other = together(
+        feed_sum(
+            follow(place, give, keep, small, down_own), [acts], [down_weight], False, block, "feed_out_keep", (0,)
+        ),
+        take,
+        take_feed,
+        small_take,
+        down_other,
+    )
+    give, keep = split(keep, take, 0)
+    take = swapped(give, "seq", 4)
+    small = small + small_take
+    small_take = swapped(small, "seq", 1)
     (gate_part, up_part), small_take = together(
         last_sums(*follow(([fourth_keep, late_keep], [fourth_take, late_take]), give)), small_take
     )
@@ -1087,7 +1075,9 @@
     down_part = jnp.where(core == seq_z0, down_own, down_other.astype(jnp.float32))
     input_grad = input_grad.reshape(row_count, span_length, model_width)
     both_part = wide(keep, take)
-    in_part, out_part = both_part[:, : 2 * half], both_part[:, 2 * half :]
+    past = both_part.shape[1] - half
+    in_part = jnp.concatenate([both_part[:, :half], both_part[:, past:]], axis=1)
+    out_part = both_part[:, half:past]
     small = small + small_take
     small = lax.dynamic_slice_in_dim(small, seq * (model_width // 8), model_width // 8, 1)
     return (

time: 345 us -> 336 us (0.974)
  local copies, waits for them, and re-layouts: 22.2 us -> 13.1 us
  waiting for transfers between devices: 30.8 us -> 23.5 us
  Pallas kernels: 203 us -> 209 us
    unnamed x126 -> x120, local copies, waits for them, and re-layouts: 12.2 us -> 5.49 us
    ppermute x1, waiting for transfers between devices: 6.32 us -> 0.48 us  [fast(): lax.ppermute(down, ('seq', 'row'), [(s * 4 + r, (s ^ 2) * 4 + r) for s in...]
    pallas_call x3 -> x4, Pallas kernels: 9.02 us -> 12.5 us  [the longest x2 6.32 us: side_by_side(): pl.pallas_call(kernel, grid=(shape[0],), in_specs=[spec(2, size) for size...]
    ppermute x42 -> x40, starting transfers between devices: 40.5 us -> 42 us  [swapped(): return lax.ppermute(value, axis, [(i, i ^ bit) for i in range(length)])]
    ppermute x42 -> x40, waiting for transfers between devices: 24.5 us -> 23 us  [swapped(): return lax.ppermute(value, axis, [(i, i ^ bit) for i in range(length)])]
    convert_element_type x24 -> x23, other arithmetic: 29.7 us -> 28.8 us  [narrow(): return value.astype(jnp.bfloat16)]
  transfers between devices with their start and end apart: 46 -> 44, of which waited for: 13 -> 10; matrix products, arithmetic and copies ran while one was open for 11% -> 10% of each run, Pallas kernels for 51% -> 54%
where the time goes in v5:
time: 336 us; the launch traced here: 332 us
  Pallas kernels  209 us (62%)
  starting transfers between devices  51.1 us (15%)
  other arithmetic  32.7 us (10%)
  waiting for transfers between devices  23.5 us (7%)
  local copies, waits for them, and re-layouts  13.1 us (4%)
    pallas_call x3, Pallas kernels, feed_chunk(): pl.pallas_call(kernel, out_shape=[jax.ShapeDtypeStruct((both, span), low)...  84.1 us
    pallas_call x3, Pallas kernels, feed_sum(): pl.pallas_call(kernel, out_shape=[jax.ShapeDtypeStruct((tokens, width), l...  46.1 us
    ppermute x40, starting transfers between devices, swapped(): return lax.ppermute(value, axis, [(i, i ^ bit) for i in range(length)])  42 us
    convert_element_type x23, other arithmetic, narrow(): return value.astype(jnp.bfloat16)  28.8 us
    ppermute x40, waiting for transfers between devices, swapped(): return lax.ppermute(value, axis, [(i, i ^ bit) for i in range(length)])  23 us
    pallas_call x3, Pallas kernels, pair_grads(): pl.pallas_call(kernel, grid_spec=pltpu.PrefetchScalarGridSpec(num_scalar_...  19.8 us
    pallas_call x1, Pallas kernels, mixer_forward(): pl.pallas_call(kernel, grid=(steps,), in_specs=[rows(8), rows(width), row...  16.3 us
    pallas_call x1, Pallas kernels, mixer_middle(): pl.pallas_call(kernel, grid=(steps,), in_specs=[rows(8)] + [rows(width)]...  13 us
  transfers between devices with their start and end apart: 44, of which 10 were waited for; matrix products, arithmetic and copies ran while one was open for 10% of the time, Pallas kernels for 54%

profile of v5, /device:TPU:0, one launch (start us, length us, event | category | flops | bytes accessed | tf_op | source)
XLA Modules:
  0.0 331.8 jit_solution(15393193356984413650)
XLA Ops:
  1.4 4.9 %collective-permute-start = (bf16[2,2,1024]{2,1,0:T(2,128)(2,1)S(1)}, bf16[2,2,1024]{2,1,0:T(2,128)(2,1)S(1)}, u32[]{:S(2)}, u32[]{:S(2)}) collective-permute-start(bf16[2,2,1024]{2,1,0:T(2,128)(2,1)S(1)} %slice.223), channel_id=1, source_target_pairs={{0,4},{4,8},{8,12},{12,16},{16,20},{20,24},{24,28},{1,5},{5,9},{9,... | collective-permute-start | bytes 24584 | tf_op jit(solution)/shard_map/ppermute | solution.py:14
  7.2 3.5 %multiply_convert_fusion.own_grad_ref = bf16[1024,1024]{1,0:T(8,128)(2,1)} fusion(f32[1024]{0:T(1024)S(1)} %compare_convert_fusion.1, bf16[2,512,1024]{2,1,0:T(8,128)(2,1)} %param.23), kind=kLoop, calls=%fused_computation.1 | loop fusion | flops 3145728 | bytes 4198400 | tf_op jit(solution)/shard_map/convert_element_type | solution.py:43
  13.3 16.3 %mixer_forward.1 = (bf16[1024,1024]{1,0:T(8,128)(2,1)}, bf16[1024,1024]{1,0:T(8,128)(2,1)}, bf16[1024,1024]{1,0:T(8,128)(2,1)}, bf16[1024,1024]{1,0:T(8,128)(2,1...) custom-call(f32[1024,8]{1,0:T(8,128)S(1)} %copy.41.marks_ref, ...), custom_call_target="tpu_custom_call" | custom-call | flops 8589934592 | bytes 29360128 | tf_op jit(solution)/shard_map/mixer_forward/pallas_call | solution.py:378
  30.9 3.4 %collective-permute-done.1.other_ref = bf16[1024,1024]{1,0:T(8,128)(2,1)S(1)} collective-permute-done((bf16[1024,1024]{1,0:T(8,128)(2,1)}, bf16[1024,1024]{1,0:T(8,128)(2,1)S(1)}, u32[]{:S(2)}, u32[]{:S(2)}) %collective-permute-start.1) | collective-permute-done | bytes 2097184 | tf_op jit(solution)/shard_map/ppermute | solution.py:35
  35.6 27.9 %feed_0.1 = (bf16[2048,768]{1,0:T(8,128)(2,1)}, bf16[2048,768]{1,0:T(8,128)(2,1)}, bf16[2048,768]{1,0:T(8,128)(2,1)}, bf16[2,2,2,128,384]{4,3,2,1,0:T(8,128)(2,1...) custom-call(s32[18]{0:T(128)} %stack.82.place_ref, ...), custom_call_target="tpu_custom_call" | custom-call | flops 19327352832 | bytes 25165824 | tf_op jit(solution)/shard_map/feed_0/pallas_call | solution.py:176
  68.2 28.1 %feed_1.1 = (bf16[2048,768]{1,0:T(8,128)(2,1)}, bf16[2048,768]{1,0:T(8,128)(2,1)}, bf16[2048,768]{1,0:T(8,128)(2,1)}, bf16[2,2,2,128,384]{4,3,2,1,0:T(8,128)(2,1...) custom-call(s32[18]{0:T(128)} %stack.82.place_ref, ...), custom_call_target="tpu_custom_call" | custom-call | flops 19327352832 | bytes 25165824 | tf_op jit(solution)/shard_map/feed_1/pallas_call | solution.py:176
  103.1 28.1 %feed_2.1 = (bf16[2048,768]{1,0:T(8,128)(2,1)}, bf16[2048,768]{1,0:T(8,128)(2,1)}, bf16[2048,768]{1,0:T(8,128)(2,1)}, bf16[2,2,2,128,384]{4,3,2,1,0:T(8,128)(2,1...) custom-call(s32[18]{0:T(128)} %stack.82.place_ref, ...), custom_call_target="tpu_custom_call" | custom-call | flops 19327352832 | bytes 25165824 | tf_op jit(solution)/shard_map/feed_2/pallas_call | solution.py:176
  139.9 27.7 %normed_two_grad.1 = (bf16[1024,1024]{1,0:T(8,128)(2,1)S(1)}, bf16[1024,1024]{1,0:T(8,128)(2,1)}) custom-call(s32[18]{0:T(128)S(1)} %copy-done.3, bf16[2048,768]{1,0:T(8,128)(2,1)} %get-tuple-element.211.refs_0_, bf16[2048,768]{1,0:T(8,128)(2,1)} %get-tuple-element.212.refs_1_, bf16[2048,768]{1,0:T(8,128)(2,1)} %get-tuple-element.213.refs_2_, ...), custom_call_target="tpu_custom_call" | custom-call | flops 19327352832 | bytes 25165824 | tf_op jit(solution)/shard_map/normed_two_grad/pallas_call | solution.py:291
  167.8 2.5 fusion.20
  170.8 2.2 fusion.19
  173.6 3.0 third_sums.1
  177.2 2.2 add_convert_fusion.5
  179.6 13.0 %mixer_middle.1 = (f32[1024,1024]{1,0:T(8,128)}, bf16[1024,1024]{1,0:T(8,128)(2,1)S(1)}, bf16[1024,1024]{1,0:T(8,128)(2,1)S(1)}, f32[1024,1024]{1,0:T(8,128)}, f32[8,1024]{1,0:T(8,128)S(1)}) custom-call(f32[1024,8]{1,0:T(8,128)S(1)} %copy.42.marks_ref, bf16[1024,1024]{1,0:T(8,128)(2,1)S(1)} %get-tuple-element.233.own_ref, ...), custom_call_target="tpu_custom_call" | custom-call | flops 2147483648 | bytes 33554432 | tf_op jit(solution)/shard_map/mixer_middle/pallas_call | solution.py:444
  192.6 3.1 late_sums.1
  199.4 4.4 %out_grads.1 = (bf16[2,8,128,256]{3,2,1,0:T(8,128)(2,1)S(1)}, bf16[2,8,128,256]{3,2,1,0:T(8,128)(2,1)S(1)}) custom-call(s32[18]{0:T(128)S(1)} %copy-done.3, bf16[1024,1024]{1,0:T(8,128)(2,1)S(1)} %copy-done.8, bf16[1024,1024]{1,0:T(8,128)(2,1)S(1)} %get-tuple-element.246.right_ref), custom_call_target="tpu_custom_call" | custom-call | flops 2147483648 | bytes 8388608 | tf_op jit(solution)/shard_map/out_grads/pallas_call | solution.py:526
  207.2 2.6 collective-permute-start.23
  211.3 2.6 collective-permute-start.24
  215.5 5.9 %project_grads.1.right_ref.grad_ref = bf16[1024,3072]{1,0:T(8,128)(2,1)S(1)} custom-call(f32[1024,8]{1,0:T(8,128)S(1)} %copy.43.marks_ref, f32[1024,1024]{1,0:T(8,128)} %get-tuple-element.254.conv_ref, f32[16,1024]{1,0:T(8,128)} %pad_bitcast_fusion.after_ref, bf16[1024,1024]{1,0:T(8,128)(2,1)} %get-tuple-element.260.gate_ref, ...), custom_call_target="tpu_custom_call" | custom-call | flops 10485760 | bytes 16777216 | tf_op jit(solution)/shard_map/project_grads/pallas_call | solution.py:488
  221.4 7.7 %in_grads_give.1 = bf16[2,8,128,768]{3,2,1,0:T(8,128)(2,1)S(1)} custom-call(s32[18]{0:T(128)S(1)} %copy-done.3, bf16[1024,1024]{1,0:T(8,128)(2,1)S(1)} %copy-done.7, bf16[1024,3072]{1,0:T(8,128)(2,1)S(1)} %project_grads.1.right_ref.grad_ref), custom_call_target="tpu_custom_call" | custom-call | flops 3221225472 | bytes 8388608 | tf_op jit(solution)/shard_map/in_grads_give/pallas_call | solution.py:526
  229.1 2.8 collective-permute-done.24.refs_2_
  231.9 2.3 fusion.8
  238.2 7.7 %in_grads_keep.1 = bf16[2,8,128,768]{3,2,1,0:T(8,128)(2,1)S(1)} custom-call(s32[18]{0:T(128)S(1)} %copy-done.3, bf16[1024,1024]{1,0:T(8,128)(2,1)S(1)} %copy-done.7, bf16[1024,3072]{1,0:T(8,128)(2,1)S(1)} %project_grads.1.right_ref.grad_ref), custom_call_target="tpu_custom_call" | custom-call | flops 3221225472 | bytes 8388608 | tf_op jit(solution)/shard_map/in_grads_keep/pallas_call | solution.py:526
  245.9 2.7 collective-permute-done.26.refs_3_
  255.5 9.5 %mixer_backward.1 = (bf16[1024,1024]{1,0:T(8,128)(2,1)}, f32[8,1024]{1,0:T(8,128)S(1)}) custom-call(bf16[1024,3072]{1,0:T(8,128)(2,1)S(1)} %project_grads.1.right_ref.grad_ref, bf16[1024,3072]{1,0:T(8,128)(2,1)S(1)} %bitcast.168, bf16[1024,1024]{1,0:T(8,128)(2,1)S(1)} %bitcast.166, f32[1024,1024]{1,0:T(8,128)S(1)} %copy-done.6, ...), custom_call_target="tpu_custom_call" | custom-call | flops 6442450944 | bytes 20971520 | tf_op jit(solution)/shard_map/mixer_backward/pallas_call | solution.py:568
  265.1 6.2 %collective-permute-done.29 = bf16[2,4,128,384]{3,2,1,0:T(8,128)(2,1)S(1)} collective-permute-done((bf16[2,4,128,384]{3,2,1,0:T(8,128)(2,1)S(1)}, bf16[2,4,128,384]{3,2,1,0:T(8,128)(2,1)S(1)}, u32[]{:S(2)}, u32[]{:S(2)}) %collective-permute-start.29) | collective-permute-done | bytes 786464 | tf_op jit(solution)/shard_map/ppermute | solution.py:35
  273.2 3.9 %y_sums.1 = (bf16[4,128,640]{2,1,0:T(8,128)(2,1)}, bf16[4,128,640]{2,1,0:T(8,128)(2,1)}) custom-call(bf16[8,128,384]{2,1,0:T(8,128)(2,1)} %get-tuple-element.329.refs_0_, bf16[8,128,256]{2,1,0:T(8,128)(2,1)} %get-tuple-element.332.refs_1_, bf16[8,128,384]{2,1,0:T(8,128)(2,1)} %copy-done.24, bf16[8,128,256]{2,1,0:T(8,128)(2,1)} %copy-done.30), custom_call_target="tpu_custom_call" | custom-call | tf_op jit(solution)/shard_map/y_sums/pallas_call | solution.py:801
  284.1 8.9 %feed_out_give.1 = bf16[1024,1024]{1,0:T(8,128)(2,1)S(1)} custom-call(s32[18]{0:T(128)S(1)} %copy-done.3, bf16[2048,768]{1,0:T(8,128)(2,1)S(1)} %copy-done.9, bf16[2048,768]{1,0:T(8,128)(2,1)} %get-tuple-element.291.refs_1_, bf16[2048,768]{1,0:T(8,128)(2,1)} %get-tuple-element.292.refs_2_, bf16[4608,1024]{1,0:T(8,128)(2,1)} %refs_3_.3), custom_call_target="tpu_custom_call" | custom-call | flops 9663676416 | bytes 25165824 | tf_op jit(solution)/shard_map/feed_out_give/pallas_call | solution.py:291
  295.9 2.4 z_sums.1
  302.3 9.6 %feed_out_keep.1 = bf16[1024,1024]{1,0:T(8,128)(2,1)S(1)} custom-call(s32[18]{0:T(128)S(1)} %copy-done.3, bf16[2048,768]{1,0:T(8,128)(2,1)S(1)} %copy-done.10, bf16[2048,768]{1,0:T(8,128)(2,1)} %get-tuple-element.291.refs_1_, bf16[2048,768]{1,0:T(8,128)(2,1)} %get-tuple-element.292.refs_2_, bf16[4608,1024]{1,0:T(8,128)(2,1)} %refs_3_.3), custom_call_target="tpu_custom_call" | custom-call | flops 9663676416 | bytes 25165824 | tf_op jit(solution)/shard_map/feed_out_keep/pallas_call | solution.py:291
  316.0 2.2 last_sums.1
  319.8 3.7 %add_convert_fusion = bf16[1024,1024]{1,0:T(8,128)(2,1)} fusion(f32[1024,1024]{1,0:T(8,128)S(1)} %copy-done.11, bf16[1024,1024]{1,0:T(8,128)(2,1)} %collective-permute-done.37, bf16[1024,1024]{1,0:T(8,128)(2,1)S(1)} %feed_out_keep.1, f32[1024]{0:T(1024)S(1)} %copy-done.41), kind=kLoop, calls=%fused_computation | loop fusion | flops 6291456 | bytes 10489856 | tf_op jit(solution)/shard_map/convert_element_type | solution.py:43
  325.5 3.4 %collective-permute-done.42 = f32[8,1024]{1,0:T(8,128)S(1)} collective-permute-done((f32[8,1024]{1,0:T(8,128)S(1)}, f32[8,1024]{1,0:T(8,128)S(1)}, u32[]{:S(2)}, u32[]{:S(2)}) %collective-permute-start.42) | collective-permute-done | bytes 32800 | tf_op jit(solution)/shard_map/ppermute | solution.py:35
  (264 shorter events, 75.4 us)
Async XLA Ops:
  10.7 20.2 %collective-permute-start.2 = (bf16[1024,1024]{1,0:T(8,128)(2,1)}, bf16[1024,1024]{1,0:T(8,128)(2,1)}, u32[]{:S(2)}, u32[]{:S(2)}) collective-permute-start(bf16[1024,1024]{1,0:T(8,128)(2,1)} %multiply_convert_fusion.own_grad_ref), channel_id=1, source_target_pairs={{0,1},{1,0},{2,3},{3,2},{4,5},{5,4},{6,7},{7,6},{8,9},{9,8},{10,11... | collective-permute-start | bytes 6291464 | tf_op jit(solution)/shard_map/ppermute | solution.py:35
  63.5 32.8 %collective-permute-start.3 = (bf16[2,2,2,128,384]{4,3,2,1,0:T(8,128)(2,1)}, bf16[2,2,2,128,384]{4,3,2,1,0:T(8,128)(2,1)S(1)}, u32[]{:S(2)}, u32[]{:S(2)}) collective-permute-start(bf16[2,2,2,128,384]{4,3,2,1,0:T(8,128)(2,1)} %get-tuple-element.182), channel_id=1, source_target_pairs={{0,8},{4,12},{8,0},{12,4},{16,24},{20,28},{24,16},{28,20},{1,9},{5... | collective-permute-start | bytes 2359304 | tf_op jit(solution)/shard_map/ppermute | solution.py:35
  65.1 31.1 %collective-permute-start.4 = (bf16[2,2,2,128,384]{4,3,2,1,0:T(8,128)(2,1)}, bf16[2,2,2,128,384]{4,3,2,1,0:T(8,128)(2,1)S(1)}, u32[]{:S(2)}, u32[]{:S(2)}) collective-permute-start(bf16[2,2,2,128,384]{4,3,2,1,0:T(8,128)(2,1)} %get-tuple-element.183), channel_id=1, source_target_pairs={{0,4},{4,0},{8,12},{12,8},{16,20},{20,16},{24,28},{28,24},{1,5},{5... | collective-permute-start | bytes 2359304 | tf_op jit(solution)/shard_map/ppermute | solution.py:35
  66.7 29.6 %collective-permute-start.5 = (bf16[2,384,512]{2,1,0:T(8,128)(2,1)}, bf16[2,384,512]{2,1,0:T(8,128)(2,1)S(1)}, u32[]{:S(2)}, u32[]{:S(2)}) collective-permute-start(bf16[2,384,512]{2,1,0:T(8,128)(2,1)} %get-tuple-element.184), channel_id=1, source_target_pairs={{0,2},{1,3},{2,0},{3,1},{4,6},{5,7},{6,4},{7,5},{8,10},{9,11},{10,... | collective-permute-start | bytes 2359304 | tf_op jit(solution)/shard_map/ppermute | solution.py:35
  97.3 34.0 %collective-permute-start.10 = (bf16[2,2,128,384]{3,2,1,0:T(8,128)(2,1)S(1)}, bf16[2,2,128,384]{3,2,1,0:T(8,128)(2,1)S(1)}, u32[]{:S(2)}, u32[]{:S(2)}) collective-permute-start(bf16[2,2,128,384]{3,2,1,0:T(8,128)(2,1)S(1)} %get-tuple-element.347), channel_id=1, source_target_pairs={{0,8},{4,12},{8,0},{12,4},{16,24},{20,28},{24,16},{28,20},{1,9},{5... | collective-permute-start | bytes 1179656 | tf_op jit(solution)/shard_map/ppermute | solution.py:35
  98.7 32.6 %collective-permute-start.9 = (bf16[2,2,128,384]{3,2,1,0:T(8,128)(2,1)S(1)}, bf16[2,2,128,384]{3,2,1,0:T(8,128)(2,1)S(1)}, u32[]{:S(2)}, u32[]{:S(2)}) collective-permute-start(bf16[2,2,128,384]{3,2,1,0:T(8,128)(2,1)S(1)} %get-tuple-element.349), channel_id=1, source_target_pairs={{0,4},{4,0},{8,12},{12,8},{16,20},{20,16},{24,28},{28,24},{1,5},{5... | collective-permute-start | bytes 1179656 | tf_op jit(solution)/shard_map/ppermute | solution.py:35
  99.4 31.9 %collective-permute-start.6 = (bf16[2,2,2,128,384]{4,3,2,1,0:T(8,128)(2,1)}, bf16[2,2,2,128,384]{4,3,2,1,0:T(8,128)(2,1)S(1)}, u32[]{:S(2)}, u32[]{:S(2)}) collective-permute-start(bf16[2,2,2,128,384]{4,3,2,1,0:T(8,128)(2,1)} %get-tuple-element.200), channel_id=1, source_target_pairs={{0,8},{4,12},{8,0},{12,4},{16,24},{20,28},{24,16},{28,20},{1,9},{5... | collective-permute-start | bytes 2359304 | tf_op jit(solution)/shard_map/ppermute | solution.py:35
  101.0 30.2 %collective-permute-start.7 = (bf16[2,2,2,128,384]{4,3,2,1,0:T(8,128)(2,1)S(1)}, bf16[2,2,2,128,384]{4,3,2,1,0:T(8,128)(2,1)S(1)}, u32[]{:S(2)}, u32[]{:S(2)}) collective-permute-start(bf16[2,2,2,128,384]{4,3,2,1,0:T(8,128)(2,1)S(1)} %copy-done.52), channel_id=1, source_target_pairs={{0,4},{4,0},{8,12},{12,8},{16,20},{20,16},{24,28},{28,24},{1,5},{5... | collective-permute-start | bytes 2359304 | tf_op jit(solution)/shard_map/ppermute | solution.py:35
  102.6 28.7 %collective-permute-start.8 = (bf16[2,384,512]{2,1,0:T(8,128)(2,1)S(1)}, bf16[2,384,512]{2,1,0:T(8,128)(2,1)S(1)}, u32[]{:S(2)}, u32[]{:S(2)}) collective-permute-start(bf16[2,384,512]{2,1,0:T(8,128)(2,1)S(1)} %copy-done.50), channel_id=1, source_target_pairs={{0,2},{1,3},{2,0},{3,1},{4,6},{5,7},{6,4},{7,5},{8,10},{9,11},{10,... | collective-permute-start | bytes 2359304 | tf_op jit(solution)/shard_map/ppermute | solution.py:35
  132.3 35.4 %collective-permute-start.15 = (bf16[2,2,128,384]{3,2,1,0:T(8,128)(2,1)S(1)}, bf16[2,2,128,384]{3,2,1,0:T(8,128)(2,1)}, u32[]{:S(2)}, u32[]{:S(2)}) collective-permute-start(bf16[2,2,128,384]{3,2,1,0:T(8,128)(2,1)S(1)} %get-tuple-element.343), channel_id=1, source_target_pairs={{0,8},{4,12},{8,0},{12,4},{16,24},{20,28},{24,16},{28,20},{1,9},{5... | collective-permute-start | bytes 1179656 | tf_op jit(solution)/shard_map/ppermute | solution.py:35
  133.7 33.9 %collective-permute-start.14 = (bf16[2,2,128,384]{3,2,1,0:T(8,128)(2,1)S(1)}, bf16[2,2,128,384]{3,2,1,0:T(8,128)(2,1)S(1)}, u32[]{:S(2)}, u32[]{:S(2)}) collective-permute-start(bf16[2,2,128,384]{3,2,1,0:T(8,128)(2,1)S(1)} %get-tuple-element.345), channel_id=1, source_target_pairs={{0,4},{4,0},{8,12},{12,8},{16,20},{20,16},{24,28},{28,24},{1,5},{5... | collective-permute-start | bytes 1179656 | tf_op jit(solution)/shard_map/ppermute | solution.py:35
  135.3 32.3 %collective-permute-start.11 = (bf16[2,2,2,128,384]{4,3,2,1,0:T(8,128)(2,1)S(1)}, bf16[2,2,2,128,384]{4,3,2,1,0:T(8,128)(2,1)}, u32[]{:S(2)}, u32[]{:S(2)}) collective-permute-start(bf16[2,2,2,128,384]{4,3,2,1,0:T(8,128)(2,1)S(1)} %copy-done.51), channel_id=1, source_target_pairs={{0,8},{4,12},{8,0},{12,4},{16,24},{20,28},{24,16},{28,20},{1,9},{5... | collective-permute-start | bytes 2359304 | tf_op jit(solution)/shard_map/ppermute | solution.py:35
  136.9 30.8 %collective-permute-start.12 = (bf16[2,2,2,128,384]{4,3,2,1,0:T(8,128)(2,1)S(1)}, bf16[2,2,2,128,384]{4,3,2,1,0:T(8,128)(2,1)}, u32[]{:S(2)}, u32[]{:S(2)}) collective-permute-start(bf16[2,2,2,128,384]{4,3,2,1,0:T(8,128)(2,1)S(1)} %copy-done.49), channel_id=1, source_target_pairs={{0,4},{4,0},{8,12},{12,8},{16,20},{20,16},{24,28},{28,24},{1,5},{5... | collective-permute-start | bytes 2359304 | tf_op jit(solution)/shard_map/ppermute | solution.py:35
  138.4 29.2 %collective-permute-start.13 = (bf16[2,384,512]{2,1,0:T(8,128)(2,1)S(1)}, bf16[2,384,512]{2,1,0:T(8,128)(2,1)}, u32[]{:S(2)}, u32[]{:S(2)}) collective-permute-start(bf16[2,384,512]{2,1,0:T(8,128)(2,1)S(1)} %copy-done.48), channel_id=1, source_target_pairs={{0,2},{1,3},{2,0},{3,1},{4,6},{5,7},{6,4},{7,5},{8,10},{9,11},{10,... | collective-permute-start | bytes 2359304 | tf_op jit(solution)/shard_map/ppermute | solution.py:35
  170.3 22.3 %collective-permute-start.18 = (bf16[2,2,128,384]{3,2,1,0:T(8,128)(2,1)}, bf16[2,2,128,384]{3,2,1,0:T(8,128)(2,1)}, u32[]{:S(2)}, u32[]{:S(2)}) collective-permute-start(bf16[2,2,128,384]{3,2,1,0:T(8,128)(2,1)} %get-tuple-element.338), channel_id=1, source_target_pairs={{0,8},{4,12},{8,0},{12,4},{16,24},{20,28},{24,16},{28,20},{1,9},{5... | collective-permute-start | bytes 1179656 | tf_op jit(solution)/shard_map/ppermute | solution.py:35
  173.0 19.7 %collective-permute-start.17 = (bf16[2,2,128,384]{3,2,1,0:T(8,128)(2,1)}, bf16[2,2,128,384]{3,2,1,0:T(8,128)(2,1)}, u32[]{:S(2)}, u32[]{:S(2)}) collective-permute-start(bf16[2,2,128,384]{3,2,1,0:T(8,128)(2,1)} %get-tuple-element.340), channel_id=1, source_target_pairs={{0,4},{4,0},{8,12},{12,8},{16,20},{20,16},{24,28},{28,24},{1,5},{5... | collective-permute-start | bytes 1179656 | tf_op jit(solution)/shard_map/ppermute | solution.py:35
  176.6 27.2 %collective-permute-start.20 = (bf16[2,4,128,384]{3,2,1,0:T(8,128)(2,1)}, bf16[2,4,128,384]{3,2,1,0:T(8,128)(2,1)}, u32[]{:S(2)}, u32[]{:S(2)}) collective-permute-start(bf16[2,4,128,384]{3,2,1,0:T(8,128)(2,1)} %get-tuple-element.255), channel_id=1, source_target_pairs={{0,2},{1,3},{2,0},{3,1},{4,6},{5,7},{6,4},{7,5},{8,10},{9,11},{10,... | collective-permute-start | bytes 2359304 | tf_op jit(solution)/shard_map/ppermute | solution.py:35
  206.1 25.8 %collective-permute-start.21 = (bf16[2,8,128,256]{3,2,1,0:T(8,128)(2,1)S(1)}, bf16[2,8,128,256]{3,2,1,0:T(8,128)(2,1)}, u32[]{:S(2)}, u32[]{:S(2)}) collective-permute-start(bf16[2,8,128,256]{3,2,1,0:T(8,128)(2,1)S(1)} %get-tuple-element.265), channel_id=1, source_target_pairs={{0,1},{1,0},{2,3},{3,2},{4,5},{5,4},{6,7},{7,6},{8,9},{9,8},{10,11... | collective-permute-start | bytes 3145736 | tf_op jit(solution)/shard_map/ppermute | solution.py:35
  207.2 24.7 %collective-permute-start.23 = (bf16[576,512]{1,0:T(8,128)(2,1)}, bf16[576,512]{1,0:T(8,128)(2,1)S(1)}, u32[]{:S(2)}, u32[]{:S(2)}) collective-permute-start(bf16[576,512]{1,0:T(8,128)(2,1)} %get-tuple-element.351), channel_id=1, source_target_pairs={{0,4},{4,0},{8,12},{12,8},{16,20},{20,16},{24,28},{28,24},{1,5},{5... | collective-permute-start | bytes 1769480 | tf_op jit(solution)/shard_map/ppermute | solution.py:35
  209.8 19.3 %collective-permute-start.22 = (bf16[2,2,128,384]{3,2,1,0:T(8,128)(2,1)}, bf16[2,2,128,384]{3,2,1,0:T(8,128)(2,1)}, u32[]{:S(2)}, u32[]{:S(2)}) collective-permute-start(bf16[2,2,128,384]{3,2,1,0:T(8,128)(2,1)} %get-tuple-element.266), channel_id=1, source_target_pairs={{0,2},{1,3},{2,0},{3,1},{4,6},{5,7},{6,4},{7,5},{8,10},{9,11},{10,... | collective-permute-start | bytes 1179656 | tf_op jit(solution)/shard_map/ppermute | solution.py:35
  211.3 20.6 %collective-permute-start.24 = (bf16[4,128,384]{2,1,0:T(8,128)(2,1)}, bf16[4,128,384]{2,1,0:T(8,128)(2,1)}, u32[]{:S(2)}, u32[]{:S(2)}) collective-permute-start(bf16[4,128,384]{2,1,0:T(8,128)(2,1)} %get-tuple-element.337), channel_id=1, source_target_pairs={{0,16},{4,20},{8,24},{12,28},{16,0},{20,4},{24,8},{28,12},{1,17},{... | collective-permute-start | bytes 1179656 | tf_op jit(solution)/shard_map/ppermute | solution.py:35
  231.9 18.3 %collective-permute-start.25 = (bf16[2,8,128,768]{3,2,1,0:T(8,128)(2,1)S(1)}, bf16[2,8,128,768]{3,2,1,0:T(8,128)(2,1)S(1)}, u32[]{:S(2)}, u32[]{:S(2)}) collective-permute-start(bf16[2,8,128,768]{3,2,1,0:T(8,128)(2,1)S(1)} %in_grads_give.1), channel_id=1, source_target_pairs={{0,1},{1,0},{2,3},{3,2},{4,5},{5,4},{6,7},{7,6},{8,9},{9,8},{10,11... | collective-permute-start | bytes 9437192 | tf_op jit(solution)/shard_map/ppermute | solution.py:35
  234.2 14.3 %collective-permute-start.26 = (bf16[8,128,256]{2,1,0:T(8,128)(2,1)S(1)}, bf16[8,128,256]{2,1,0:T(8,128)(2,1)S(1)}, u32[]{:S(2)}, u32[]{:S(2)}) collective-permute-start(bf16[8,128,256]{2,1,0:T(8,128)(2,1)S(1)} %get-tuple-element.333), channel_id=1, source_target_pairs={{0,2},{1,3},{2,0},{3,1},{4,6},{5,7},{6,4},{7,5},{8,10},{9,11},{10,... | collective-permute-start | bytes 1572872 | tf_op jit(solution)/shard_map/ppermute | solution.py:35
  234.8 15.5 %collective-permute-start.27 = (bf16[576,512]{1,0:T(8,128)(2,1)S(1)}, bf16[576,512]{1,0:T(8,128)(2,1)S(1)}, u32[]{:S(2)}, u32[]{:S(2)}) collective-permute-start(bf16[576,512]{1,0:T(8,128)(2,1)S(1)} %copy-done.28), channel_id=1, source_target_pairs={{0,4},{4,0},{8,12},{12,8},{16,20},{20,16},{24,28},{28,24},{1,5},{5... | collective-permute-start | bytes 1769480 | tf_op jit(solution)/shard_map/ppermute | solution.py:35
  236.3 28.8 %collective-permute-start.30 = (bf16[576,512]{1,0:T(8,128)(2,1)S(1)}, bf16[576,512]{1,0:T(8,128)(2,1)S(1)}, u32[]{:S(2)}, u32[]{:S(2)}) collective-permute-start(bf16[576,512]{1,0:T(8,128)(2,1)S(1)} %fusion.1), channel_id=1, source_target_pairs={{0,16},{4,20},{8,24},{12,28},{16,0},{20,4},{24,8},{28,12},{1,17},{... | collective-permute-start | bytes 1769480 | tf_op jit(solution)/shard_map/ppermute | solution.py:35
  252.4 18.9 %collective-permute-start.29 = (bf16[2,4,128,384]{3,2,1,0:T(8,128)(2,1)S(1)}, bf16[2,4,128,384]{3,2,1,0:T(8,128)(2,1)S(1)}, u32[]{:S(2)}, u32[]{:S(2)}) collective-permute-start(bf16[2,4,128,384]{3,2,1,0:T(8,128)(2,1)S(1)} %fusion.4), channel_id=1, source_target_pairs={{0,4},{4,0},{8,12},{12,8},{16,20},{20,16},{24,28},{28,24},{1,5},{5... | collective-permute-start | bytes 2359304 | tf_op jit(solution)/shard_map/ppermute | solution.py:35
  253.8 18.5 %collective-permute-start.28 = (bf16[8,128,384]{2,1,0:T(8,128)(2,1)S(1)}, bf16[8,128,384]{2,1,0:T(8,128)(2,1)S(1)}, u32[]{:S(2)}, u32[]{:S(2)}) collective-permute-start(bf16[8,128,384]{2,1,0:T(8,128)(2,1)S(1)} %get-tuple-element.328), channel_id=1, source_target_pairs={{0,2},{1,3},{2,0},{3,1},{4,6},{5,7},{6,4},{7,5},{8,10},{9,11},{10,... | collective-permute-start | bytes 2359304 | tf_op jit(solution)/shard_map/ppermute | solution.py:35
  277.2 16.3 %collective-permute-start.34 = (bf16[576,512]{1,0:T(8,128)(2,1)S(1)}, bf16[576,512]{1,0:T(8,128)(2,1)S(1)}, u32[]{:S(2)}, u32[]{:S(2)}) collective-permute-start(bf16[576,512]{1,0:T(8,128)(2,1)S(1)} %add_convert_fusion.8), channel_id=1, source_target_pairs={{1,9},{3,11},{5,13},{7,15},{8,0},{10,2},{12,4},{14,6},{17,25},{19,... | collective-permute-start | bytes 1769480 | tf_op jit(solution)/shard_map/ppermute | solution.py:1019
  278.8 16.2 %collective-permute-start.31 = (bf16[4,128,640]{2,1,0:T(8,128)(2,1)}, bf16[4,128,640]{2,1,0:T(8,128)(2,1)S(1)}, u32[]{:S(2)}, u32[]{:S(2)}) collective-permute-start(bf16[4,128,640]{2,1,0:T(8,128)(2,1)} %get-tuple-element.286), channel_id=1, source_target_pairs={{0,4},{4,0},{8,12},{12,8},{16,20},{20,16},{24,28},{28,24},{1,5},{5... | collective-permute-start | bytes 1966088 | tf_op jit(solution)/shard_map/ppermute | solution.py:35
  295.0 17.2 %collective-permute-start.37 = (bf16[1024,1024]{1,0:T(8,128)(2,1)S(1)}, bf16[1024,1024]{1,0:T(8,128)(2,1)}, u32[]{:S(2)}, u32[]{:S(2)}) collective-permute-start(bf16[1024,1024]{1,0:T(8,128)(2,1)S(1)} %feed_out_give.1), channel_id=1, source_target_pairs={{0,1},{1,0},{2,3},{3,2},{4,5},{5,4},{6,7},{7,6},{8,9},{9,8},{10,11... | collective-permute-start | bytes 6291464 | tf_op jit(solution)/shard_map/ppermute | solution.py:35
  298.3 13.9 %collective-permute-start.36 = (bf16[2,128,1024]{2,1,0:T(8,128)(2,1)}, bf16[2,128,1024]{2,1,0:T(8,128)(2,1)S(1)}, u32[]{:S(2)}, u32[]{:S(2)}) collective-permute-start(bf16[2,128,1024]{2,1,0:T(8,128)(2,1)} %get-tuple-element.297), channel_id=1, source_target_pairs={{0,8},{4,12},{8,0},{12,4},{16,24},{20,28},{24,16},{28,20},{1,9},{5... | collective-permute-start | bytes 1572872 | tf_op jit(solution)/shard_map/ppermute | solution.py:35
  314.1 15.9 %collective-permute-start.43 = (bf16[128,1024]{1,0:T(8,128)(2,1)S(1)}, bf16[128,1024]{1,0:T(8,128)(2,1)S(1)}, u32[]{:S(2)}, u32[]{:S(2)}) collective-permute-start(bf16[128,1024]{1,0:T(8,128)(2,1)S(1)} %fusion.25), channel_id=1, source_target_pairs={{0,16},{4,20},{8,24},{12,28},{16,0},{20,4},{24,8},{28,12},{1,17},{... | collective-permute-start | bytes 786440 | tf_op jit(solution)/shard_map/ppermute | solution.py:35
  (67 other events, 432.9 us)
